TPU v7x, 32 devices: a whole 2x2x4 slice. The times are simulated.
32 devices in a mesh: mem: 16 (over z, x, core), hist: 2 (over y).
Axes of the slice: x: 2, y: 2, z: 4, core: 2. Of those that a mesh axis runs over, the one named last changes fastest.
Arguments:
- memory_block: bfloat16 [64, 16, 64, 128], P('mem', 'hist'), may hold values from -1.5 to 1.5
- memory_rows: bfloat16 [32768, 2, 128], P(('mem', 'hist')), may hold values from -6 to 6
- panel_rows: bfloat16 [8192, 2, 128], P(('hist', 'mem')), may hold values from -6 to 6
- time_deal: int32 [64], replicated, may hold values from 0 to 63, each once
- column_times: int32 [16], replicated, may hold values from 0 to 63
- window_start: int32 [1], replicated, may hold values from 0 to 32
- coupling: float32 [64, 64], replicated, may hold values from -0.375 to 0.375
- hamiltonian: bfloat16 [64, 64], replicated, may hold values from -6 to 6
Outputs:
- new_rows: bfloat16 [8192, 2, 128], P(('hist', 'mem'))
- new_sigma: bfloat16 [8192, 2, 128], P(('hist', 'mem'))
Inputs may be any that keep to these rules, and one draw needn't show every extreme that they name: `time_deal`: each of 0 to 63 once.
All inputs are finite; a program needn't handle non-finite values.
Results may differ from a plain program's by a relative error of at most 0.014.
Values may be sent and summed in bfloat16 or wider, within the bound.
No kernel may reach another device: no remote copies, remote signals or barrier semaphores. Data moves between devices by JAX's collectives and lax.ppermute only.
A program may use at most 64 MiB of HBM per device.

v0:
```python
import jax
import jax.numpy as jnp
from jax import lax
from jax.sharding import PartitionSpec as P

P_SIZE = 8


time_step = 0.02


def sigma_of(tiles, coupling):
    orbitals = coupling.shape[0]
    real_part = tiles[..., :orbitals]
    imag_part = tiles[..., orbitals:]
    bubble = real_part * real_part + imag_part * imag_part
    screened = jnp.einsum("ik,...kpl->...ipl", coupling, bubble, precision=lax.Precision.HIGHEST)
    screening = jnp.einsum("...ipl,jl->...ipj", screened, coupling, precision=lax.Precision.HIGHEST)
    return -jnp.concatenate([real_part * screening, imag_part * screening], -1)


def row_sigma(row_block, coupling):
    orbitals = coupling.shape[0]
    shaped = row_block.astype(jnp.float32).reshape(
        -1, orbitals, row_block.shape[1], row_block.shape[2]
    )
    result = sigma_of(shaped, coupling).astype(jnp.bfloat16)
    return result.reshape(row_block.shape)


def complex_form(tiles):
    orbitals = tiles.shape[-1] // 2
    real_part = tiles[..., :orbitals]
    imag_part = tiles[..., orbitals:]
    upper = jnp.concatenate([real_part, imag_part], -1)
    lower = jnp.concatenate([-imag_part, real_part], -1)
    return jnp.concatenate([upper, lower], -2)


def advance(row_block, collision, hamiltonian):
    orbitals = hamiltonian.shape[0]
    shaped = row_block.reshape(-1, orbitals, row_block.shape[1], row_block.shape[2])
    applied = jnp.einsum("ik,nkpc->nipc", hamiltonian, shaped, preferred_element_type=jnp.float32)
    turned = jnp.concatenate([applied[..., orbitals:], -applied[..., :orbitals]], -1)
    summed = turned.reshape(row_block.shape) + collision
    return (row_block.astype(jnp.float32) + time_step * summed).astype(jnp.bfloat16)


def local(
    memory_block,
    memory_rows,
    panel_rows,
    time_deal,
    column_times,
    window_start,
    coupling,
    hamiltonian,
):
    orbitals = coupling.shape[0]
    panels = panel_rows.shape[1]
    slots = memory_block.shape[0]
    columns = memory_block.shape[1]
    mem_index = lax.axis_index("mem")
    hist_index = lax.axis_index("hist")
    own_rows = panel_rows.shape[0]
    gathered = lax.all_gather(memory_rows, "hist", axis=0, tiled=True)
    slot_sigma = row_sigma(gathered, coupling)
    slot_sigma = slot_sigma.reshape(slots, P_SIZE, orbitals, panels, 2 * orbitals)
    slot_times = lax.dynamic_slice_in_dim(time_deal, mem_index * slots, slots, 0)
    local_columns = lax.dynamic_slice_in_dim(column_times, hist_index * columns, columns, 0)
    causal = (slot_times[:, None] >= local_columns[None, :]) & (
        slot_times[:, None] >= window_start[0]
    )
    forms = complex_form(memory_block) * causal[:, :, None, None].astype(jnp.bfloat16)
    tiles = own_rows * lax.axis_size("mem") // orbitals
    tile_ids = jnp.arange(tiles, dtype=jnp.int32)
    picked_sigma = jnp.take(slot_sigma, tile_ids % P_SIZE, axis=1)
    picked_forms = jnp.take(forms, tile_ids // P_SIZE, axis=1)
    term = jnp.einsum(
        "kqipr,kqrc->qipc", picked_sigma, picked_forms, preferred_element_type=jnp.float32
    )
    own_sum = lax.psum_scatter(
        term.reshape(own_rows * lax.axis_size("mem"), panels, 2 * orbitals),
        "mem",
        scatter_dimension=0,
        tiled=True,
    )
    advanced = advance(panel_rows, own_sum, hamiltonian)
    new_sigma = row_sigma(advanced, coupling)
    return (advanced, new_sigma)


def solution(mesh):
    in_specs = (
        P("mem", "hist", None, None),
        P(("mem", "hist"), None, None),
        P(("hist", "mem"), None, None),
        P(),
        P(),
        P(),
        P(),
        P(),
    )
    out_specs = (P(("hist", "mem"), None, None), P(("hist", "mem"), None, None))
    return jax.shard_map(local, mesh=mesh, in_specs=in_specs, out_specs=out_specs, check_vma=False)
```

profile of v0, /device:TPU:0, one launch (start us, length us, event | category | flops | bytes accessed | tf_op | source)
XLA Modules:
  0.0 140.1 jit_solution(16360215267609154875)
XLA Ops:
  7.2 0.0 copy-start
  7.2 0.0 copy-start.1
  7.2 0.0 all-gather.2.cloned.1.call-start
  7.2 2.0 %copy.14 = bf16[1024,2,128]{2,0,1:T(8,128)(2,1)} copy(bf16[1024,2,128]{2,1,0:T(2,128)(2,1)} %param.9) | data formatting | bytes 1048576 | tf_op args[1]
  9.2 0.0 all-gather.2.cloned.1.call-update
  9.2 0.0 reduce-scatter.2.cloned.1.call-start
  9.9 0.7 dynamic_slice.7
  10.7 0.7 broadcast_compare_fusion
  11.4 0.1 and_convert_fusion
  11.5 0.0 copy-done.1
  11.5 0.2 slice_negate_fusion
  11.7 0.5 maximum_multiply_fusion
  12.2 5.5 %gather_fusion.1 = bf16[64,4,128,128]{3,2,1,0:T(8,128)(2,1)} fusion(bf16[4,8,128,128]{3,2,1,0:T(8,128)(2,1)S(1)} %maximum_multiply_fusion, s32[1024]{0:T(1024)S(1)} %pad_clamp_fusion), kind=kCustom, calls=%fused_computation.1 | custom fusion | bytes 16777472 | tf_op jit(solution)/shard_map/jit(_take)/gather | solution.py:78
  17.8 15.8 %all-gather.2.cloned.1.call-done = bf16[2048,2,128]{2,0,1:T(8,128)(2,1)} async-done(((bf16[1024,2,128]{2,0,1:T(8,128)(2,1)}), bf16[2048,2,128]{2,0,1:T(8,128)(2,1)}) %all-gather.2.cloned.1.call-update) | async-done | bytes 1048592 | tf_op jit(solution)/shard_map/all_gather | solution.py:66
  33.6 2.3 %fusion.34 = (f32[32,64,2,64]{3,1,0,2:T(8,128)S(1)}, f32[32,64,2,64]{3,1,0,2:T(8,128)S(1)}) fusion(bf16[32,64,2,128]{3,1,0,2:T(8,128)(2,1)} %bitcast.67), kind=kLoop, calls=%fused_computation.70 | loop fusion | bytes 4194304 | tf_op jit(solution)/shard_map/slice | solution.py:14
  35.9 0.0 copy-done
  35.9 2.3 %fusion.9 = f32[32,2,64,64]{2,3,1,0:T(8,128)S(1)} fusion(f32[32,64,2,64]{3,1,0,2:T(8,128)S(1)} %get-tuple-element.9, f32[32,64,2,64]{3,1,0,2:T(8,128)S(1)} %get-tuple-element.8, f32[64,64]{1,0:T(8,128)S(1)} %copy-done), kind=kOutput, calls=%fused_computation.13 | convolution fusion | flops 202113024 | bytes 3162112 | tf_op jit(solution)/shard_map/ik,...kpl->...ipl/dot_general | solution.py:17
  38.1 1.9 %copy_multiply_fusion.1 = (f32[32,64,2,64]{3,1,2,0:T(8,128)S(1)}, f32[32,64,2,64]{3,1,2,0:T(8,128)S(1)}) fusion(f32[32,64,2,64]{3,1,0,2:T(8,128)S(1)} %get-tuple-element.8, f32[32,64,2,64]{3,1,0,2:T(8,128)S(1)} %get-tuple-element.9, f32[64,64]{1,0:T(8,128)S(1)} %copy-done, f32[32,2,64,64]{2,3,1,0:T(8,128)S(1)} %fusion.9), kind=kOutput, calls=%fused_computation.19 | convolution fusion | flops 201850880 | bytes 5259264 | tf_op jit(solution)/shard_map/...ipl,jl->...ipj/dot_general | solution.py:18
  40.0 0.6 fusion.6
  40.7 5.2 %gather_fusion = bf16[64,4,64,2,128]{4,2,3,1,0:T(8,128)(2,1)} fusion(bf16[4,8,64,2,128]{4,2,3,1,0:T(8,128)(2,1)S(1)} %fusion.6, s32[1024]{0:T(1024)S(1)} %pad_clamp_fusion.1), kind=kCustom, calls=%fused_computation | custom fusion | bytes 16777472 | tf_op jit(solution)/shard_map/jit(_take)/gather | solution.py:77
  45.9 10.2 %fusion = f32[64,64,2,128,1]{3,1,4,0,2:T(8,128)} fusion(bf16[64,4,128,128]{3,2,1,0:T(8,128)(2,1)} %gather_fusion.1, pred[64]{0:T(512)(128)(4,1)S(1)} %compare_and_fusion, bf16[64,4,64,2,128]{4,2,3,1,0:T(8,128)(2,1)} %gather_fusion, pred[64]{0:T(512)(128)(4,1)S(1)} %compare_and_fusion.1), kind=kOutput, calls=%fused_computation.2 | convolution fusion | flops 1082130432 | bytes 20971648 | tf_op jit(solution)/shard_map/kqipr,kqrc->qipc/dot_general | solution.py:79
  56.1 0.0 copy-start.2
  56.1 0.0 copy-start.3
  56.1 0.0 reduce-scatter.2.cloned.1.call-update
  56.1 0.9 copy-done.2
  57.0 0.0 copy-done.3
  57.0 0.2 convolution_bitcast_fusion
  57.2 0.1 fusion.35
  57.3 0.1 pad_maximum_fusion
  57.5 71.5 %reduce-scatter.2.cloned.1.call-done = f32[256,2,128]{2,0,1:T(8,128)} async-done(((f32[4096,2,128]{2,0,1:T(8,128)}), f32[256,2,128]{2,0,1:T(8,128)}) %reduce-scatter.2.cloned.1.call-update) | async-done | bytes 262160 | tf_op jit(solution)/shard_map/reduce_scatter | solution.py:82
  129.0 1.0 fusion.18
  130.0 0.8 copy.23
  130.8 0.1 fusion.36
  130.9 0.4 convolution_bitcast_fusion.1
  131.3 0.4 copy_multiply_fusion.3
  131.7 0.1 copy.21
  131.8 0.2 concatenate.32
  132.1 0.2 copy.22
  132.2 0.2 concatenate.33
  132.4 0.8 copy.24
  (8 shorter events, 0.1 us)
Async XLA Ops:
  7.2 28.7 %copy-start = (f32[64,64]{1,0:T(8,128)S(1)}, f32[64,64]{1,0:T(8,128)}, u32[]{:S(2)}) copy-start(f32[64,64]{1,0:T(8,128)} %param.14) | copy-start | bytes 49156
  7.2 4.3 %copy-start.1 = (bf16[4,8,64,128]{3,2,1,0:T(8,128)(2,1)S(1)}, bf16[4,8,64,128]{3,2,1,0:T(8,128)(2,1)}, u32[]{:S(2)}) copy-start(bf16[4,8,64,128]{3,2,1,0:T(8,128)(2,1)} %param.8) | copy-start | bytes 1572868
  7.2 26.4 %all-gather.2.cloned.1.call-start = ((), (), s32[]{:S(2)}) async-start(), calls=%async_computation.1 | async-start | bytes 1572864 | tf_op jit(solution)/shard_map/all_gather | solution.py:66
  9.2 119.8 %reduce-scatter.2.cloned.1.call-start = ((), (), s32[]{:S(2)}) async-start(), calls=%async_computation.2 | async-start | bytes 4456448 | tf_op jit(solution)/shard_map/reduce_scatter | solution.py:82
  56.1 0.9 copy-start.2
  56.1 0.9 copy-start.3
Sparse Core Ops, SparseCore 0:
  9.5 23.9 all-gather.1
  56.2 72.7 reduce-scatter.1
where the time goes:
time: 140 us
  waiting for transfers between devices  87.4 us (62%)
  local copies, waits for them, and re-layouts  19.1 us (14%)
  matrix products  15.3 us (11%)
  between operations  14.9 us (11%)
  other arithmetic  3.43 us (2%)
    reduce_scatter x1, waiting for transfers between devices, local(): lax.psum_scatter(term.reshape(own_rows * lax.axis_size('mem'), panels, 2...  71.5 us
    all_gather x1, waiting for transfers between devices, local(): gathered = lax.all_gather(memory_rows, 'hist', axis=0, tiled=True)  15.8 us
    dot_general x1, matrix products, local(): jnp.einsum('kqipr,kqrc->qipc', picked_sigma, picked_forms, preferred_elem...  10.2 us
    gather x1, local copies, waits for them, and re-layouts, local(): picked_forms = jnp.take(forms, tile_ids // P_SIZE, axis=1)  5.55 us
    gather x1, local copies, waits for them, and re-layouts, local(): picked_sigma = jnp.take(slot_sigma, tile_ids % P_SIZE, axis=1)  5.24 us
    unnamed x11, local copies, waits for them, and re-layouts  4.42 us
  transfers between devices with their start and end apart: 2, of which 2 were waited for; matrix products, arithmetic and copies ran while one was open for 6% of the time, Pallas kernels for 0%

commit v1 on v0

v1 whole, which is shorter than its diff:
```python
import functools

import jax
import jax.numpy as jnp
from jax import lax
from jax.experimental import pallas as pl
from jax.experimental.pallas import tpu as pltpu
from jax.sharding import PartitionSpec as P

P_SIZE = 8
CHUNKS = 2


time_step = 0.02
F32 = jnp.float32
BF16 = jnp.bfloat16


def dot(left, right):
    return jnp.dot(left, right, preferred_element_type=F32)


def halves(value):
    top = value.astype(BF16)
    return top, (value - top.astype(F32)).astype(BF16)


def sigma_tiles(tiles, consts):
    n, rows, lanes = tiles.shape
    right_top, right_low, left_top, left_low = consts
    flat = tiles.reshape(n * rows, lanes).astype(F32)
    top, low = halves(flat * flat)
    screened = dot(top, right_top) + (dot(low, right_top) + dot(top, right_low))
    top, low = halves(screened)
    top, low = top.reshape(n, rows, lanes), low.reshape(n, rows, lanes)
    out = []
    step = 2 if n % 2 == 0 else 1
    for start in range(0, n, step):
        tops = jnp.concatenate([top[start + s] for s in range(step)], 1)
        lows = jnp.concatenate([low[start + s] for s in range(step)], 1)
        both = dot(left_top, tops) + (dot(left_top, lows) + dot(left_low, tops))
        for s in range(step):
            out.append(both[:, s * lanes:(s + 1) * lanes])
    screening = jnp.stack(out).reshape(n * rows, lanes)
    return (-flat * screening).reshape(n, rows, lanes)


def call(body, outs, *args, flops=0, **keywords):
    moved = sum(a.size * a.dtype.itemsize for a in list(args) + list(outs))
    return pl.pallas_call(
        body,
        out_shape=outs,
        cost_estimate=pl.CostEstimate(flops=flops, bytes_accessed=moved, transcendentals=0),
        **keywords,
    )(*args)


def shape(dims, kind):
    return jax.ShapeDtypeStruct(tuple(dims), kind)


def split_body(rows_ref, *outs):
    core = lax.axis_index("mem") & 1
    parts = len(outs) // 2
    for c in range(parts):
        size = outs[2 * c].shape[2]
        outs[2 * c][...] = rows_ref[:, :, core, c * size:(c + 1) * size]
        outs[2 * c + 1][...] = rows_ref[:, :, 1 - core, c * size:(c + 1) * size]


def early_body(n_early, slot_of, groups, chunks, deal_ref, columns_ref, start_ref, block_ref, other_ref, coupling_ref, ham_ref, panel_ref, *refs):
    early = refs[:n_early * chunks]
    weights_ref, consts_ref, base_ref = refs[n_early * chunks:n_early * chunks + 3]
    sigmas = refs[n_early * chunks + 3:]
    orbitals = coupling_ref.shape[0]
    rows = consts_ref.shape[1]
    panels = rows // orbitals
    mem, hist = lax.axis_index("mem"), lax.axis_index("hist")
    core, pair = mem & 1, mem >> 1
    slots, columns = block_ref.shape[0], block_ref.shape[1]

    spread = (lax.broadcasted_iota(jnp.int32, (rows, orbitals), 0) // panels == lax.broadcasted_iota(jnp.int32, (rows, orbitals), 1)).astype(F32)
    row_at = lax.broadcasted_iota(jnp.int32, (rows, rows), 0)
    lane_at = lax.broadcasted_iota(jnp.int32, (rows, rows), 1)
    same = (row_at % panels == lane_at % panels).astype(F32)

    def exact(left, right, dims):
        return lax.dot_general(left, right, (dims, ((), ())), precision=lax.Precision.HIGHEST, preferred_element_type=F32)

    def rowed(matrix):
        return exact(exact(spread, matrix, ((1,), (0,))), spread, ((1,), (1,))) * same

    lanes = 2 * orbitals
    fold = (lax.broadcasted_iota(jnp.int32, (lanes, orbitals), 0) % orbitals == lax.broadcasted_iota(jnp.int32, (lanes, orbitals), 1)).astype(F32)
    coupling = coupling_ref[...]
    right = exact(exact(fold, coupling, ((1,), (1,))), fold, ((1,), (1,)))
    right_top, right_low = halves(right)
    left_top, left_low = halves(rowed(coupling))
    for at, value in enumerate((right_top, right_low, left_top, left_low)):
        consts_ref[at] = value
    consts = (right_top, right_low, left_top, left_low)

    ham = rowed(ham_ref[...].astype(F32)).astype(BF16)
    sign = jnp.where(lax.broadcasted_iota(jnp.int32, (rows, lanes), 1) < orbitals, 1.0, -1.0).astype(F32)
    for tile in range(panel_ref.shape[0]):
        values = panel_ref[tile]
        turned = pltpu.roll(dot(ham, values), orbitals, 1) * sign
        base_ref[tile] = values.astype(F32) + time_step * turned

    for at in range(n_early * chunks):
        source = early[at]
        tiles = sigma_tiles(source[...].reshape((-1,) + source.shape[3:]), consts)
        sigmas[at][...] = tiles.astype(BF16).reshape(source.shape)

    flip = jnp.where(lax.broadcasted_iota(jnp.int32, (orbitals, lanes), 1) < orbitals, -1.0, 1.0).astype(F32)
    own_column = pair // groups
    begin = start_ref[0]
    for q in range(2 * slots):
        foreign, local = slot_of(q, hist)
        source = other_ref if foreign else block_ref
        mem_of = (mem ^ 1) if foreign else mem
        time = deal_ref[mem_of * slots + local]
        for apart in range(columns):
            column = own_column ^ apart
            keep = jnp.logical_and(time >= columns_ref[hist * columns + column], time >= begin)
            upper = source[local, column].astype(F32) * jnp.where(keep, 1.0, 0.0).astype(F32)
            lower = pltpu.roll(upper, orbitals, 1) * flip
            weights_ref[q * lanes:q * lanes + orbitals, apart * lanes:(apart + 1) * lanes] = upper.astype(BF16)
            weights_ref[q * lanes + orbitals:(q + 1) * lanes, apart * lanes:(apart + 1) * lanes] = lower.astype(BF16)


def term_body(n_done, n_late, order, groups, consts_ref, weights_ref, *refs):
    done, late = refs[:n_done], refs[n_done:n_done + n_late]
    send_ref, keep_ref, left_ref = refs[n_done + n_late:]
    pair = lax.axis_index("mem") >> 1
    own_group = pair % groups
    consts = tuple(consts_ref[at] for at in range(4))
    rows, lanes = send_ref.shape[1:]
    for step in range(groups):
        group = own_group ^ step
        q = 0
        for at, source in enumerate(done + late):
            tiles = source[:, group]
            count = tiles.shape[0]
            if at >= n_done:
                tiles = sigma_tiles(tiles.reshape((-1,) + tiles.shape[2:]), consts).astype(BF16).reshape(tiles.shape)
            for s in range(count):
                left_ref[:, q * lanes:(q + 1) * lanes] = tiles[s].reshape(rows, lanes)
                q += 1
        total = dot(left_ref[...], weights_ref[...])
        for place, block in enumerate(order):
            if block % groups != step:
                continue
            apart = block // groups
            value = total[:, apart * lanes:(apart + 1) * lanes]
            if place < len(order) // 2:
                send_ref[place] = value.astype(BF16)
            else:
                keep_ref[place - len(order) // 2] = value


def add_body(keep_ref, got_ref, send_ref, next_ref):
    half = send_ref.shape[0]
    send_ref[...] = (keep_ref[:half] + got_ref[:half].astype(F32)).astype(BF16)
    next_ref[...] = keep_ref[half:] + got_ref[half:].astype(F32)


def last_body(chunks, consts_ref, base_ref, *refs):
    keeps, gots = refs[:chunks], refs[chunks:2 * chunks]
    rows_ref, sigma_ref = refs[2 * chunks:]
    consts = tuple(consts_ref[at] for at in range(4))
    size = base_ref.shape[0] // chunks
    for c in range(chunks):
        here = slice(c * size, (c + 1) * size)
        collision = (keeps[c][...] + gots[c][...].astype(F32)).reshape((size,) + base_ref.shape[1:])
        rows = (base_ref[here] + time_step * collision).astype(BF16)
        rows_ref[here] = rows
        sigma_ref[here] = sigma_tiles(rows, consts).astype(BF16)


def block_order(count, masks):
    order = [0]
    for mask in reversed(masks):
        order = [block ^ mask for block in order] + order
    return order


def exchange(value, mem_mask, hist_mask):
    mems, hists = lax.axis_size("mem"), lax.axis_size("hist")
    pairs = [(m * hists + h, (m ^ mem_mask) * hists + (h ^ hist_mask)) for m in range(mems) for h in range(hists)]
    return lax.ppermute(value, ("mem", "hist"), pairs)


def local(memory_block, memory_rows, panel_rows, time_deal, column_times, window_start, coupling, hamiltonian):
    orbitals = coupling.shape[0]
    panels, lanes = panel_rows.shape[1:]
    rows = orbitals * panels
    slots = memory_block.shape[0]
    columns = memory_block.shape[1]
    pairs = lax.axis_size("mem") // 2
    own_tiles = panel_rows.shape[0] // orbitals
    groups = P_SIZE // (2 * own_tiles)
    chunks = CHUNKS if own_tiles % CHUNKS == 0 else 1
    part = own_tiles // chunks
    two_hist = lax.axis_size("hist") == 2

    if not two_hist:
        memory_rows = lax.all_gather(memory_rows, "hist", axis=0, tiled=True)
    held = memory_rows.shape[0] // (P_SIZE * orbitals)
    tiles = memory_rows.reshape(held, groups, 2, own_tiles, rows, lanes)
    panel_tiles = panel_rows.reshape(own_tiles, rows, lanes)
    piece = shape((held, groups, part, rows, lanes), BF16)
    split = call(split_body, [piece] * (2 * chunks), tiles)
    mine, other = split[0::2], split[1::2]

    if two_hist:
        same_core = [exchange(mine[c], 0, 1) for c in range(chunks)]
        cross = [exchange(other[c], 1, 1) for c in range(chunks)]
    partner_block = exchange(memory_block, 1, 0)
    partner = [exchange(other[c], 1, 0) for c in range(chunks)]

    if two_hist:
        def slot_of(q, hist):
            return (q // held) % 2, (hist ^ (q // (2 * held))) * held + q % held
    else:
        def slot_of(q, hist):
            return q // held, q % held

    early = [mine, partner]
    n_early = len(early)
    flat_early = [array for source in early for array in source]
    smem = pl.BlockSpec(memory_space=pltpu.SMEM)
    vmem = pl.BlockSpec(memory_space=pltpu.VMEM)
    outs = [
        shape((2 * slots * lanes, columns * lanes), BF16),
        shape((4, rows, lanes), BF16),
        shape((own_tiles, rows, lanes), F32),
    ] + [piece] * (n_early * chunks)
    weights, consts, base, *sigmas = call(
        functools.partial(early_body, n_early, slot_of, groups, chunks),
        outs,
        time_deal, column_times, window_start, memory_block, partner_block, coupling, hamiltonian, panel_tiles, *flat_early,
        in_specs=[smem] * 3 + [vmem] * (5 + n_early * chunks),
    )

    bits = [1 << b for b in range(pairs.bit_length() - 1)]
    if len(bits) > 1:
        bits[-1] |= bits[-2]
    finals = []
    for c in range(chunks):
        masks = list(bits)
        order = block_order(pairs, masks)
        height = part * rows
        done = [sigmas[e * chunks + c] for e in range(n_early)]
        late = [same_core[c], cross[c]] if two_hist else []
        send, keep = call(
            functools.partial(term_body, len(done), len(late), order, groups),
            [shape((pairs // 2, height, lanes), BF16), shape((pairs // 2, height, lanes), F32)],
            consts, weights, *done, *late,
            flops=2 * height * groups * 2 * slots * lanes * columns * lanes,
            scratch_shapes=[pltpu.VMEM((height, 2 * slots * lanes), BF16)],
        )
        for at, mask in enumerate(masks):
            got = exchange(send, 2 * mask, 0)
            if at + 1 < len(masks):
                half = keep.shape[0] // 2
                send, keep = call(
                    add_body,
                    [shape((half, height, lanes), BF16), shape((half, height, lanes), F32)],
                    keep, got,
                )
        finals.append((keep, got))

    result = shape((own_tiles, rows, lanes), BF16)
    new_rows, new_sigma = call(
        functools.partial(last_body, chunks),
        [result, result],
        consts, base, *[keep for keep, _ in finals], *[got for _, got in finals],
    )
    return new_rows.reshape(panel_rows.shape), new_sigma.reshape(panel_rows.shape)


def solution(mesh):
    in_specs = (
        P("mem", "hist", None, None),
        P(("mem", "hist"), None, None),
        P(("hist", "mem"), None, None),
        P(),
        P(),
        P(),
        P(),
        P(),
    )
    out_specs = (P(("hist", "mem"), None, None), P(("hist", "mem"), None, None))
    return jax.shard_map(local, mesh=mesh, in_specs=in_specs, out_specs=out_specs, check_vma=False)
```

time: 140 us -> 55 us (0.39)
  waiting for transfers between devices: 87.4 us -> 7.77 us
  Pallas kernels: 0 us -> 24.3 us
  starting transfers between devices: 0.08 us -> 15.7 us
  matrix products: 15.3 us -> 0 us
  local copies, waits for them, and re-layouts: 19.1 us -> 5.46 us
  between operations: 14.9 us -> 1.38 us
  other arithmetic: 3.43 us -> 0 us
    reduce_scatter x1 -> x0, waiting for transfers between devices: 71.5 us -> none  [local(): lax.psum_scatter(term.reshape(own_rows * lax.axis_size('mem'), panels, 2...]
    pallas_call x0 -> x9, Pallas kernels: none -> 24.3 us  [call(): pl.pallas_call(body, out_shape=outs, cost_estimate=pl.CostEstimate(flops=...]
    all_gather x1 -> x0, waiting for transfers between devices: 15.8 us -> none  [local(): gathered = lax.all_gather(memory_rows, 'hist', axis=0, tiled=True)]
    ppermute x0 -> x13, starting transfers between devices: none -> 15.7 us  [exchange(): return lax.ppermute(value, ('mem', 'hist'), pairs)]
    dot_general x6 -> x0, matrix products: 15.3 us -> none  [the longest x1 10.2 us: local(): jnp.einsum('kqipr,kqrc->qipc', picked_sigma, picked_forms, preferred_elem...]
    gather x2 -> x0, local copies, waits for them, and re-layouts: 10.8 us -> none  [the longest x1 5.55 us: local(): picked_forms = jnp.take(forms, tile_ids // P_SIZE, axis=1)]
    ppermute x0 -> x13, waiting for transfers between devices: none -> 7.77 us  [exchange(): return lax.ppermute(value, ('mem', 'hist'), pairs)]
    slice x2 -> x0, local copies, waits for them, and re-layouts: 2.37 us -> none  [sigma_of(): real_part = tiles[..., :orbitals]]
  transfers between devices with their start and end apart: 2 -> 13, of which waited for: 2 -> 3; matrix products, arithmetic and copies ran while one was open for 6% -> 0% of each run, Pallas kernels for 0% -> 40%
where the time goes in v1:
time: 55 us; the launch traced here: 54.6 us
  Pallas kernels  24.3 us (44%)
  starting transfers between devices  15.7 us (29%)
  waiting for transfers between devices  7.77 us (14%)
  local copies, waits for them, and re-layouts  5.46 us (10%)
  between operations  1.38 us (3%)
    pallas_call x9, Pallas kernels, call(): pl.pallas_call(body, out_shape=outs, cost_estimate=pl.CostEstimate(flops=...  24.3 us
    ppermute x13, starting transfers between devices, exchange(): return lax.ppermute(value, ('mem', 'hist'), pairs)  15.7 us
    ppermute x13, waiting for transfers between devices, exchange(): return lax.ppermute(value, ('mem', 'hist'), pairs)  7.77 us
    unnamed x26, local copies, waits for them, and re-layouts  5.46 us
  transfers between devices with their start and end apart: 13, of which 3 were waited for; matrix products, arithmetic and copies ran while one was open for 0% of the time, Pallas kernels for 40%

profile of v1, /device:TPU:0, one launch (start us, length us, event | category | flops | bytes accessed | tf_op | source)
XLA Modules:
  0.0 54.6 jit_solution(17414534876002562212)
XLA Ops:
  0.6 0.6 %collective-permute-start = (bf16[4,8,64,128]{3,2,1,0:T(8,128)(2,1)}, bf16[4,8,64,128]{3,2,1,0:T(8,128)(2,1)S(1)}, u32[]{:S(2)}, u32[]{:S(2)}) collective-permute-start(bf16[4,8,64,128]{3,2,1,0:T(8,128)(2,1)} %block_ref.1), channel_id=1, source_target_pairs={{0,2},{1,3},{2,0},{3,1},{4,6},{5,7},{6,4},{7,5},{8,10},{9,11},{10,... | collective-permute-start | bytes 1572872 | tf_op jit(solution)/shard_map/ppermute | solution.py:191
  1.2 1.9 %shard_map.95 = (bf16[2,1,2,128,128]{4,3,2,1,0:T(8,128)(2,1)}, bf16[2,1,2,128,128]{4,3,2,1,0:T(8,128)(2,1)}, bf16[2,1,2,128,128]{4,3,2,1,0:T(8,128)(2,1)}, bf16[2,1,2,128,128]{4,3,2,1,0:T(8,128)(2,1)}) custom-call(bf16[2,1,2,4,128,128]{5,4,3,2,1,0:T(8,128)(2,1)} %bitcast.4), custom_call_target="tpu_custom_call" | custom-call | bytes 1048576 | tf_op jit(solution)/shard_map/pallas_call | solution.py:50
  3.0 0.0 collective-permute-start.1
  3.1 0.5 collective-permute-start.2
  3.5 2.5 %collective-permute-start.7 = (bf16[2,1,2,128,128]{4,3,2,1,0:T(8,128)(2,1)}, bf16[2,1,2,128,128]{4,3,2,1,0:T(8,128)(2,1)S(1)}, u32[]{:S(2)}, u32[]{:S(2)}) collective-permute-start(bf16[2,1,2,128,128]{4,3,2,1,0:T(8,128)(2,1)} %get-tuple-element.28.refs_1_), channel_id=1, source_target_pairs={{0,1},{1,0},{2,3},{3,2},{4,5},{5,4},{6,7},{7,6},{8,9},{9,8},{10,11... | collective-permute-start | bytes 393224 | tf_op jit(solution)/shard_map/ppermute | solution.py:191
  6.1 0.1 collective-permute-start.8
  6.2 0.0 collective-permute-done.1.refs_2_
  6.2 1.7 %collective-permute-start.3 = (bf16[2,1,2,128,128]{4,3,2,1,0:T(8,128)(2,1)}, bf16[2,1,2,128,128]{4,3,2,1,0:T(8,128)(2,1)S(1)}, u32[]{:S(2)}, u32[]{:S(2)}) collective-permute-start(bf16[2,1,2,128,128]{4,3,2,1,0:T(8,128)(2,1)} %get-tuple-element.27.refs_0_), channel_id=1, source_target_pairs={{0,1},{1,0},{2,3},{3,2},{4,5},{5,4},{6,7},{7,6},{8,9},{9,8},{10,11... | collective-permute-start | bytes 393224 | tf_op jit(solution)/shard_map/ppermute | solution.py:191
  7.9 0.0 collective-permute-done.2.refs_3_
  7.9 0.0 collective-permute-start.4
  8.6 0.0 collective-permute-done.other_ref
  8.6 0.0 copy-start
  8.6 0.8 %copy-done = bf16[4,8,64,128]{3,2,1,0:T(8,128)(2,1)} copy-done((bf16[4,8,64,128]{3,2,1,0:T(8,128)(2,1)}, bf16[4,8,64,128]{3,2,1,0:T(8,128)(2,1)S(1)}, u32[]{:S(2)}) %copy-start) | copy-done | bytes 524312
  9.4 5.0 %shard_map.96 = (bf16[1024,1024]{1,0:T(8,128)(2,1)}, bf16[4,128,128]{2,1,0:T(8,128)(2,1)}, f32[4,128,128]{2,1,0:T(8,128)}, bf16[2,1,2,128,128]{4,3,2,1,0:T(8,128...) custom-call(s32[64]{0:T(128)} %deal_ref.1, ...), custom_call_target="tpu_custom_call" | custom-call | bytes 4743492 | tf_op jit(solution)/shard_map/pallas_call | solution.py:50
  14.4 0.0 collective-permute-done.7.refs_2_
  14.4 0.0 copy-start.9
  14.4 0.0 collective-permute-done.8.refs_3_
  14.5 0.6 %copy-done.9 = bf16[2,1,2,128,128]{4,3,2,1,0:T(8,128)(2,1)} copy-done((bf16[2,1,2,128,128]{4,3,2,1,0:T(8,128)(2,1)}, bf16[2,1,2,128,128]{4,3,2,1,0:T(8,128)(2,1)S(1)}, u32[]{:S(2)}) %copy-start.9) | copy-done | bytes 131096
  15.1 0.0 copy-done.10
  15.1 4.0 %shard_map.100 = (bf16[4,256,128]{2,1,0:T(8,128)(2,1)}, f32[4,256,128]{2,1,0:T(8,128)}) custom-call(bf16[4,128,128]{2,1,0:T(8,128)(2,1)} %get-tuple-element.31.consts_ref, bf16[1024,1024]{1,0:T(8,128)(2,1)} %get-tuple-element.33.weights_ref, bf16[2,1,2,128,128]{4,3,2,1,0:T(8,128)(2,1)} %get-tuple-element.41.refs_0_, ...), custom_call_target="tpu_custom_call" | custom-call | flops 536870912 | bytes 3538944 | tf_op jit(solution)/shard_map/pallas_call | solution.py:50
  19.1 1.6 %collective-permute-start.9 = (bf16[4,256,128]{2,1,0:T(8,128)(2,1)}, bf16[4,256,128]{2,1,0:T(8,128)(2,1)S(1)}, u32[]{:S(2)}, u32[]{:S(2)}) collective-permute-start(bf16[4,256,128]{2,1,0:T(8,128)(2,1)} %get-tuple-element.44), channel_id=1, source_target_pairs={{0,4},{1,5},{2,6},{3,7},{4,0},{5,1},{6,2},{7,3},{8,12},{9,13},{10,... | collective-permute-start | bytes 786440 | tf_op jit(solution)/shard_map/ppermute | solution.py:191
  20.7 0.0 collective-permute-done.3.refs_2_
  20.8 0.0 collective-permute-done.4.refs_3_
  20.8 0.0 copy-start.8
  20.8 0.6 %copy-done.7 = bf16[2,1,2,128,128]{4,3,2,1,0:T(8,128)(2,1)} copy-done((bf16[2,1,2,128,128]{4,3,2,1,0:T(8,128)(2,1)}, bf16[2,1,2,128,128]{4,3,2,1,0:T(8,128)(2,1)S(1)}, u32[]{:S(2)}) %copy-start.7) | copy-done | bytes 131096
  21.4 0.0 copy-done.8
  21.4 4.0 %shard_map.97 = (bf16[4,256,128]{2,1,0:T(8,128)(2,1)}, f32[4,256,128]{2,1,0:T(8,128)}) custom-call(bf16[4,128,128]{2,1,0:T(8,128)(2,1)} %get-tuple-element.31.consts_ref, bf16[1024,1024]{1,0:T(8,128)(2,1)} %get-tuple-element.33.weights_ref, bf16[2,1,2,128,128]{4,3,2,1,0:T(8,128)(2,1)} %get-tuple-element.34.refs_0_, ...), custom_call_target="tpu_custom_call" | custom-call | flops 536870912 | bytes 3538944 | tf_op jit(solution)/shard_map/pallas_call | solution.py:50
  25.4 0.4 collective-permute-start.5
  25.8 2.1 %collective-permute-done.9.got_ref = bf16[4,256,128]{2,1,0:T(8,128)(2,1)S(1)} collective-permute-done((bf16[4,256,128]{2,1,0:T(8,128)(2,1)}, bf16[4,256,128]{2,1,0:T(8,128)(2,1)S(1)}, u32[]{:S(2)}, u32[]{:S(2)}) %collective-permute-start.9) | collective-permute-done | bytes 262176 | tf_op jit(solution)/shard_map/ppermute | solution.py:191
  27.9 0.7 %copy-done.1 = bf16[4,256,128]{2,1,0:T(8,128)(2,1)} copy-done((bf16[4,256,128]{2,1,0:T(8,128)(2,1)}, bf16[4,256,128]{2,1,0:T(8,128)(2,1)S(1)}, u32[]{:S(2)}) %copy-start.1) | copy-done | bytes 262168
  28.6 1.9 %shard_map.101 = (bf16[2,256,128]{2,1,0:T(8,128)(2,1)}, f32[2,256,128]{2,1,0:T(8,128)}) custom-call(f32[4,256,128]{2,1,0:T(8,128)} %get-tuple-element.43.keep_ref, bf16[4,256,128]{2,1,0:T(8,128)(2,1)} %copy-done.1), custom_call_target="tpu_custom_call" | custom-call | bytes 1179648 | tf_op jit(solution)/shard_map/pallas_call | solution.py:50
  30.5 1.8 %collective-permute-start.10 = (bf16[2,256,128]{2,1,0:T(8,128)(2,1)}, bf16[2,256,128]{2,1,0:T(8,128)(2,1)S(1)}, u32[]{:S(2)}, u32[]{:S(2)}) collective-permute-start(bf16[2,256,128]{2,1,0:T(8,128)(2,1)} %get-tuple-element.46), channel_id=1, source_target_pairs={{0,8},{1,9},{2,10},{3,11},{4,12},{5,13},{6,14},{7,15},{8,0},{9,1},... | collective-permute-start | bytes 393224 | tf_op jit(solution)/shard_map/ppermute | solution.py:191
  32.3 1.8 %collective-permute-done.5.got_ref = bf16[4,256,128]{2,1,0:T(8,128)(2,1)S(1)} collective-permute-done((bf16[4,256,128]{2,1,0:T(8,128)(2,1)}, bf16[4,256,128]{2,1,0:T(8,128)(2,1)S(1)}, u32[]{:S(2)}, u32[]{:S(2)}) %collective-permute-start.5) | collective-permute-done | bytes 262176 | tf_op jit(solution)/shard_map/ppermute | solution.py:191
  34.1 0.7 %copy-done.2 = bf16[4,256,128]{2,1,0:T(8,128)(2,1)} copy-done((bf16[4,256,128]{2,1,0:T(8,128)(2,1)}, bf16[4,256,128]{2,1,0:T(8,128)(2,1)S(1)}, u32[]{:S(2)}) %copy-start.2) | copy-done | bytes 262168
  34.8 1.9 %shard_map.98 = (bf16[2,256,128]{2,1,0:T(8,128)(2,1)}, f32[2,256,128]{2,1,0:T(8,128)}) custom-call(f32[4,256,128]{2,1,0:T(8,128)} %get-tuple-element.36.keep_ref, bf16[4,256,128]{2,1,0:T(8,128)(2,1)} %copy-done.2), custom_call_target="tpu_custom_call" | custom-call | bytes 1179648 | tf_op jit(solution)/shard_map/pallas_call | solution.py:50
  36.6 1.6 %collective-permute-start.6 = (bf16[2,256,128]{2,1,0:T(8,128)(2,1)}, bf16[2,256,128]{2,1,0:T(8,128)(2,1)S(1)}, u32[]{:S(2)}, u32[]{:S(2)}) collective-permute-start(bf16[2,256,128]{2,1,0:T(8,128)(2,1)} %get-tuple-element.39), channel_id=1, source_target_pairs={{0,8},{1,9},{2,10},{3,11},{4,12},{5,13},{6,14},{7,15},{8,0},{9,1},... | collective-permute-start | bytes 393224 | tf_op jit(solution)/shard_map/ppermute | solution.py:191
  38.2 0.0 collective-permute-done.10.got_ref
  38.2 0.7 %copy-done.5 = bf16[2,256,128]{2,1,0:T(8,128)(2,1)} copy-done((bf16[2,256,128]{2,1,0:T(8,128)(2,1)}, bf16[2,256,128]{2,1,0:T(8,128)(2,1)S(1)}, u32[]{:S(2)}) %copy-start.5) | copy-done | bytes 131096
  38.9 1.7 %shard_map.102 = (bf16[1,256,128]{2,1,0:T(8,128)(2,1)}, f32[1,256,128]{2,1,0:T(8,128)}) custom-call(f32[2,256,128]{2,1,0:T(8,128)} %get-tuple-element.45.keep_ref, bf16[2,256,128]{2,1,0:T(8,128)(2,1)} %copy-done.5), custom_call_target="tpu_custom_call" | custom-call | bytes 589824 | tf_op jit(solution)/shard_map/pallas_call | solution.py:50
  40.6 2.5 %collective-permute-start.12 = (bf16[1,256,128]{2,1,0:T(8,128)(2,1)}, bf16[1,256,128]{2,1,0:T(8,128)(2,1)S(1)}, u32[]{:S(2)}, u32[]{:S(2)}) collective-permute-start(bf16[1,256,128]{2,1,0:T(8,128)(2,1)} %get-tuple-element.49), channel_id=1, source_target_pairs={{0,24},{1,25},{2,26},{3,27},{4,28},{5,29},{6,30},{7,31},{8,16},{9,... | collective-permute-start | bytes 196616 | tf_op jit(solution)/shard_map/ppermute | solution.py:191
  43.0 0.0 collective-permute-done.6.got_ref
  43.0 0.7 %copy-done.6 = bf16[2,256,128]{2,1,0:T(8,128)(2,1)} copy-done((bf16[2,256,128]{2,1,0:T(8,128)(2,1)}, bf16[2,256,128]{2,1,0:T(8,128)(2,1)S(1)}, u32[]{:S(2)}) %copy-start.6) | copy-done | bytes 131096
  43.7 1.7 %shard_map.99 = (bf16[1,256,128]{2,1,0:T(8,128)(2,1)}, f32[1,256,128]{2,1,0:T(8,128)}) custom-call(f32[2,256,128]{2,1,0:T(8,128)} %get-tuple-element.38.keep_ref, bf16[2,256,128]{2,1,0:T(8,128)(2,1)} %copy-done.6), custom_call_target="tpu_custom_call" | custom-call | bytes 589824 | tf_op jit(solution)/shard_map/pallas_call | solution.py:50
  45.4 2.4 %collective-permute-start.11 = (bf16[1,256,128]{2,1,0:T(8,128)(2,1)}, bf16[1,256,128]{2,1,0:T(8,128)(2,1)S(1)}, u32[]{:S(2)}, u32[]{:S(2)}) collective-permute-start(bf16[1,256,128]{2,1,0:T(8,128)(2,1)} %get-tuple-element.48), channel_id=1, source_target_pairs={{0,24},{1,25},{2,26},{3,27},{4,28},{5,29},{6,30},{7,31},{8,16},{9,... | collective-permute-start | bytes 196616 | tf_op jit(solution)/shard_map/ppermute | solution.py:191
  47.7 0.0 collective-permute-done.12.refs_3_
  47.7 3.9 %collective-permute-done.11.refs_2_ = bf16[1,256,128]{2,1,0:T(8,128)(2,1)S(1)} collective-permute-done((bf16[1,256,128]{2,1,0:T(8,128)(2,1)}, bf16[1,256,128]{2,1,0:T(8,128)(2,1)S(1)}, u32[]{:S(2)}, u32[]{:S(2)}) %collective-permute-start.11) | collective-permute-done | bytes 65568 | tf_op jit(solution)/shard_map/ppermute | solution.py:191
  51.6 0.6 %copy-done.12 = bf16[1,256,128]{2,1,0:T(8,128)(2,1)} copy-done((bf16[1,256,128]{2,1,0:T(8,128)(2,1)}, bf16[1,256,128]{2,1,0:T(8,128)(2,1)S(1)}, u32[]{:S(2)}) %copy-start.12) | copy-done | bytes 65560
  52.2 2.3 %shard_map.103 = (bf16[4,128,128]{2,1,0:T(8,128)(2,1)}, bf16[4,128,128]{2,1,0:T(8,128)(2,1)}) custom-call(bf16[4,128,128]{2,1,0:T(8,128)(2,1)} %get-tuple-element.31.consts_ref, f32[4,128,128]{2,1,0:T(8,128)} %get-tuple-element.32.base_ref, f32[1,256,128]{2,1,0:T(8,128)} %get-tuple-element.40.refs_0_, f32[1,256,128]{2,1,0:T(8,128)} %get-tuple-element.47.refs_1_, ...), custom_call_target="tpu_custom_call" | custom-call | bytes 1048576 | tf_op jit(solution)/shard_map/pallas_call | solution.py:50
  (13 shorter events, 0.0 us)
Async XLA Ops:
  0.6 8.0 %collective-permute-start = (bf16[4,8,64,128]{3,2,1,0:T(8,128)(2,1)}, bf16[4,8,64,128]{3,2,1,0:T(8,128)(2,1)S(1)}, u32[]{:S(2)}, u32[]{:S(2)}) collective-permute-start(bf16[4,8,64,128]{3,2,1,0:T(8,128)(2,1)} %block_ref.1), channel_id=1, source_target_pairs={{0,2},{1,3},{2,0},{3,1},{4,6},{5,7},{6,4},{7,5},{8,10},{9,11},{10,... | collective-permute-start | bytes 1572872 | tf_op jit(solution)/shard_map/ppermute | solution.py:191
  3.0 3.1 %collective-permute-start.1 = (bf16[2,1,2,128,128]{4,3,2,1,0:T(8,128)(2,1)}, bf16[2,1,2,128,128]{4,3,2,1,0:T(8,128)(2,1)S(1)}, u32[]{:S(2)}, u32[]{:S(2)}) collective-permute-start(bf16[2,1,2,128,128]{4,3,2,1,0:T(8,128)(2,1)} %get-tuple-element.29), channel_id=1, source_target_pairs={{0,2},{1,3},{2,0},{3,1},{4,6},{5,7},{6,4},{7,5},{8,10},{9,11},{10,... | collective-permute-start | bytes 393224 | tf_op jit(solution)/shard_map/ppermute | solution.py:191
  3.1 4.9 %collective-permute-start.2 = (bf16[2,1,2,128,128]{4,3,2,1,0:T(8,128)(2,1)}, bf16[2,1,2,128,128]{4,3,2,1,0:T(8,128)(2,1)S(1)}, u32[]{:S(2)}, u32[]{:S(2)}) collective-permute-start(bf16[2,1,2,128,128]{4,3,2,1,0:T(8,128)(2,1)} %get-tuple-element.30), channel_id=1, source_target_pairs={{0,2},{1,3},{2,0},{3,1},{4,6},{5,7},{6,4},{7,5},{8,10},{9,11},{10,... | collective-permute-start | bytes 393224 | tf_op jit(solution)/shard_map/ppermute | solution.py:191
  3.5 10.9 %collective-permute-start.7 = (bf16[2,1,2,128,128]{4,3,2,1,0:T(8,128)(2,1)}, bf16[2,1,2,128,128]{4,3,2,1,0:T(8,128)(2,1)S(1)}, u32[]{:S(2)}, u32[]{:S(2)}) collective-permute-start(bf16[2,1,2,128,128]{4,3,2,1,0:T(8,128)(2,1)} %get-tuple-element.28.refs_1_), channel_id=1, source_target_pairs={{0,1},{1,0},{2,3},{3,2},{4,5},{5,4},{6,7},{7,6},{8,9},{9,8},{10,11... | collective-permute-start | bytes 393224 | tf_op jit(solution)/shard_map/ppermute | solution.py:191
  6.1 8.4 %collective-permute-start.8 = (bf16[2,1,2,128,128]{4,3,2,1,0:T(8,128)(2,1)}, bf16[2,1,2,128,128]{4,3,2,1,0:T(8,128)(2,1)S(1)}, u32[]{:S(2)}, u32[]{:S(2)}) collective-permute-start(bf16[2,1,2,128,128]{4,3,2,1,0:T(8,128)(2,1)} %get-tuple-element.30), channel_id=1, source_target_pairs={{0,3},{1,2},{2,1},{3,0},{4,7},{5,6},{6,5},{7,4},{8,11},{9,10},{10,... | collective-permute-start | bytes 393224 | tf_op jit(solution)/shard_map/ppermute | solution.py:191
  6.2 2.4 %copy-start.3 = (bf16[2,1,2,128,128]{4,3,2,1,0:T(8,128)(2,1)}, bf16[2,1,2,128,128]{4,3,2,1,0:T(8,128)(2,1)S(1)}, u32[]{:S(2)}) copy-start(bf16[2,1,2,128,128]{4,3,2,1,0:T(8,128)(2,1)S(1)} %collective-permute-done.1.refs_2_) | copy-start | bytes 393220
  6.2 14.6 %collective-permute-start.3 = (bf16[2,1,2,128,128]{4,3,2,1,0:T(8,128)(2,1)}, bf16[2,1,2,128,128]{4,3,2,1,0:T(8,128)(2,1)S(1)}, u32[]{:S(2)}, u32[]{:S(2)}) collective-permute-start(bf16[2,1,2,128,128]{4,3,2,1,0:T(8,128)(2,1)} %get-tuple-element.27.refs_0_), channel_id=1, source_target_pairs={{0,1},{1,0},{2,3},{3,2},{4,5},{5,4},{6,7},{7,6},{8,9},{9,8},{10,11... | collective-permute-start | bytes 393224 | tf_op jit(solution)/shard_map/ppermute | solution.py:191
  7.9 0.7 %copy-start.4 = (bf16[2,1,2,128,128]{4,3,2,1,0:T(8,128)(2,1)}, bf16[2,1,2,128,128]{4,3,2,1,0:T(8,128)(2,1)S(1)}, u32[]{:S(2)}) copy-start(bf16[2,1,2,128,128]{4,3,2,1,0:T(8,128)(2,1)S(1)} %collective-permute-done.2.refs_3_) | copy-start | bytes 393220
  7.9 12.8 %collective-permute-start.4 = (bf16[2,1,2,128,128]{4,3,2,1,0:T(8,128)(2,1)}, bf16[2,1,2,128,128]{4,3,2,1,0:T(8,128)(2,1)S(1)}, u32[]{:S(2)}, u32[]{:S(2)}) collective-permute-start(bf16[2,1,2,128,128]{4,3,2,1,0:T(8,128)(2,1)} %get-tuple-element.29), channel_id=1, source_target_pairs={{0,3},{1,2},{2,1},{3,0},{4,7},{5,6},{6,5},{7,4},{8,11},{9,10},{10,... | collective-permute-start | bytes 393224 | tf_op jit(solution)/shard_map/ppermute | solution.py:191
  8.6 0.8 %copy-start = (bf16[4,8,64,128]{3,2,1,0:T(8,128)(2,1)}, bf16[4,8,64,128]{3,2,1,0:T(8,128)(2,1)S(1)}, u32[]{:S(2)}) copy-start(bf16[4,8,64,128]{3,2,1,0:T(8,128)(2,1)S(1)} %collective-permute-done.other_ref) | copy-start | bytes 1572868
  14.4 0.7 %copy-start.9 = (bf16[2,1,2,128,128]{4,3,2,1,0:T(8,128)(2,1)}, bf16[2,1,2,128,128]{4,3,2,1,0:T(8,128)(2,1)S(1)}, u32[]{:S(2)}) copy-start(bf16[2,1,2,128,128]{4,3,2,1,0:T(8,128)(2,1)S(1)} %collective-permute-done.7.refs_2_) | copy-start | bytes 393220
  14.5 0.7 %copy-start.10 = (bf16[2,1,2,128,128]{4,3,2,1,0:T(8,128)(2,1)}, bf16[2,1,2,128,128]{4,3,2,1,0:T(8,128)(2,1)S(1)}, u32[]{:S(2)}) copy-start(bf16[2,1,2,128,128]{4,3,2,1,0:T(8,128)(2,1)S(1)} %collective-permute-done.8.refs_3_) | copy-start | bytes 393220
  19.1 8.8 %collective-permute-start.9 = (bf16[4,256,128]{2,1,0:T(8,128)(2,1)}, bf16[4,256,128]{2,1,0:T(8,128)(2,1)S(1)}, u32[]{:S(2)}, u32[]{:S(2)}) collective-permute-start(bf16[4,256,128]{2,1,0:T(8,128)(2,1)} %get-tuple-element.44), channel_id=1, source_target_pairs={{0,4},{1,5},{2,6},{3,7},{4,0},{5,1},{6,2},{7,3},{8,12},{9,13},{10,... | collective-permute-start | bytes 786440 | tf_op jit(solution)/shard_map/ppermute | solution.py:191
  20.7 0.7 %copy-start.7 = (bf16[2,1,2,128,128]{4,3,2,1,0:T(8,128)(2,1)}, bf16[2,1,2,128,128]{4,3,2,1,0:T(8,128)(2,1)S(1)}, u32[]{:S(2)}) copy-start(bf16[2,1,2,128,128]{4,3,2,1,0:T(8,128)(2,1)S(1)} %collective-permute-done.3.refs_2_) | copy-start | bytes 393220
  20.8 0.7 %copy-start.8 = (bf16[2,1,2,128,128]{4,3,2,1,0:T(8,128)(2,1)}, bf16[2,1,2,128,128]{4,3,2,1,0:T(8,128)(2,1)S(1)}, u32[]{:S(2)}) copy-start(bf16[2,1,2,128,128]{4,3,2,1,0:T(8,128)(2,1)S(1)} %collective-permute-done.4.refs_3_) | copy-start | bytes 393220
  25.4 8.6 %collective-permute-start.5 = (bf16[4,256,128]{2,1,0:T(8,128)(2,1)}, bf16[4,256,128]{2,1,0:T(8,128)(2,1)S(1)}, u32[]{:S(2)}, u32[]{:S(2)}) collective-permute-start(bf16[4,256,128]{2,1,0:T(8,128)(2,1)} %get-tuple-element.37), channel_id=1, source_target_pairs={{0,4},{1,5},{2,6},{3,7},{4,0},{5,1},{6,2},{7,3},{8,12},{9,13},{10,... | collective-permute-start | bytes 786440 | tf_op jit(solution)/shard_map/ppermute | solution.py:191
  27.9 0.7 %copy-start.1 = (bf16[4,256,128]{2,1,0:T(8,128)(2,1)}, bf16[4,256,128]{2,1,0:T(8,128)(2,1)S(1)}, u32[]{:S(2)}) copy-start(bf16[4,256,128]{2,1,0:T(8,128)(2,1)S(1)} %collective-permute-done.9.got_ref) | copy-start | bytes 786436
  30.5 7.7 %collective-permute-start.10 = (bf16[2,256,128]{2,1,0:T(8,128)(2,1)}, bf16[2,256,128]{2,1,0:T(8,128)(2,1)S(1)}, u32[]{:S(2)}, u32[]{:S(2)}) collective-permute-start(bf16[2,256,128]{2,1,0:T(8,128)(2,1)} %get-tuple-element.46), channel_id=1, source_target_pairs={{0,8},{1,9},{2,10},{3,11},{4,12},{5,13},{6,14},{7,15},{8,0},{9,1},... | collective-permute-start | bytes 393224 | tf_op jit(solution)/shard_map/ppermute | solution.py:191
  34.1 0.7 %copy-start.2 = (bf16[4,256,128]{2,1,0:T(8,128)(2,1)}, bf16[4,256,128]{2,1,0:T(8,128)(2,1)S(1)}, u32[]{:S(2)}) copy-start(bf16[4,256,128]{2,1,0:T(8,128)(2,1)S(1)} %collective-permute-done.5.got_ref) | copy-start | bytes 786436
  36.6 6.4 %collective-permute-start.6 = (bf16[2,256,128]{2,1,0:T(8,128)(2,1)}, bf16[2,256,128]{2,1,0:T(8,128)(2,1)S(1)}, u32[]{:S(2)}, u32[]{:S(2)}) collective-permute-start(bf16[2,256,128]{2,1,0:T(8,128)(2,1)} %get-tuple-element.39), channel_id=1, source_target_pairs={{0,8},{1,9},{2,10},{3,11},{4,12},{5,13},{6,14},{7,15},{8,0},{9,1},... | collective-permute-start | bytes 393224 | tf_op jit(solution)/shard_map/ppermute | solution.py:191
  38.2 0.7 %copy-start.5 = (bf16[2,256,128]{2,1,0:T(8,128)(2,1)}, bf16[2,256,128]{2,1,0:T(8,128)(2,1)S(1)}, u32[]{:S(2)}) copy-start(bf16[2,256,128]{2,1,0:T(8,128)(2,1)S(1)} %collective-permute-done.10.got_ref) | copy-start | bytes 393220
  40.6 7.2 %collective-permute-start.12 = (bf16[1,256,128]{2,1,0:T(8,128)(2,1)}, bf16[1,256,128]{2,1,0:T(8,128)(2,1)S(1)}, u32[]{:S(2)}, u32[]{:S(2)}) collective-permute-start(bf16[1,256,128]{2,1,0:T(8,128)(2,1)} %get-tuple-element.49), channel_id=1, source_target_pairs={{0,24},{1,25},{2,26},{3,27},{4,28},{5,29},{6,30},{7,31},{8,16},{9,... | collective-permute-start | bytes 196616 | tf_op jit(solution)/shard_map/ppermute | solution.py:191
  43.0 0.7 %copy-start.6 = (bf16[2,256,128]{2,1,0:T(8,128)(2,1)}, bf16[2,256,128]{2,1,0:T(8,128)(2,1)S(1)}, u32[]{:S(2)}) copy-start(bf16[2,256,128]{2,1,0:T(8,128)(2,1)S(1)} %collective-permute-done.6.got_ref) | copy-start | bytes 393220
  45.4 6.3 %collective-permute-start.11 = (bf16[1,256,128]{2,1,0:T(8,128)(2,1)}, bf16[1,256,128]{2,1,0:T(8,128)(2,1)S(1)}, u32[]{:S(2)}, u32[]{:S(2)}) collective-permute-start(bf16[1,256,128]{2,1,0:T(8,128)(2,1)} %get-tuple-element.48), channel_id=1, source_target_pairs={{0,24},{1,25},{2,26},{3,27},{4,28},{5,29},{6,30},{7,31},{8,16},{9,... | collective-permute-start | bytes 196616 | tf_op jit(solution)/shard_map/ppermute | solution.py:191
  47.7 3.9 %copy-start.11 = (bf16[1,256,128]{2,1,0:T(8,128)(2,1)}, bf16[1,256,128]{2,1,0:T(8,128)(2,1)S(1)}, u32[]{:S(2)}) copy-start(bf16[1,256,128]{2,1,0:T(8,128)(2,1)S(1)} %collective-permute-done.12.refs_3_) | copy-start | bytes 196612
  51.6 0.6 %copy-start.12 = (bf16[1,256,128]{2,1,0:T(8,128)(2,1)}, bf16[1,256,128]{2,1,0:T(8,128)(2,1)S(1)}, u32[]{:S(2)}) copy-start(bf16[1,256,128]{2,1,0:T(8,128)(2,1)S(1)} %collective-permute-done.11.refs_2_) | copy-start | bytes 196612

commit v2 on v1

--- a/solution.py
+++ b/solution.py
@@ -51,6 +51,7 @@
         body,
         out_shape=outs,
         cost_estimate=pl.CostEstimate(flops=flops, bytes_accessed=moved, transcendentals=0),
+        compiler_params=pltpu.CompilerParams(vmem_limit_bytes=16 << 20),
         **keywords,
     )(*args)
 

time: 55 us -> 44.8 us (0.81)
  Pallas kernels: 24.3 us -> 7.1 us
  waiting for transfers between devices: 7.77 us -> 11.6 us
  starting transfers between devices: 15.7 us -> 18.5 us
    pallas_call x9, Pallas kernels: 24.3 us -> 7.1 us  [call(): pl.pallas_call(body, out_shape=outs, cost_estimate=pl.CostEstimate(flops=...]
    ppermute x13, waiting for transfers between devices: 7.77 us -> 11.6 us  [exchange(): return lax.ppermute(value, ('mem', 'hist'), pairs)]
    ppermute x13, starting transfers between devices: 15.7 us -> 18.5 us  [exchange(): return lax.ppermute(value, ('mem', 'hist'), pairs)]
    unnamed x26 -> x14, local copies, waits for them, and re-layouts: 5.46 us -> 5.77 us
  transfers between devices with their start and end apart: 13 -> 13, of which waited for: 3 -> 4; matrix products, arithmetic and copies ran while one was open for 0% -> 0% of each run, Pallas kernels for 40% -> 13%
where the time goes in v2:
time: 44.8 us; the launch traced here: 44.4 us
  starting transfers between devices  18.5 us (41%)
  waiting for transfers between devices  11.6 us (26%)
  Pallas kernels  7.1 us (16%)
  local copies, waits for them, and re-layouts  5.77 us (13%)
  between operations  1.37 us (3%)
    ppermute x13, starting transfers between devices, exchange(): return lax.ppermute(value, ('mem', 'hist'), pairs)  18.5 us
    ppermute x13, waiting for transfers between devices, exchange(): return lax.ppermute(value, ('mem', 'hist'), pairs)  11.6 us
    pallas_call x9, Pallas kernels, call(): pl.pallas_call(body, out_shape=outs, cost_estimate=pl.CostEstimate(flops=...  7.1 us
    unnamed x14, local copies, waits for them, and re-layouts  5.77 us
  transfers between devices with their start and end apart: 13, of which 4 were waited for; matrix products, arithmetic and copies ran while one was open for 0% of the time, Pallas kernels for 13%

profile of v2, /device:TPU:0, one launch (start us, length us, event | category | flops | bytes accessed | tf_op | source)
XLA Modules:
  0.0 44.4 jit_solution(9357857810326492878)
XLA Ops:
  0.6 0.6 %collective-permute-start = (bf16[4,8,64,128]{3,2,1,0:T(8,128)(2,1)}, bf16[4,8,64,128]{3,2,1,0:T(8,128)(2,1)S(1)}, u32[]{:S(2)}, u32[]{:S(2)}) collective-permute-start(bf16[4,8,64,128]{3,2,1,0:T(8,128)(2,1)} %block_ref.1), channel_id=1, source_target_pairs={{0,2},{1,3},{2,0},{3,1},{4,6},{5,7},{6,4},{7,5},{8,10},{9,11},{10,... | collective-permute-start | bytes 1572872 | tf_op jit(solution)/shard_map/ppermute | solution.py:192
  1.2 0.0 copy-start
  1.2 1.0 %copy-done = bf16[1024,2,128]{2,1,0:T(2,128)(2,1)S(1)} copy-done((bf16[1024,2,128]{2,1,0:T(2,128)(2,1)S(1)}, bf16[1024,2,128]{2,1,0:T(2,128)(2,1)}, u32[]{:S(2)}) %copy-start) | copy-done | bytes 524312
  2.3 0.1 collective-permute-start.1
  2.4 0.5 %collective-permute-start.2 = (bf16[2,1,2,128,128]{4,3,2,1,0:T(8,128)(2,1)S(1)}, bf16[2,1,2,128,128]{4,3,2,1,0:T(8,128)(2,1)S(1)}, u32[]{:S(2)}, u32[]{:S(2)}) collective-permute-start(bf16[2,1,2,128,128]{4,3,2,1,0:T(8,128)(2,1)S(1)} %get-tuple-element.30), channel_id=1, source_target_pairs={{0,2},{1,3},{2,0},{3,1},{4,6},{5,7},{6,4},{7,5},{8,10},{9,11},{10,... | collective-permute-start | bytes 393224 | tf_op jit(solution)/shard_map/ppermute | solution.py:192
  2.8 2.6 %collective-permute-start.7 = (bf16[2,1,2,128,128]{4,3,2,1,0:T(8,128)(2,1)S(1)}, bf16[2,1,2,128,128]{4,3,2,1,0:T(8,128)(2,1)S(1)}, u32[]{:S(2)}, u32[]{:S(2)}) collective-permute-start(bf16[2,1,2,128,128]{4,3,2,1,0:T(8,128)(2,1)S(1)} %get-tuple-element.28.refs_1_), channel_id=1, source_target_pairs={{0,1},{1,0},{2,3},{3,2},{4,5},{5,4},{6,7},{7,6},{8,9},{9,8},{10,11... | collective-permute-start | bytes 393224 | tf_op jit(solution)/shard_map/ppermute | solution.py:192
  5.4 0.0 collective-permute-start.8
  5.5 0.0 collective-permute-done.1.refs_2_
  5.5 1.7 %collective-permute-start.3 = (bf16[2,1,2,128,128]{4,3,2,1,0:T(8,128)(2,1)S(1)}, bf16[2,1,2,128,128]{4,3,2,1,0:T(8,128)(2,1)S(1)}, u32[]{:S(2)}, u32[]{:S(2)}) collective-permute-start(bf16[2,1,2,128,128]{4,3,2,1,0:T(8,128)(2,1)S(1)} %get-tuple-element.27.refs_0_), channel_id=1, source_target_pairs={{0,1},{1,0},{2,3},{3,2},{4,5},{5,4},{6,7},{7,6},{8,9},{9,8},{10,11... | collective-permute-start | bytes 393224 | tf_op jit(solution)/shard_map/ppermute | solution.py:192
  7.2 0.0 collective-permute-done.2.refs_3_
  7.2 0.0 collective-permute-start.4
  7.9 0.0 collective-permute-done.other_ref
  7.9 0.0 copy-start.1
  7.9 1.0 %copy-done.1 = bf16[4,8,64,128]{3,2,1,0:T(8,128)(2,1)S(1)} copy-done((bf16[4,8,64,128]{3,2,1,0:T(8,128)(2,1)S(1)}, bf16[4,8,64,128]{3,2,1,0:T(8,128)(2,1)}, u32[]{:S(2)}) %copy-start.1) | copy-done | bytes 524312
  9.0 0.0 copy-start.2
  9.0 0.9 %copy-done.2 = bf16[256,2,128]{2,1,0:T(2,128)(2,1)S(1)} copy-done((bf16[256,2,128]{2,1,0:T(2,128)(2,1)S(1)}, bf16[256,2,128]{2,1,0:T(2,128)(2,1)}, u32[]{:S(2)}) %copy-start.2) | copy-done | bytes 131096
  9.9 0.0 copy-start.3
  9.9 0.8 %copy-done.3 = f32[64,64]{1,0:T(8,128)S(1)} copy-done((f32[64,64]{1,0:T(8,128)S(1)}, f32[64,64]{1,0:T(8,128)}, u32[]{:S(2)}) %copy-start.3) | copy-done | bytes 16408
  10.6 0.0 copy-start.4
  10.6 0.7 %copy-done.4 = bf16[64,64]{1,0:T(8,128)(2,1)S(1)} copy-done((bf16[64,64]{1,0:T(8,128)(2,1)S(1)}, bf16[64,64]{1,0:T(8,128)(2,1)}, u32[]{:S(2)}) %copy-start.4) | copy-done | bytes 8216
  11.3 0.0 copy-start.5
  11.3 0.7 %copy-done.5 = s32[64]{0:T(128)S(1)} copy-done((s32[64]{0:T(128)S(1)}, s32[64]{0:T(128)}, u32[]{:S(2)}) %copy-start.5) | copy-done | bytes 280
  12.0 0.0 copy-start.6
  12.0 0.7 %copy-done.6 = s32[16]{0:T(128)S(1)} copy-done((s32[16]{0:T(128)S(1)}, s32[16]{0:T(128)}, u32[]{:S(2)}) %copy-start.6) | copy-done | bytes 88
  12.6 2.8 %shard_map.96 = (bf16[1024,1024]{1,0:T(8,128)(2,1)S(1)}, bf16[4,128,128]{2,1,0:T(8,128)(2,1)S(1)}, f32[4,128,128]{2,1,0:T(8,128)S(1)}, bf16[2,1,2,128,128]{4,3,2...) custom-call(s32[64]{0:T(128)S(1)} %copy-done.5, ...), custom_call_target="tpu_custom_call" | custom-call | bytes 4743492 | tf_op jit(solution)/shard_map/pallas_call | solution.py:50
  15.5 0.0 collective-permute-done.7.refs_2_
  15.5 0.0 collective-permute-done.8.refs_3_
  15.5 1.4 %shard_map.100 = (bf16[4,256,128]{2,1,0:T(8,128)(2,1)S(1)}, f32[4,256,128]{2,1,0:T(8,128)S(1)}) custom-call(bf16[4,128,128]{2,1,0:T(8,128)(2,1)S(1)} %get-tuple-element.31.consts_ref, bf16[1024,1024]{1,0:T(8,128)(2,1)S(1)} %get-tuple-element.33.weights_ref, bf16[2,1,2,128,128]{4,3,2,1,0:T(8,128)(2,1)S(1)} %get-tuple-element.41.refs_0_, ...), custom_call_target="tpu_custom_call" | custom-call | flops 536870912 | bytes 3538944 | tf_op jit(solution)/shard_map/pallas_call | solution.py:50
  16.9 1.7 %collective-permute-start.9 = (bf16[4,256,128]{2,1,0:T(8,128)(2,1)S(1)}, bf16[4,256,128]{2,1,0:T(8,128)(2,1)S(1)}, u32[]{:S(2)}, u32[]{:S(2)}) collective-permute-start(bf16[4,256,128]{2,1,0:T(8,128)(2,1)S(1)} %get-tuple-element.44), channel_id=1, source_target_pairs={{0,4},{1,5},{2,6},{3,7},{4,0},{5,1},{6,2},{7,3},{8,12},{9,13},{10,... | collective-permute-start | bytes 786440 | tf_op jit(solution)/shard_map/ppermute | solution.py:192
  18.7 0.0 collective-permute-done.3.refs_2_
  18.7 0.0 collective-permute-done.4.refs_3_
  18.7 1.4 %shard_map.97 = (bf16[4,256,128]{2,1,0:T(8,128)(2,1)S(1)}, f32[4,256,128]{2,1,0:T(8,128)S(1)}) custom-call(bf16[4,128,128]{2,1,0:T(8,128)(2,1)S(1)} %get-tuple-element.31.consts_ref, bf16[1024,1024]{1,0:T(8,128)(2,1)S(1)} %get-tuple-element.33.weights_ref, bf16[2,1,2,128,128]{4,3,2,1,0:T(8,128)(2,1)S(1)} %get-tuple-element.34.refs_0_, ...), custom_call_target="tpu_custom_call" | custom-call | flops 536870912 | bytes 3538944 | tf_op jit(solution)/shard_map/pallas_call | solution.py:50
  20.1 0.5 %collective-permute-start.5 = (bf16[4,256,128]{2,1,0:T(8,128)(2,1)S(1)}, bf16[4,256,128]{2,1,0:T(8,128)(2,1)S(1)}, u32[]{:S(2)}, u32[]{:S(2)}) collective-permute-start(bf16[4,256,128]{2,1,0:T(8,128)(2,1)S(1)} %get-tuple-element.37), channel_id=1, source_target_pairs={{0,4},{1,5},{2,6},{3,7},{4,0},{5,1},{6,2},{7,3},{8,12},{9,13},{10,... | collective-permute-start | bytes 786440 | tf_op jit(solution)/shard_map/ppermute | solution.py:192
  20.6 5.6 %collective-permute-done.9.got_ref = bf16[4,256,128]{2,1,0:T(8,128)(2,1)S(1)} collective-permute-done((bf16[4,256,128]{2,1,0:T(8,128)(2,1)S(1)}, bf16[4,256,128]{2,1,0:T(8,128)(2,1)S(1)}, u32[]{:S(2)}, u32[]{:S(2)}) %collective-permute-start.9) | collective-permute-done | bytes 262176 | tf_op jit(solution)/shard_map/ppermute | solution.py:192
  26.2 0.1 shard_map.101
  26.2 1.8 %collective-permute-start.10 = (bf16[2,256,128]{2,1,0:T(8,128)(2,1)S(1)}, bf16[2,256,128]{2,1,0:T(8,128)(2,1)S(1)}, u32[]{:S(2)}, u32[]{:S(2)}) collective-permute-start(bf16[2,256,128]{2,1,0:T(8,128)(2,1)S(1)} %get-tuple-element.46), channel_id=1, source_target_pairs={{0,8},{1,9},{2,10},{3,11},{4,12},{5,13},{6,14},{7,15},{8,0},{9,1},... | collective-permute-start | bytes 393224 | tf_op jit(solution)/shard_map/ppermute | solution.py:192
  28.0 3.2 %collective-permute-done.5.got_ref = bf16[4,256,128]{2,1,0:T(8,128)(2,1)S(1)} collective-permute-done((bf16[4,256,128]{2,1,0:T(8,128)(2,1)S(1)}, bf16[4,256,128]{2,1,0:T(8,128)(2,1)S(1)}, u32[]{:S(2)}, u32[]{:S(2)}) %collective-permute-start.5) | collective-permute-done | bytes 262176 | tf_op jit(solution)/shard_map/ppermute | solution.py:192
  31.2 0.1 shard_map.98
  31.3 1.9 %collective-permute-start.6 = (bf16[2,256,128]{2,1,0:T(8,128)(2,1)S(1)}, bf16[2,256,128]{2,1,0:T(8,128)(2,1)S(1)}, u32[]{:S(2)}, u32[]{:S(2)}) collective-permute-start(bf16[2,256,128]{2,1,0:T(8,128)(2,1)S(1)} %get-tuple-element.39), channel_id=1, source_target_pairs={{0,8},{1,9},{2,10},{3,11},{4,12},{5,13},{6,14},{7,15},{8,0},{9,1},... | collective-permute-start | bytes 393224 | tf_op jit(solution)/shard_map/ppermute | solution.py:192
  33.1 0.0 collective-permute-done.10.got_ref
  33.2 2.5 %collective-permute-start.12 = (bf16[1,256,128]{2,1,0:T(8,128)(2,1)S(1)}, bf16[1,256,128]{2,1,0:T(8,128)(2,1)S(1)}, u32[]{:S(2)}, u32[]{:S(2)}) collective-permute-start(bf16[1,256,128]{2,1,0:T(8,128)(2,1)S(1)} %get-tuple-element.49), channel_id=1, source_target_pairs={{0,24},{1,25},{2,26},{3,27},{4,28},{5,29},{6,30},{7,31},{8,16},{9,... | collective-permute-start | bytes 196616 | tf_op jit(solution)/shard_map/ppermute | solution.py:192
  35.7 0.6 %collective-permute-done.6.got_ref = bf16[2,256,128]{2,1,0:T(8,128)(2,1)S(1)} collective-permute-done((bf16[2,256,128]{2,1,0:T(8,128)(2,1)S(1)}, bf16[2,256,128]{2,1,0:T(8,128)(2,1)S(1)}, u32[]{:S(2)}, u32[]{:S(2)}) %collective-permute-start.6) | collective-permute-done | bytes 131104 | tf_op jit(solution)/shard_map/ppermute | solution.py:192
  36.4 4.5 %collective-permute-start.11 = (bf16[1,256,128]{2,1,0:T(8,128)(2,1)S(1)}, bf16[1,256,128]{2,1,0:T(8,128)(2,1)S(1)}, u32[]{:S(2)}, u32[]{:S(2)}) collective-permute-start(bf16[1,256,128]{2,1,0:T(8,128)(2,1)S(1)} %get-tuple-element.48), channel_id=1, source_target_pairs={{0,24},{1,25},{2,26},{3,27},{4,28},{5,29},{6,30},{7,31},{8,16},{9,... | collective-permute-start | bytes 196616 | tf_op jit(solution)/shard_map/ppermute | solution.py:192
  40.9 0.0 collective-permute-done.12.refs_3_
  40.9 2.2 %collective-permute-done.11.refs_2_ = bf16[1,256,128]{2,1,0:T(8,128)(2,1)S(1)} collective-permute-done((bf16[1,256,128]{2,1,0:T(8,128)(2,1)S(1)}, bf16[1,256,128]{2,1,0:T(8,128)(2,1)S(1)}, u32[]{:S(2)}, u32[]{:S(2)}) %collective-permute-start.11) | collective-permute-done | bytes 65568 | tf_op jit(solution)/shard_map/ppermute | solution.py:192
  43.2 1.2 %shard_map.103 = (bf16[4,128,128]{2,1,0:T(8,128)(2,1)}, bf16[4,128,128]{2,1,0:T(8,128)(2,1)}) custom-call(bf16[4,128,128]{2,1,0:T(8,128)(2,1)S(1)} %get-tuple-element.31.consts_ref, f32[4,128,128]{2,1,0:T(8,128)S(1)} %get-tuple-element.32.base_ref, f32[1,256,128]{2,1,0:T(8,128)S(1)} %get-tuple-element.40.refs_0_, ...), custom_call_target="tpu_custom_call" | custom-call | bytes 1048576 | tf_op jit(solution)/shard_map/pallas_call | solution.py:50
  (3 shorter events, 0.1 us)
Async XLA Ops:
  0.6 7.3 %collective-permute-start = (bf16[4,8,64,128]{3,2,1,0:T(8,128)(2,1)}, bf16[4,8,64,128]{3,2,1,0:T(8,128)(2,1)S(1)}, u32[]{:S(2)}, u32[]{:S(2)}) collective-permute-start(bf16[4,8,64,128]{3,2,1,0:T(8,128)(2,1)} %block_ref.1), channel_id=1, source_target_pairs={{0,2},{1,3},{2,0},{3,1},{4,6},{5,7},{6,4},{7,5},{8,10},{9,11},{10,... | collective-permute-start | bytes 1572872 | tf_op jit(solution)/shard_map/ppermute | solution.py:192
  1.2 1.0 %copy-start = (bf16[1024,2,128]{2,1,0:T(2,128)(2,1)S(1)}, bf16[1024,2,128]{2,1,0:T(2,128)(2,1)}, u32[]{:S(2)}) copy-start(bf16[1024,2,128]{2,1,0:T(2,128)(2,1)} %param.9) | copy-start | bytes 1572868
  2.3 3.2 %collective-permute-start.1 = (bf16[2,1,2,128,128]{4,3,2,1,0:T(8,128)(2,1)S(1)}, bf16[2,1,2,128,128]{4,3,2,1,0:T(8,128)(2,1)S(1)}, u32[]{:S(2)}, u32[]{:S(2)}) collective-permute-start(bf16[2,1,2,128,128]{4,3,2,1,0:T(8,128)(2,1)S(1)} %get-tuple-element.29), channel_id=1, source_target_pairs={{0,2},{1,3},{2,0},{3,1},{4,6},{5,7},{6,4},{7,5},{8,10},{9,11},{10,... | collective-permute-start | bytes 393224 | tf_op jit(solution)/shard_map/ppermute | solution.py:192
  2.4 4.9 %collective-permute-start.2 = (bf16[2,1,2,128,128]{4,3,2,1,0:T(8,128)(2,1)S(1)}, bf16[2,1,2,128,128]{4,3,2,1,0:T(8,128)(2,1)S(1)}, u32[]{:S(2)}, u32[]{:S(2)}) collective-permute-start(bf16[2,1,2,128,128]{4,3,2,1,0:T(8,128)(2,1)S(1)} %get-tuple-element.30), channel_id=1, source_target_pairs={{0,2},{1,3},{2,0},{3,1},{4,6},{5,7},{6,4},{7,5},{8,10},{9,11},{10,... | collective-permute-start | bytes 393224 | tf_op jit(solution)/shard_map/ppermute | solution.py:192
  2.8 12.6 %collective-permute-start.7 = (bf16[2,1,2,128,128]{4,3,2,1,0:T(8,128)(2,1)S(1)}, bf16[2,1,2,128,128]{4,3,2,1,0:T(8,128)(2,1)S(1)}, u32[]{:S(2)}, u32[]{:S(2)}) collective-permute-start(bf16[2,1,2,128,128]{4,3,2,1,0:T(8,128)(2,1)S(1)} %get-tuple-element.28.refs_1_), channel_id=1, source_target_pairs={{0,1},{1,0},{2,3},{3,2},{4,5},{5,4},{6,7},{7,6},{8,9},{9,8},{10,11... | collective-permute-start | bytes 393224 | tf_op jit(solution)/shard_map/ppermute | solution.py:192
  5.4 10.1 %collective-permute-start.8 = (bf16[2,1,2,128,128]{4,3,2,1,0:T(8,128)(2,1)S(1)}, bf16[2,1,2,128,128]{4,3,2,1,0:T(8,128)(2,1)S(1)}, u32[]{:S(2)}, u32[]{:S(2)}) collective-permute-start(bf16[2,1,2,128,128]{4,3,2,1,0:T(8,128)(2,1)S(1)} %get-tuple-element.30), channel_id=1, source_target_pairs={{0,3},{1,2},{2,1},{3,0},{4,7},{5,6},{6,5},{7,4},{8,11},{9,10},{10,... | collective-permute-start | bytes 393224 | tf_op jit(solution)/shard_map/ppermute | solution.py:192
  5.5 13.2 %collective-permute-start.3 = (bf16[2,1,2,128,128]{4,3,2,1,0:T(8,128)(2,1)S(1)}, bf16[2,1,2,128,128]{4,3,2,1,0:T(8,128)(2,1)S(1)}, u32[]{:S(2)}, u32[]{:S(2)}) collective-permute-start(bf16[2,1,2,128,128]{4,3,2,1,0:T(8,128)(2,1)S(1)} %get-tuple-element.27.refs_0_), channel_id=1, source_target_pairs={{0,1},{1,0},{2,3},{3,2},{4,5},{5,4},{6,7},{7,6},{8,9},{9,8},{10,11... | collective-permute-start | bytes 393224 | tf_op jit(solution)/shard_map/ppermute | solution.py:192
  7.2 11.4 %collective-permute-start.4 = (bf16[2,1,2,128,128]{4,3,2,1,0:T(8,128)(2,1)S(1)}, bf16[2,1,2,128,128]{4,3,2,1,0:T(8,128)(2,1)S(1)}, u32[]{:S(2)}, u32[]{:S(2)}) collective-permute-start(bf16[2,1,2,128,128]{4,3,2,1,0:T(8,128)(2,1)S(1)} %get-tuple-element.29), channel_id=1, source_target_pairs={{0,3},{1,2},{2,1},{3,0},{4,7},{5,6},{6,5},{7,4},{8,11},{9,10},{10,... | collective-permute-start | bytes 393224 | tf_op jit(solution)/shard_map/ppermute | solution.py:192
  7.9 1.0 %copy-start.1 = (bf16[4,8,64,128]{3,2,1,0:T(8,128)(2,1)S(1)}, bf16[4,8,64,128]{3,2,1,0:T(8,128)(2,1)}, u32[]{:S(2)}) copy-start(bf16[4,8,64,128]{3,2,1,0:T(8,128)(2,1)} %block_ref.1) | copy-start | bytes 1572868
  9.0 0.9 %copy-start.2 = (bf16[256,2,128]{2,1,0:T(2,128)(2,1)S(1)}, bf16[256,2,128]{2,1,0:T(2,128)(2,1)}, u32[]{:S(2)}) copy-start(bf16[256,2,128]{2,1,0:T(2,128)(2,1)} %param.10) | copy-start | bytes 393220
  9.9 0.8 %copy-start.3 = (f32[64,64]{1,0:T(8,128)S(1)}, f32[64,64]{1,0:T(8,128)}, u32[]{:S(2)}) copy-start(f32[64,64]{1,0:T(8,128)} %coupling_ref.1) | copy-start | bytes 49156
  10.6 0.7 %copy-start.4 = (bf16[64,64]{1,0:T(8,128)(2,1)S(1)}, bf16[64,64]{1,0:T(8,128)(2,1)}, u32[]{:S(2)}) copy-start(bf16[64,64]{1,0:T(8,128)(2,1)} %ham_ref.1) | copy-start | bytes 24580
  11.3 0.7 %copy-start.5 = (s32[64]{0:T(128)S(1)}, s32[64]{0:T(128)}, u32[]{:S(2)}) copy-start(s32[64]{0:T(128)} %deal_ref.1) | copy-start | bytes 772
  12.0 0.7 %copy-start.6 = (s32[16]{0:T(128)S(1)}, s32[16]{0:T(128)}, u32[]{:S(2)}) copy-start(s32[16]{0:T(128)} %columns_ref.1) | copy-start | bytes 196
  16.9 9.2 %collective-permute-start.9 = (bf16[4,256,128]{2,1,0:T(8,128)(2,1)S(1)}, bf16[4,256,128]{2,1,0:T(8,128)(2,1)S(1)}, u32[]{:S(2)}, u32[]{:S(2)}) collective-permute-start(bf16[4,256,128]{2,1,0:T(8,128)(2,1)S(1)} %get-tuple-element.44), channel_id=1, source_target_pairs={{0,4},{1,5},{2,6},{3,7},{4,0},{5,1},{6,2},{7,3},{8,12},{9,13},{10,... | collective-permute-start | bytes 786440 | tf_op jit(solution)/shard_map/ppermute | solution.py:192
  20.1 11.1 %collective-permute-start.5 = (bf16[4,256,128]{2,1,0:T(8,128)(2,1)S(1)}, bf16[4,256,128]{2,1,0:T(8,128)(2,1)S(1)}, u32[]{:S(2)}, u32[]{:S(2)}) collective-permute-start(bf16[4,256,128]{2,1,0:T(8,128)(2,1)S(1)} %get-tuple-element.37), channel_id=1, source_target_pairs={{0,4},{1,5},{2,6},{3,7},{4,0},{5,1},{6,2},{7,3},{8,12},{9,13},{10,... | collective-permute-start | bytes 786440 | tf_op jit(solution)/shard_map/ppermute | solution.py:192
  26.2 6.9 %collective-permute-start.10 = (bf16[2,256,128]{2,1,0:T(8,128)(2,1)S(1)}, bf16[2,256,128]{2,1,0:T(8,128)(2,1)S(1)}, u32[]{:S(2)}, u32[]{:S(2)}) collective-permute-start(bf16[2,256,128]{2,1,0:T(8,128)(2,1)S(1)} %get-tuple-element.46), channel_id=1, source_target_pairs={{0,8},{1,9},{2,10},{3,11},{4,12},{5,13},{6,14},{7,15},{8,0},{9,1},... | collective-permute-start | bytes 393224 | tf_op jit(solution)/shard_map/ppermute | solution.py:192
  31.3 5.1 %collective-permute-start.6 = (bf16[2,256,128]{2,1,0:T(8,128)(2,1)S(1)}, bf16[2,256,128]{2,1,0:T(8,128)(2,1)S(1)}, u32[]{:S(2)}, u32[]{:S(2)}) collective-permute-start(bf16[2,256,128]{2,1,0:T(8,128)(2,1)S(1)} %get-tuple-element.39), channel_id=1, source_target_pairs={{0,8},{1,9},{2,10},{3,11},{4,12},{5,13},{6,14},{7,15},{8,0},{9,1},... | collective-permute-start | bytes 393224 | tf_op jit(solution)/shard_map/ppermute | solution.py:192
  33.2 7.8 %collective-permute-start.12 = (bf16[1,256,128]{2,1,0:T(8,128)(2,1)S(1)}, bf16[1,256,128]{2,1,0:T(8,128)(2,1)S(1)}, u32[]{:S(2)}, u32[]{:S(2)}) collective-permute-start(bf16[1,256,128]{2,1,0:T(8,128)(2,1)S(1)} %get-tuple-element.49), channel_id=1, source_target_pairs={{0,24},{1,25},{2,26},{3,27},{4,28},{5,29},{6,30},{7,31},{8,16},{9,... | collective-permute-start | bytes 196616 | tf_op jit(solution)/shard_map/ppermute | solution.py:192
  36.4 6.8 %collective-permute-start.11 = (bf16[1,256,128]{2,1,0:T(8,128)(2,1)S(1)}, bf16[1,256,128]{2,1,0:T(8,128)(2,1)S(1)}, u32[]{:S(2)}, u32[]{:S(2)}) collective-permute-start(bf16[1,256,128]{2,1,0:T(8,128)(2,1)S(1)} %get-tuple-element.48), channel_id=1, source_target_pairs={{0,24},{1,25},{2,26},{3,27},{4,28},{5,29},{6,30},{7,31},{8,16},{9,... | collective-permute-start | bytes 196616 | tf_op jit(solution)/shard_map/ppermute | solution.py:192

commit v3 on v1

--- a/solution.py
+++ b/solution.py
@@ -7,8 +7,10 @@
 from jax.experimental.pallas import tpu as pltpu
 from jax.sharding import PartitionSpec as P
 
+
 P_SIZE = 8
 CHUNKS = 2
+PREFETCH_FLOPS = 2_000_000_000
 
 
 time_step = 0.02
@@ -45,12 +47,13 @@
     return (-flat * screening).reshape(n, rows, lanes)
 
 
-def call(body, outs, *args, flops=0, **keywords):
+def call(body, outs, *args, flops=0, grant=16, **keywords):
     moved = sum(a.size * a.dtype.itemsize for a in list(args) + list(outs))
     return pl.pallas_call(
         body,
         out_shape=outs,
         cost_estimate=pl.CostEstimate(flops=flops, bytes_accessed=moved, transcendentals=0),
+        compiler_params=pltpu.CompilerParams(vmem_limit_bytes=grant << 20),
         **keywords,
     )(*args)
 
@@ -59,16 +62,22 @@
     return jax.ShapeDtypeStruct(tuple(dims), kind)
 
 
-def split_body(rows_ref, *outs):
+def split_body(rows_ref, *refs):
     core = lax.axis_index("mem") & 1
-    parts = len(outs) // 2
-    for c in range(parts):
-        size = outs[2 * c].shape[2]
-        outs[2 * c][...] = rows_ref[:, :, core, c * size:(c + 1) * size]
-        outs[2 * c + 1][...] = rows_ref[:, :, 1 - core, c * size:(c + 1) * size]
-
-
-def early_body(n_early, slot_of, groups, chunks, deal_ref, columns_ref, start_ref, block_ref, other_ref, coupling_ref, ham_ref, panel_ref, *refs):
+    outs, sems = refs[:-1], refs[-1]
+    copies = []
+    for at, out in enumerate(outs):
+        size = out.shape[2]
+        first = (at // 2) * size
+        half = core if at % 2 == 0 else 1 - core
+        copies.append(pltpu.make_async_copy(rows_ref.at[:, :, half, first:first + size], out, sems.at[at]))
+    for copy in copies:
+        copy.start()
+    for copy in copies:
+        copy.wait()
+
+
+def early_body(n_early, slot_of, groups, chunks, deal_ref, columns_ref, start_ref, coupling_ref, ham_ref, panel_ref, block_ref, other_ref, *refs):
     early = refs[:n_early * chunks]
     weights_ref, consts_ref, base_ref = refs[n_early * chunks:n_early * chunks + 3]
     sigmas = refs[n_early * chunks + 3:]
@@ -76,7 +85,7 @@
     rows = consts_ref.shape[1]
     panels = rows // orbitals
     mem, hist = lax.axis_index("mem"), lax.axis_index("hist")
-    core, pair = mem & 1, mem >> 1
+    pair = mem >> 1
     slots, columns = block_ref.shape[0], block_ref.shape[1]
 
     spread = (lax.broadcasted_iota(jnp.int32, (rows, orbitals), 0) // panels == lax.broadcasted_iota(jnp.int32, (rows, orbitals), 1)).astype(F32)
@@ -100,17 +109,17 @@
         consts_ref[at] = value
     consts = (right_top, right_low, left_top, left_low)
 
+    for at in range(n_early * chunks):
+        source = early[at]
+        tiles = sigma_tiles(source[...].reshape((-1,) + source.shape[3:]), consts)
+        sigmas[at][...] = tiles.astype(BF16).reshape(source.shape)
+
     ham = rowed(ham_ref[...].astype(F32)).astype(BF16)
     sign = jnp.where(lax.broadcasted_iota(jnp.int32, (rows, lanes), 1) < orbitals, 1.0, -1.0).astype(F32)
     for tile in range(panel_ref.shape[0]):
         values = panel_ref[tile]
         turned = pltpu.roll(dot(ham, values), orbitals, 1) * sign
         base_ref[tile] = values.astype(F32) + time_step * turned
-
-    for at in range(n_early * chunks):
-        source = early[at]
-        tiles = sigma_tiles(source[...].reshape((-1,) + source.shape[3:]), consts)
-        sigmas[at][...] = tiles.astype(BF16).reshape(source.shape)
 
     flip = jnp.where(lax.broadcasted_iota(jnp.int32, (orbitals, lanes), 1) < orbitals, -1.0, 1.0).astype(F32)
     own_column = pair // groups
@@ -129,13 +138,13 @@
             weights_ref[q * lanes + orbitals:(q + 1) * lanes, apart * lanes:(apart + 1) * lanes] = lower.astype(BF16)
 
 
-def term_body(n_done, n_late, order, groups, consts_ref, weights_ref, *refs):
+def term_body(n_done, n_late, places, groups, consts_ref, weights_ref, *refs):
     done, late = refs[:n_done], refs[n_done:n_done + n_late]
-    send_ref, keep_ref, left_ref = refs[n_done + n_late:]
+    outs, left_ref = refs[n_done + n_late:-1], refs[-1]
     pair = lax.axis_index("mem") >> 1
     own_group = pair % groups
     consts = tuple(consts_ref[at] for at in range(4))
-    rows, lanes = send_ref.shape[1:]
+    rows, lanes = outs[0].shape[1:]
     for step in range(groups):
         group = own_group ^ step
         q = 0
@@ -148,41 +157,62 @@
                 left_ref[:, q * lanes:(q + 1) * lanes] = tiles[s].reshape(rows, lanes)
                 q += 1
         total = dot(left_ref[...], weights_ref[...])
-        for place, block in enumerate(order):
-            if block % groups != step:
-                continue
-            apart = block // groups
-            value = total[:, apart * lanes:(apart + 1) * lanes]
-            if place < len(order) // 2:
-                send_ref[place] = value.astype(BF16)
-            else:
-                keep_ref[place - len(order) // 2] = value
-
-
-def add_body(keep_ref, got_ref, send_ref, next_ref):
-    half = send_ref.shape[0]
-    send_ref[...] = (keep_ref[:half] + got_ref[:half].astype(F32)).astype(BF16)
-    next_ref[...] = keep_ref[half:] + got_ref[half:].astype(F32)
-
-
-def last_body(chunks, consts_ref, base_ref, *refs):
-    keeps, gots = refs[:chunks], refs[chunks:2 * chunks]
-    rows_ref, sigma_ref = refs[2 * chunks:]
+        for block, (to, place) in places.items():
+            if block % groups == step:
+                apart = block // groups
+                value = total[:, apart * lanes:(apart + 1) * lanes]
+                outs[to][place] = value.astype(outs[to].dtype)
+
+
+def add_body(n_got, keep_ref, *refs):
+    gots, outs = refs[:n_got], refs[n_got:]
+    total = keep_ref[...]
+    for got in gots:
+        total = total + got[...].astype(F32)
+    size = outs[0].shape[0]
+    for at, out in enumerate(outs):
+        out[...] = total[at * size:(at + 1) * size].astype(out.dtype)
+
+
+def last_body(chunks, n_got, consts_ref, base_ref, *refs):
+    keeps, gots = refs[:chunks], refs[chunks:chunks + chunks * n_got]
+    rows_ref, sigma_ref = refs[chunks + chunks * n_got:]
     consts = tuple(consts_ref[at] for at in range(4))
     size = base_ref.shape[0] // chunks
     for c in range(chunks):
         here = slice(c * size, (c + 1) * size)
-        collision = (keeps[c][...] + gots[c][...].astype(F32)).reshape((size,) + base_ref.shape[1:])
+        collision = keeps[c][...]
+        for got in gots[c * n_got:(c + 1) * n_got]:
+            collision = collision + got[...].astype(F32)
+        collision = collision.reshape((size,) + base_ref.shape[1:])
         rows = (base_ref[here] + time_step * collision).astype(BF16)
         rows_ref[here] = rows
         sigma_ref[here] = sigma_tiles(rows, consts).astype(BF16)
 
 
-def block_order(count, masks):
-    order = [0]
-    for mask in reversed(masks):
-        order = [block ^ mask for block in order] + order
-    return order
+def step_masks(count):
+    bits = [1 << b for b in range(count.bit_length() - 1)]
+    steps = []
+    while bits:
+        take = 1 if len(bits) % 2 else 2
+        here, bits = bits[:take], bits[take:]
+        masks = [0]
+        for bit in here:
+            masks = masks + [mask ^ bit for mask in masks]
+        steps.append(masks[2:] + masks[1:2] + [0] if take == 2 else masks[::-1])
+    return steps
+
+
+def block_places(steps, parts):
+    def spread(rest):
+        if not rest:
+            return [0]
+        inner = spread(rest[1:])
+        return [mask ^ block for mask in rest[0] for block in inner]
+
+    inner = spread(steps[1:])
+    size = len(inner) // parts
+    return {mask ^ block: (place // size * len(steps[0]) + to, place % size) for to, mask in enumerate(steps[0]) for place, block in enumerate(inner)}
 
 
 def exchange(value, mem_mask, hist_mask):
@@ -210,7 +240,17 @@
     tiles = memory_rows.reshape(held, groups, 2, own_tiles, rows, lanes)
     panel_tiles = panel_rows.reshape(own_tiles, rows, lanes)
     piece = shape((held, groups, part, rows, lanes), BF16)
-    split = call(split_body, [piece] * (2 * chunks), tiles)
+    hbm = pl.BlockSpec(memory_space=pltpu.HBM)
+    smem = pl.BlockSpec(memory_space=pltpu.SMEM)
+    vmem = pl.BlockSpec(memory_space=pltpu.VMEM)
+    split = call(
+        split_body,
+        [piece] * (2 * chunks),
+        tiles,
+        in_specs=[hbm],
+        flops=PREFETCH_FLOPS,
+        scratch_shapes=[pltpu.SemaphoreType.DMA((2 * chunks,))],
+    )
     mine, other = split[0::2], split[1::2]
 
     if two_hist:
@@ -229,8 +269,6 @@
     early = [mine, partner]
     n_early = len(early)
     flat_early = [array for source in early for array in source]
-    smem = pl.BlockSpec(memory_space=pltpu.SMEM)
-    vmem = pl.BlockSpec(memory_space=pltpu.VMEM)
     outs = [
         shape((2 * slots * lanes, columns * lanes), BF16),
         shape((4, rows, lanes), BF16),
@@ -239,43 +277,50 @@
     weights, consts, base, *sigmas = call(
         functools.partial(early_body, n_early, slot_of, groups, chunks),
         outs,
-        time_deal, column_times, window_start, memory_block, partner_block, coupling, hamiltonian, panel_tiles, *flat_early,
+        time_deal, column_times, window_start, coupling, hamiltonian, panel_tiles, memory_block, partner_block, *flat_early,
         in_specs=[smem] * 3 + [vmem] * (5 + n_early * chunks),
     )
 
-    bits = [1 << b for b in range(pairs.bit_length() - 1)]
-    if len(bits) > 1:
-        bits[-1] |= bits[-2]
-    finals = []
+    steps = step_masks(pairs)
+    parts = 2 if len(steps) > 1 else 1
+    keeps, received = [], []
     for c in range(chunks):
-        masks = list(bits)
-        order = block_order(pairs, masks)
         height = part * rows
         done = [sigmas[e * chunks + c] for e in range(n_early)]
         late = [same_core[c], cross[c]] if two_hist else []
-        send, keep = call(
-            functools.partial(term_body, len(done), len(late), order, groups),
-            [shape((pairs // 2, height, lanes), BF16), shape((pairs // 2, height, lanes), F32)],
+        count = pairs // len(steps[0]) // parts
+
+        def pieces(masks, count):
+            return [shape((count, height, lanes), BF16 if mask else F32) for mask in masks]
+
+        outs = call(
+            functools.partial(term_body, len(done), len(late), block_places(steps, parts), groups),
+            pieces(steps[0], count) * parts,
             consts, weights, *done, *late,
             flops=2 * height * groups * 2 * slots * lanes * columns * lanes,
             scratch_shapes=[pltpu.VMEM((height, 2 * slots * lanes), BF16)],
         )
-        for at, mask in enumerate(masks):
-            got = exchange(send, 2 * mask, 0)
-            if at + 1 < len(masks):
-                half = keep.shape[0] // 2
-                send, keep = call(
-                    add_body,
-                    [shape((half, height, lanes), BF16), shape((half, height, lanes), F32)],
-                    keep, got,
-                )
-        finals.append((keep, got))
+        size = len(steps[0])
+        state = [(outs[p * size:(p + 1) * size - 1], outs[(p + 1) * size - 1]) for p in range(parts)]
+        for at, masks in enumerate(steps):
+            gots = [[exchange(sends[i], 2 * masks[i], 0) for i in range(len(sends))] for sends, _ in state]
+            if at + 1 == len(steps):
+                break
+            after = steps[at + 1]
+            share = len(after) // len(state)
+            count = count * len(state) // len(after)
+            outs = []
+            for p, (_, keep) in enumerate(state):
+                outs += call(functools.partial(add_body, len(gots[p])), pieces(after[p * share:(p + 1) * share], count), keep, *gots[p])
+            state = [(outs[:-1], outs[-1])]
+        keeps.append(state[0][1])
+        received += gots[0]
 
     result = shape((own_tiles, rows, lanes), BF16)
     new_rows, new_sigma = call(
-        functools.partial(last_body, chunks),
+        functools.partial(last_body, chunks, len(received) // chunks),
         [result, result],
-        consts, base, *[keep for keep, _ in finals], *[got for _, got in finals],
+        consts, base, *keeps, *received,
     )
     return new_rows.reshape(panel_rows.shape), new_sigma.reshape(panel_rows.shape)
 

time: 55 us -> 40.5 us (0.74)
  Pallas kernels: 24.3 us -> 7.57 us
  starting transfers between devices: 15.7 us -> 22 us
  local copies, waits for them, and re-layouts: 5.46 us -> 1.06 us
    pallas_call x9, Pallas kernels: 24.3 us -> 7.57 us  [call(): pl.pallas_call(body, out_shape=outs, cost_estimate=pl.CostEstimate(flops=...]
    ppermute x13 -> x17, starting transfers between devices: 15.7 us -> 22 us  [exchange(): return lax.ppermute(value, ('mem', 'hist'), pairs)]
    unnamed x26 -> x14, local copies, waits for them, and re-layouts: 5.46 us -> 1.06 us
    ppermute x13 -> x17, waiting for transfers between devices: 7.77 us -> 8.31 us  [exchange(): return lax.ppermute(value, ('mem', 'hist'), pairs)]
  transfers between devices with their start and end apart: 13 -> 17, of which waited for: 3 -> 6; matrix products, arithmetic and copies ran while one was open for 0% -> 0% of each run, Pallas kernels for 40% -> 16%
where the time goes in v3:
time: 40.5 us; the launch traced here: 40.4 us
  starting transfers between devices  22 us (54%)
  waiting for transfers between devices  8.31 us (21%)
  Pallas kernels  7.57 us (19%)
  between operations  1.44 us (4%)
  local copies, waits for them, and re-layouts  1.06 us (3%)
    ppermute x17, starting transfers between devices, exchange(): return lax.ppermute(value, ('mem', 'hist'), pairs)  22 us
    ppermute x17, waiting for transfers between devices, exchange(): return lax.ppermute(value, ('mem', 'hist'), pairs)  8.31 us
    pallas_call x9, Pallas kernels, call(): pl.pallas_call(body, out_shape=outs, cost_estimate=pl.CostEstimate(flops=...  7.57 us
    unnamed x14, local copies, waits for them, and re-layouts  1.06 us
  transfers between devices with their start and end apart: 17, of which 6 were waited for; matrix products, arithmetic and copies ran while one was open for 0% of the time, Pallas kernels for 16%

profile of v3, /device:TPU:0, one launch (start us, length us, event | category | flops | bytes accessed | tf_op | source)
XLA Modules:
  0.0 40.4 jit_solution(8665369301672886932)
XLA Ops:
  0.6 0.6 %collective-permute-start = (bf16[4,8,64,128]{3,2,1,0:T(8,128)(2,1)}, bf16[4,8,64,128]{3,2,1,0:T(8,128)(2,1)S(1)}, u32[]{:S(2)}, u32[]{:S(2)}) collective-permute-start(bf16[4,8,64,128]{3,2,1,0:T(8,128)(2,1)} %block_ref.1), channel_id=1, source_target_pairs={{0,2},{1,3},{2,0},{3,1},{4,6},{5,7},{6,4},{7,5},{8,10},{9,11},{10,... | collective-permute-start | bytes 1572872 | tf_op jit(solution)/shard_map/ppermute | solution.py:221
  1.2 1.0 %copy-done.6 = bf16[1024,2,128]{2,1,0:T(2,128)(2,1)S(1)} copy-done((bf16[1024,2,128]{2,1,0:T(2,128)(2,1)S(1)}, bf16[1024,2,128]{2,1,0:T(2,128)(2,1)}, u32[]{:S(2)}) %copy-start.6) | copy-done | bytes 524312
  2.2 0.0 copy-start.4
  2.3 0.0 copy-start.5
  2.3 0.4 shard_map.95
  2.7 0.1 collective-permute-start.1
  2.7 0.5 %collective-permute-start.2 = (bf16[2,1,2,128,128]{4,3,2,1,0:T(8,128)(2,1)S(1)}, bf16[2,1,2,128,128]{4,3,2,1,0:T(8,128)(2,1)S(1)}, u32[]{:S(2)}, u32[]{:S(2)}) collective-permute-start(bf16[2,1,2,128,128]{4,3,2,1,0:T(8,128)(2,1)S(1)} %get-tuple-element.34), channel_id=1, source_target_pairs={{0,2},{1,3},{2,0},{3,1},{4,6},{5,7},{6,4},{7,5},{8,10},{9,11},{10,... | collective-permute-start | bytes 393224 | tf_op jit(solution)/shard_map/ppermute | solution.py:221
  3.2 2.6 %collective-permute-start.6 = (bf16[2,1,2,128,128]{4,3,2,1,0:T(8,128)(2,1)S(1)}, bf16[2,1,2,128,128]{4,3,2,1,0:T(8,128)(2,1)S(1)}, u32[]{:S(2)}, u32[]{:S(2)}) collective-permute-start(bf16[2,1,2,128,128]{4,3,2,1,0:T(8,128)(2,1)S(1)} %get-tuple-element.32.refs_1_), channel_id=1, source_target_pairs={{0,1},{1,0},{2,3},{3,2},{4,5},{5,4},{6,7},{7,6},{8,9},{9,8},{10,11... | collective-permute-start | bytes 393224 | tf_op jit(solution)/shard_map/ppermute | solution.py:221
  5.8 0.0 collective-permute-start.7
  5.9 0.0 collective-permute-done.1.refs_2_
  5.9 1.7 %collective-permute-start.3 = (bf16[2,1,2,128,128]{4,3,2,1,0:T(8,128)(2,1)S(1)}, bf16[2,1,2,128,128]{4,3,2,1,0:T(8,128)(2,1)S(1)}, u32[]{:S(2)}, u32[]{:S(2)}) collective-permute-start(bf16[2,1,2,128,128]{4,3,2,1,0:T(8,128)(2,1)S(1)} %get-tuple-element.31.refs_0_), channel_id=1, source_target_pairs={{0,1},{1,0},{2,3},{3,2},{4,5},{5,4},{6,7},{7,6},{8,9},{9,8},{10,11... | collective-permute-start | bytes 393224 | tf_op jit(solution)/shard_map/ppermute | solution.py:221
  7.6 0.0 collective-permute-done.2.refs_3_
  7.6 0.0 collective-permute-start.4
  8.3 0.0 collective-permute-done.other_ref
  8.3 0.0 copy-done
  8.3 0.0 copy-done.1
  8.3 0.0 copy-done.2
  8.3 0.0 copy-done.3
  8.3 0.0 copy-done.4
  8.4 0.0 copy-done.5
  8.4 3.0 %shard_map.96 = (bf16[1024,1024]{1,0:T(8,128)(2,1)S(1)}, bf16[4,128,128]{2,1,0:T(8,128)(2,1)S(1)}, f32[4,128,128]{2,1,0:T(8,128)S(1)}, bf16[2,1,2,128,128]{4,3,2...) custom-call(s32[64]{0:T(128)S(1)} %copy-done.4, ...), custom_call_target="tpu_custom_call" | custom-call | bytes 4743492 | tf_op jit(solution)/shard_map/pallas_call | solution.py:52
  11.4 0.0 collective-permute-done.6.refs_2_
  11.4 1.1 %collective-permute-done.7.refs_3_ = bf16[2,1,2,128,128]{4,3,2,1,0:T(8,128)(2,1)S(1)} collective-permute-done((bf16[2,1,2,128,128]{4,3,2,1,0:T(8,128)(2,1)S(1)}, bf16[2,1,2,128,128]{4,3,2,1,0:T(8,128)(2,1)S(1)}, u32[]{:S(2)}, u32[]{:S(2)}) %collective-permute-start.7) | collective-permute-done | bytes 131104 | tf_op jit(solution)/shard_map/ppermute | solution.py:221
  12.5 1.4 %shard_map.99 = (bf16[2,256,128]{2,1,0:T(8,128)(2,1)S(1)}, f32[2,256,128]{2,1,0:T(8,128)S(1)}, bf16[2,256,128]{2,1,0:T(8,128)(2,1)S(1)}, f32[2,256,128]{2,1,0:T(8,128)S(1)}) custom-call(bf16[4,128,128]{2,1,0:T(8,128)(2,1)S(1)} %get-tuple-element.35.consts_ref, bf16[1024,1024]{1,0:T(8,128)(2,1)S(1)} %get-tuple-element.37.weights_ref, ...), custom_call_target="tpu_custom_call" | custom-call | flops 536870912 | bytes 3538944 | tf_op jit(solution)/shard_map/pallas_call | solution.py:52
  13.9 1.6 %collective-permute-start.13 = (bf16[2,256,128]{2,1,0:T(8,128)(2,1)S(1)}, bf16[2,256,128]{2,1,0:T(8,128)(2,1)S(1)}, u32[]{:S(2)}, u32[]{:S(2)}) collective-permute-start(bf16[2,256,128]{2,1,0:T(8,128)(2,1)S(1)} %get-tuple-element.54), channel_id=1, source_target_pairs={{0,4},{1,5},{2,6},{3,7},{4,0},{5,1},{6,2},{7,3},{8,12},{9,13},{10,... | collective-permute-start | bytes 393224 | tf_op jit(solution)/shard_map/ppermute | solution.py:221
  15.5 0.3 collective-permute-done.3.refs_2_
  15.8 2.3 %collective-permute-done.4.refs_3_ = bf16[2,1,2,128,128]{4,3,2,1,0:T(8,128)(2,1)S(1)} collective-permute-done((bf16[2,1,2,128,128]{4,3,2,1,0:T(8,128)(2,1)S(1)}, bf16[2,1,2,128,128]{4,3,2,1,0:T(8,128)(2,1)S(1)}, u32[]{:S(2)}, u32[]{:S(2)}) %collective-permute-start.4) | collective-permute-done | bytes 131104 | tf_op jit(solution)/shard_map/ppermute | solution.py:221
  18.1 1.4 %shard_map.97 = (bf16[2,256,128]{2,1,0:T(8,128)(2,1)S(1)}, f32[2,256,128]{2,1,0:T(8,128)S(1)}, bf16[2,256,128]{2,1,0:T(8,128)(2,1)S(1)}, f32[2,256,128]{2,1,0:T(8,128)S(1)}) custom-call(bf16[4,128,128]{2,1,0:T(8,128)(2,1)S(1)} %get-tuple-element.35.consts_ref, bf16[1024,1024]{1,0:T(8,128)(2,1)S(1)} %get-tuple-element.37.weights_ref, ...), custom_call_target="tpu_custom_call" | custom-call | flops 536870912 | bytes 3538944 | tf_op jit(solution)/shard_map/pallas_call | solution.py:52
  19.5 1.5 %collective-permute-start.9 = (bf16[2,256,128]{2,1,0:T(8,128)(2,1)S(1)}, bf16[2,256,128]{2,1,0:T(8,128)(2,1)S(1)}, u32[]{:S(2)}, u32[]{:S(2)}) collective-permute-start(bf16[2,256,128]{2,1,0:T(8,128)(2,1)S(1)} %get-tuple-element.49), channel_id=1, source_target_pairs={{0,4},{1,5},{2,6},{3,7},{4,0},{5,1},{6,2},{7,3},{8,12},{9,13},{10,... | collective-permute-start | bytes 393224 | tf_op jit(solution)/shard_map/ppermute | solution.py:221
  21.0 0.6 %collective-permute-start.8 = (bf16[2,256,128]{2,1,0:T(8,128)(2,1)S(1)}, bf16[2,256,128]{2,1,0:T(8,128)(2,1)S(1)}, u32[]{:S(2)}, u32[]{:S(2)}) collective-permute-start(bf16[2,256,128]{2,1,0:T(8,128)(2,1)S(1)} %get-tuple-element.46), channel_id=1, source_target_pairs={{0,4},{1,5},{2,6},{3,7},{4,0},{5,1},{6,2},{7,3},{8,12},{9,13},{10,... | collective-permute-start | bytes 393224 | tf_op jit(solution)/shard_map/ppermute | solution.py:221
  21.6 1.4 %collective-permute-start.5 = (bf16[2,256,128]{2,1,0:T(8,128)(2,1)S(1)}, bf16[2,256,128]{2,1,0:T(8,128)(2,1)S(1)}, u32[]{:S(2)}, u32[]{:S(2)}) collective-permute-start(bf16[2,256,128]{2,1,0:T(8,128)(2,1)S(1)} %get-tuple-element.41), channel_id=1, source_target_pairs={{0,4},{1,5},{2,6},{3,7},{4,0},{5,1},{6,2},{7,3},{8,12},{9,13},{10,... | collective-permute-start | bytes 393224 | tf_op jit(solution)/shard_map/ppermute | solution.py:221
  23.0 0.0 collective-permute-done.13.refs_0_
  23.1 2.7 %collective-permute-start.14 = (bf16[1,256,128]{2,1,0:T(8,128)(2,1)S(1)}, bf16[1,256,128]{2,1,0:T(8,128)(2,1)S(1)}, u32[]{:S(2)}, u32[]{:S(2)}) collective-permute-start(bf16[1,256,128]{2,1,0:T(8,128)(2,1)S(1)} %get-tuple-element.55), channel_id=1, source_target_pairs={{0,16},{1,17},{2,18},{3,19},{4,20},{5,21},{6,22},{7,23},{8,24},{9,... | collective-permute-start | bytes 196616 | tf_op jit(solution)/shard_map/ppermute | solution.py:221
  25.7 1.3 %collective-permute-start.15 = (bf16[1,256,128]{2,1,0:T(8,128)(2,1)S(1)}, bf16[1,256,128]{2,1,0:T(8,128)(2,1)S(1)}, u32[]{:S(2)}, u32[]{:S(2)}) collective-permute-start(bf16[1,256,128]{2,1,0:T(8,128)(2,1)S(1)} %get-tuple-element.56), channel_id=1, source_target_pairs={{0,24},{1,25},{2,26},{3,27},{4,28},{5,29},{6,30},{7,31},{8,16},{9,... | collective-permute-start | bytes 196616 | tf_op jit(solution)/shard_map/ppermute | solution.py:221
  27.1 0.0 collective-permute-done.9.refs_0_
  27.1 1.8 %collective-permute-start.10 = (bf16[1,256,128]{2,1,0:T(8,128)(2,1)S(1)}, bf16[1,256,128]{2,1,0:T(8,128)(2,1)S(1)}, u32[]{:S(2)}, u32[]{:S(2)}) collective-permute-start(bf16[1,256,128]{2,1,0:T(8,128)(2,1)S(1)} %get-tuple-element.50), channel_id=1, source_target_pairs={{0,16},{1,17},{2,18},{3,19},{4,20},{5,21},{6,22},{7,23},{8,24},{9,... | collective-permute-start | bytes 196616 | tf_op jit(solution)/shard_map/ppermute | solution.py:221
  28.9 0.0 collective-permute-done.8.refs_0_
  28.9 3.4 %collective-permute-start.11 = (bf16[1,256,128]{2,1,0:T(8,128)(2,1)S(1)}, bf16[1,256,128]{2,1,0:T(8,128)(2,1)S(1)}, u32[]{:S(2)}, u32[]{:S(2)}) collective-permute-start(bf16[1,256,128]{2,1,0:T(8,128)(2,1)S(1)} %get-tuple-element.51), channel_id=1, source_target_pairs={{0,24},{1,25},{2,26},{3,27},{4,28},{5,29},{6,30},{7,31},{8,16},{9,... | collective-permute-start | bytes 196616 | tf_op jit(solution)/shard_map/ppermute | solution.py:221
  32.3 0.0 collective-permute-done.5.refs_0_
  32.3 0.4 %collective-permute-start.16 = (bf16[1,256,128]{2,1,0:T(8,128)(2,1)S(1)}, bf16[1,256,128]{2,1,0:T(8,128)(2,1)S(1)}, u32[]{:S(2)}, u32[]{:S(2)}) collective-permute-start(bf16[1,256,128]{2,1,0:T(8,128)(2,1)S(1)} %get-tuple-element.57), channel_id=1, source_target_pairs={{0,8},{1,9},{2,10},{3,11},{4,12},{5,13},{6,14},{7,15},{8,0},{9,1},... | collective-permute-start | bytes 196616 | tf_op jit(solution)/shard_map/ppermute | solution.py:221
  32.8 0.0 collective-permute-done.14.refs_5_
  32.8 1.7 %collective-permute-start.12 = (bf16[1,256,128]{2,1,0:T(8,128)(2,1)S(1)}, bf16[1,256,128]{2,1,0:T(8,128)(2,1)S(1)}, u32[]{:S(2)}, u32[]{:S(2)}) collective-permute-start(bf16[1,256,128]{2,1,0:T(8,128)(2,1)S(1)} %get-tuple-element.52), channel_id=1, source_target_pairs={{0,8},{1,9},{2,10},{3,11},{4,12},{5,13},{6,14},{7,15},{8,0},{9,1},... | collective-permute-start | bytes 196616 | tf_op jit(solution)/shard_map/ppermute | solution.py:221
  34.5 0.0 collective-permute-done.15.refs_6_
  34.5 2.3 %collective-permute-done.10.refs_2_ = bf16[1,256,128]{2,1,0:T(8,128)(2,1)S(1)} collective-permute-done((bf16[1,256,128]{2,1,0:T(8,128)(2,1)S(1)}, bf16[1,256,128]{2,1,0:T(8,128)(2,1)S(1)}, u32[]{:S(2)}, u32[]{:S(2)}) %collective-permute-start.10) | collective-permute-done | bytes 65568 | tf_op jit(solution)/shard_map/ppermute | solution.py:221
  36.8 0.0 collective-permute-done.11.refs_3_
  36.8 1.1 %collective-permute-done.16.refs_7_ = bf16[1,256,128]{2,1,0:T(8,128)(2,1)S(1)} collective-permute-done((bf16[1,256,128]{2,1,0:T(8,128)(2,1)S(1)}, bf16[1,256,128]{2,1,0:T(8,128)(2,1)S(1)}, u32[]{:S(2)}, u32[]{:S(2)}) %collective-permute-start.16) | collective-permute-done | bytes 65568 | tf_op jit(solution)/shard_map/ppermute | solution.py:221
  38.0 1.1 %collective-permute-done.12.refs_4_ = bf16[1,256,128]{2,1,0:T(8,128)(2,1)S(1)} collective-permute-done((bf16[1,256,128]{2,1,0:T(8,128)(2,1)S(1)}, bf16[1,256,128]{2,1,0:T(8,128)(2,1)S(1)}, u32[]{:S(2)}, u32[]{:S(2)}) %collective-permute-start.12) | collective-permute-done | bytes 65568 | tf_op jit(solution)/shard_map/ppermute | solution.py:221
  39.1 1.2 %shard_map.103 = (bf16[4,128,128]{2,1,0:T(8,128)(2,1)}, bf16[4,128,128]{2,1,0:T(8,128)(2,1)}) custom-call(bf16[4,128,128]{2,1,0:T(8,128)(2,1)S(1)} %get-tuple-element.35.consts_ref, f32[4,128,128]{2,1,0:T(8,128)S(1)} %get-tuple-element.36.base_ref, f32[1,256,128]{2,1,0:T(8,128)S(1)} %get-tuple-element.42.refs_0_, ...), custom_call_target="tpu_custom_call" | custom-call | bytes 1310720 | tf_op jit(solution)/shard_map/pallas_call | solution.py:52
  (9 shorter events, 0.1 us)
Async XLA Ops:
  0.6 7.7 %collective-permute-start = (bf16[4,8,64,128]{3,2,1,0:T(8,128)(2,1)}, bf16[4,8,64,128]{3,2,1,0:T(8,128)(2,1)S(1)}, u32[]{:S(2)}, u32[]{:S(2)}) collective-permute-start(bf16[4,8,64,128]{3,2,1,0:T(8,128)(2,1)} %block_ref.1), channel_id=1, source_target_pairs={{0,2},{1,3},{2,0},{3,1},{4,6},{5,7},{6,4},{7,5},{8,10},{9,11},{10,... | collective-permute-start | bytes 1572872 | tf_op jit(solution)/shard_map/ppermute | solution.py:221
  1.2 1.0 %copy-start.6 = (bf16[1024,2,128]{2,1,0:T(2,128)(2,1)S(1)}, bf16[1024,2,128]{2,1,0:T(2,128)(2,1)}, u32[]{:S(2)}) copy-start(bf16[1024,2,128]{2,1,0:T(2,128)(2,1)} %param.9) | copy-start | bytes 1572868
  2.2 6.1 %copy-start = (bf16[4,8,64,128]{3,2,1,0:T(8,128)(2,1)S(1)}, bf16[4,8,64,128]{3,2,1,0:T(8,128)(2,1)}, u32[]{:S(2)}) copy-start(bf16[4,8,64,128]{3,2,1,0:T(8,128)(2,1)} %block_ref.1) | copy-start | bytes 1572868
  2.2 6.1 %copy-start.1 = (bf16[256,2,128]{2,1,0:T(2,128)(2,1)S(1)}, bf16[256,2,128]{2,1,0:T(2,128)(2,1)}, u32[]{:S(2)}) copy-start(bf16[256,2,128]{2,1,0:T(2,128)(2,1)} %param.10) | copy-start | bytes 393220
  2.2 6.1 %copy-start.2 = (f32[64,64]{1,0:T(8,128)S(1)}, f32[64,64]{1,0:T(8,128)}, u32[]{:S(2)}) copy-start(f32[64,64]{1,0:T(8,128)} %coupling_ref.1) | copy-start | bytes 49156
  2.2 6.1 %copy-start.3 = (bf16[64,64]{1,0:T(8,128)(2,1)S(1)}, bf16[64,64]{1,0:T(8,128)(2,1)}, u32[]{:S(2)}) copy-start(bf16[64,64]{1,0:T(8,128)(2,1)} %ham_ref.1) | copy-start | bytes 24580
  2.2 6.1 %copy-start.4 = (s32[64]{0:T(128)S(1)}, s32[64]{0:T(128)}, u32[]{:S(2)}) copy-start(s32[64]{0:T(128)} %deal_ref.1) | copy-start | bytes 772
  2.3 6.1 %copy-start.5 = (s32[16]{0:T(128)S(1)}, s32[16]{0:T(128)}, u32[]{:S(2)}) copy-start(s32[16]{0:T(128)} %columns_ref.1) | copy-start | bytes 196
  2.7 3.2 %collective-permute-start.1 = (bf16[2,1,2,128,128]{4,3,2,1,0:T(8,128)(2,1)S(1)}, bf16[2,1,2,128,128]{4,3,2,1,0:T(8,128)(2,1)S(1)}, u32[]{:S(2)}, u32[]{:S(2)}) collective-permute-start(bf16[2,1,2,128,128]{4,3,2,1,0:T(8,128)(2,1)S(1)} %get-tuple-element.33), channel_id=1, source_target_pairs={{0,2},{1,3},{2,0},{3,1},{4,6},{5,7},{6,4},{7,5},{8,10},{9,11},{10,... | collective-permute-start | bytes 393224 | tf_op jit(solution)/shard_map/ppermute | solution.py:221
  2.7 4.9 %collective-permute-start.2 = (bf16[2,1,2,128,128]{4,3,2,1,0:T(8,128)(2,1)S(1)}, bf16[2,1,2,128,128]{4,3,2,1,0:T(8,128)(2,1)S(1)}, u32[]{:S(2)}, u32[]{:S(2)}) collective-permute-start(bf16[2,1,2,128,128]{4,3,2,1,0:T(8,128)(2,1)S(1)} %get-tuple-element.34), channel_id=1, source_target_pairs={{0,2},{1,3},{2,0},{3,1},{4,6},{5,7},{6,4},{7,5},{8,10},{9,11},{10,... | collective-permute-start | bytes 393224 | tf_op jit(solution)/shard_map/ppermute | solution.py:221
  3.2 8.1 %collective-permute-start.6 = (bf16[2,1,2,128,128]{4,3,2,1,0:T(8,128)(2,1)S(1)}, bf16[2,1,2,128,128]{4,3,2,1,0:T(8,128)(2,1)S(1)}, u32[]{:S(2)}, u32[]{:S(2)}) collective-permute-start(bf16[2,1,2,128,128]{4,3,2,1,0:T(8,128)(2,1)S(1)} %get-tuple-element.32.refs_1_), channel_id=1, source_target_pairs={{0,1},{1,0},{2,3},{3,2},{4,5},{5,4},{6,7},{7,6},{8,9},{9,8},{10,11... | collective-permute-start | bytes 393224 | tf_op jit(solution)/shard_map/ppermute | solution.py:221
  5.8 6.7 %collective-permute-start.7 = (bf16[2,1,2,128,128]{4,3,2,1,0:T(8,128)(2,1)S(1)}, bf16[2,1,2,128,128]{4,3,2,1,0:T(8,128)(2,1)S(1)}, u32[]{:S(2)}, u32[]{:S(2)}) collective-permute-start(bf16[2,1,2,128,128]{4,3,2,1,0:T(8,128)(2,1)S(1)} %get-tuple-element.34), channel_id=1, source_target_pairs={{0,3},{1,2},{2,1},{3,0},{4,7},{5,6},{6,5},{7,4},{8,11},{9,10},{10,... | collective-permute-start | bytes 393224 | tf_op jit(solution)/shard_map/ppermute | solution.py:221
  5.9 9.9 %collective-permute-start.3 = (bf16[2,1,2,128,128]{4,3,2,1,0:T(8,128)(2,1)S(1)}, bf16[2,1,2,128,128]{4,3,2,1,0:T(8,128)(2,1)S(1)}, u32[]{:S(2)}, u32[]{:S(2)}) collective-permute-start(bf16[2,1,2,128,128]{4,3,2,1,0:T(8,128)(2,1)S(1)} %get-tuple-element.31.refs_0_), channel_id=1, source_target_pairs={{0,1},{1,0},{2,3},{3,2},{4,5},{5,4},{6,7},{7,6},{8,9},{9,8},{10,11... | collective-permute-start | bytes 393224 | tf_op jit(solution)/shard_map/ppermute | solution.py:221
  7.6 10.5 %collective-permute-start.4 = (bf16[2,1,2,128,128]{4,3,2,1,0:T(8,128)(2,1)S(1)}, bf16[2,1,2,128,128]{4,3,2,1,0:T(8,128)(2,1)S(1)}, u32[]{:S(2)}, u32[]{:S(2)}) collective-permute-start(bf16[2,1,2,128,128]{4,3,2,1,0:T(8,128)(2,1)S(1)} %get-tuple-element.33), channel_id=1, source_target_pairs={{0,3},{1,2},{2,1},{3,0},{4,7},{5,6},{6,5},{7,4},{8,11},{9,10},{10,... | collective-permute-start | bytes 393224 | tf_op jit(solution)/shard_map/ppermute | solution.py:221
  13.9 9.1 %collective-permute-start.13 = (bf16[2,256,128]{2,1,0:T(8,128)(2,1)S(1)}, bf16[2,256,128]{2,1,0:T(8,128)(2,1)S(1)}, u32[]{:S(2)}, u32[]{:S(2)}) collective-permute-start(bf16[2,256,128]{2,1,0:T(8,128)(2,1)S(1)} %get-tuple-element.54), channel_id=1, source_target_pairs={{0,4},{1,5},{2,6},{3,7},{4,0},{5,1},{6,2},{7,3},{8,12},{9,13},{10,... | collective-permute-start | bytes 393224 | tf_op jit(solution)/shard_map/ppermute | solution.py:221
  19.5 7.6 %collective-permute-start.9 = (bf16[2,256,128]{2,1,0:T(8,128)(2,1)S(1)}, bf16[2,256,128]{2,1,0:T(8,128)(2,1)S(1)}, u32[]{:S(2)}, u32[]{:S(2)}) collective-permute-start(bf16[2,256,128]{2,1,0:T(8,128)(2,1)S(1)} %get-tuple-element.49), channel_id=1, source_target_pairs={{0,4},{1,5},{2,6},{3,7},{4,0},{5,1},{6,2},{7,3},{8,12},{9,13},{10,... | collective-permute-start | bytes 393224 | tf_op jit(solution)/shard_map/ppermute | solution.py:221
  21.0 7.9 %collective-permute-start.8 = (bf16[2,256,128]{2,1,0:T(8,128)(2,1)S(1)}, bf16[2,256,128]{2,1,0:T(8,128)(2,1)S(1)}, u32[]{:S(2)}, u32[]{:S(2)}) collective-permute-start(bf16[2,256,128]{2,1,0:T(8,128)(2,1)S(1)} %get-tuple-element.46), channel_id=1, source_target_pairs={{0,4},{1,5},{2,6},{3,7},{4,0},{5,1},{6,2},{7,3},{8,12},{9,13},{10,... | collective-permute-start | bytes 393224 | tf_op jit(solution)/shard_map/ppermute | solution.py:221
  21.6 10.7 %collective-permute-start.5 = (bf16[2,256,128]{2,1,0:T(8,128)(2,1)S(1)}, bf16[2,256,128]{2,1,0:T(8,128)(2,1)S(1)}, u32[]{:S(2)}, u32[]{:S(2)}) collective-permute-start(bf16[2,256,128]{2,1,0:T(8,128)(2,1)S(1)} %get-tuple-element.41), channel_id=1, source_target_pairs={{0,4},{1,5},{2,6},{3,7},{4,0},{5,1},{6,2},{7,3},{8,12},{9,13},{10,... | collective-permute-start | bytes 393224 | tf_op jit(solution)/shard_map/ppermute | solution.py:221
  23.1 9.7 %collective-permute-start.14 = (bf16[1,256,128]{2,1,0:T(8,128)(2,1)S(1)}, bf16[1,256,128]{2,1,0:T(8,128)(2,1)S(1)}, u32[]{:S(2)}, u32[]{:S(2)}) collective-permute-start(bf16[1,256,128]{2,1,0:T(8,128)(2,1)S(1)} %get-tuple-element.55), channel_id=1, source_target_pairs={{0,16},{1,17},{2,18},{3,19},{4,20},{5,21},{6,22},{7,23},{8,24},{9,... | collective-permute-start | bytes 196616 | tf_op jit(solution)/shard_map/ppermute | solution.py:221
  25.7 8.8 %collective-permute-start.15 = (bf16[1,256,128]{2,1,0:T(8,128)(2,1)S(1)}, bf16[1,256,128]{2,1,0:T(8,128)(2,1)S(1)}, u32[]{:S(2)}, u32[]{:S(2)}) collective-permute-start(bf16[1,256,128]{2,1,0:T(8,128)(2,1)S(1)} %get-tuple-element.56), channel_id=1, source_target_pairs={{0,24},{1,25},{2,26},{3,27},{4,28},{5,29},{6,30},{7,31},{8,16},{9,... | collective-permute-start | bytes 196616 | tf_op jit(solution)/shard_map/ppermute | solution.py:221
  27.1 9.7 %collective-permute-start.10 = (bf16[1,256,128]{2,1,0:T(8,128)(2,1)S(1)}, bf16[1,256,128]{2,1,0:T(8,128)(2,1)S(1)}, u32[]{:S(2)}, u32[]{:S(2)}) collective-permute-start(bf16[1,256,128]{2,1,0:T(8,128)(2,1)S(1)} %get-tuple-element.50), channel_id=1, source_target_pairs={{0,16},{1,17},{2,18},{3,19},{4,20},{5,21},{6,22},{7,23},{8,24},{9,... | collective-permute-start | bytes 196616 | tf_op jit(solution)/shard_map/ppermute | solution.py:221
  28.9 8.0 %collective-permute-start.11 = (bf16[1,256,128]{2,1,0:T(8,128)(2,1)S(1)}, bf16[1,256,128]{2,1,0:T(8,128)(2,1)S(1)}, u32[]{:S(2)}, u32[]{:S(2)}) collective-permute-start(bf16[1,256,128]{2,1,0:T(8,128)(2,1)S(1)} %get-tuple-element.51), channel_id=1, source_target_pairs={{0,24},{1,25},{2,26},{3,27},{4,28},{5,29},{6,30},{7,31},{8,16},{9,... | collective-permute-start | bytes 196616 | tf_op jit(solution)/shard_map/ppermute | solution.py:221
  32.3 5.6 %collective-permute-start.16 = (bf16[1,256,128]{2,1,0:T(8,128)(2,1)S(1)}, bf16[1,256,128]{2,1,0:T(8,128)(2,1)S(1)}, u32[]{:S(2)}, u32[]{:S(2)}) collective-permute-start(bf16[1,256,128]{2,1,0:T(8,128)(2,1)S(1)} %get-tuple-element.57), channel_id=1, source_target_pairs={{0,8},{1,9},{2,10},{3,11},{4,12},{5,13},{6,14},{7,15},{8,0},{9,1},... | collective-permute-start | bytes 196616 | tf_op jit(solution)/shard_map/ppermute | solution.py:221
  32.8 6.3 %collective-permute-start.12 = (bf16[1,256,128]{2,1,0:T(8,128)(2,1)S(1)}, bf16[1,256,128]{2,1,0:T(8,128)(2,1)S(1)}, u32[]{:S(2)}, u32[]{:S(2)}) collective-permute-start(bf16[1,256,128]{2,1,0:T(8,128)(2,1)S(1)} %get-tuple-element.52), channel_id=1, source_target_pairs={{0,8},{1,9},{2,10},{3,11},{4,12},{5,13},{6,14},{7,15},{8,0},{9,1},... | collective-permute-start | bytes 196616 | tf_op jit(solution)/shard_map/ppermute | solution.py:221

commit v4 on v3

--- a/solution.py
+++ b/solution.py
@@ -62,59 +62,58 @@
     return jax.ShapeDtypeStruct(tuple(dims), kind)
 
 
-def split_body(rows_ref, *refs):
+def split_body(rows_ref, *outs):
     core = lax.axis_index("mem") & 1
-    outs, sems = refs[:-1], refs[-1]
-    copies = []
     for at, out in enumerate(outs):
         size = out.shape[2]
         first = (at // 2) * size
-        half = core if at % 2 == 0 else 1 - core
-        copies.append(pltpu.make_async_copy(rows_ref.at[:, :, half, first:first + size], out, sems.at[at]))
-    for copy in copies:
-        copy.start()
-    for copy in copies:
-        copy.wait()
-
-
-def early_body(n_early, slot_of, groups, chunks, deal_ref, columns_ref, start_ref, coupling_ref, ham_ref, panel_ref, block_ref, other_ref, *refs):
-    early = refs[:n_early * chunks]
-    weights_ref, consts_ref, base_ref = refs[n_early * chunks:n_early * chunks + 3]
-    sigmas = refs[n_early * chunks + 3:]
+        out[...] = rows_ref[:, :, core if at % 2 == 0 else 1 - core, first:first + size]
+
+
+def ready_body(count, coupling_ref, *refs):
+    sources, consts_ref, sigmas = refs[:count], refs[count], refs[count + 1:]
     orbitals = coupling_ref.shape[0]
-    rows = consts_ref.shape[1]
-    panels = rows // orbitals
-    mem, hist = lax.axis_index("mem"), lax.axis_index("hist")
-    pair = mem >> 1
-    slots, columns = block_ref.shape[0], block_ref.shape[1]
-
-    spread = (lax.broadcasted_iota(jnp.int32, (rows, orbitals), 0) // panels == lax.broadcasted_iota(jnp.int32, (rows, orbitals), 1)).astype(F32)
-    row_at = lax.broadcasted_iota(jnp.int32, (rows, rows), 0)
-    lane_at = lax.broadcasted_iota(jnp.int32, (rows, rows), 1)
-    same = (row_at % panels == lane_at % panels).astype(F32)
-
-    def exact(left, right, dims):
-        return lax.dot_general(left, right, (dims, ((), ())), precision=lax.Precision.HIGHEST, preferred_element_type=F32)
-
-    def rowed(matrix):
-        return exact(exact(spread, matrix, ((1,), (0,))), spread, ((1,), (1,))) * same
-
     lanes = 2 * orbitals
     fold = (lax.broadcasted_iota(jnp.int32, (lanes, orbitals), 0) % orbitals == lax.broadcasted_iota(jnp.int32, (lanes, orbitals), 1)).astype(F32)
     coupling = coupling_ref[...]
     right = exact(exact(fold, coupling, ((1,), (1,))), fold, ((1,), (1,)))
-    right_top, right_low = halves(right)
-    left_top, left_low = halves(rowed(coupling))
-    for at, value in enumerate((right_top, right_low, left_top, left_low)):
+    consts = (*halves(right), *halves(row_matrix(coupling, consts_ref.shape[1])))
+    for at, value in enumerate(consts):
         consts_ref[at] = value
-    consts = (right_top, right_low, left_top, left_low)
-
-    for at in range(n_early * chunks):
-        source = early[at]
+    for source, sigma in zip(sources, sigmas):
         tiles = sigma_tiles(source[...].reshape((-1,) + source.shape[3:]), consts)
-        sigmas[at][...] = tiles.astype(BF16).reshape(source.shape)
-
-    ham = rowed(ham_ref[...].astype(F32)).astype(BF16)
+        sigma[...] = tiles.astype(BF16).reshape(source.shape)
+
+
+def exact(left, right, dims):
+    return lax.dot_general(left, right, (dims, ((), ())), precision=lax.Precision.HIGHEST, preferred_element_type=F32)
+
+
+def row_matrix(matrix, rows):
+    orbitals = matrix.shape[0]
+    panels = rows // orbitals
+    spread = (lax.broadcasted_iota(jnp.int32, (rows, orbitals), 0) // panels == lax.broadcasted_iota(jnp.int32, (rows, orbitals), 1)).astype(F32)
+    same = (lax.broadcasted_iota(jnp.int32, (rows, rows), 0) % panels == lax.broadcasted_iota(jnp.int32, (rows, rows), 1) % panels).astype(F32)
+    return exact(exact(spread, matrix, ((1,), (0,))), spread, ((1,), (1,))) * same
+
+
+def early_body(n_early, slot_of, groups, deal_ref, columns_ref, consts_ref, ham_ref, panel_ref, block_ref, other_ref, *refs):
+    early = refs[:n_early]
+    weights_ref, base_ref = refs[n_early:n_early + 2]
+    sigmas = refs[n_early + 2:]
+    orbitals = ham_ref.shape[0]
+    lanes = 2 * orbitals
+    rows = panel_ref.shape[1]
+    mem, hist = lax.axis_index("mem"), lax.axis_index("hist")
+    pair = mem >> 1
+    slots, columns = block_ref.shape[0], block_ref.shape[1]
+
+    consts = tuple(consts_ref[at] for at in range(4))
+    for source, sigma in zip(early, sigmas):
+        tiles = sigma_tiles(source[...].reshape((-1,) + source.shape[3:]), consts)
+        sigma[...] = tiles.astype(BF16).reshape(source.shape)
+
+    ham = row_matrix(ham_ref[...].astype(F32), rows).astype(BF16)
     sign = jnp.where(lax.broadcasted_iota(jnp.int32, (rows, lanes), 1) < orbitals, 1.0, -1.0).astype(F32)
     for tile in range(panel_ref.shape[0]):
         values = panel_ref[tile]
@@ -123,7 +122,6 @@
 
     flip = jnp.where(lax.broadcasted_iota(jnp.int32, (orbitals, lanes), 1) < orbitals, -1.0, 1.0).astype(F32)
     own_column = pair // groups
-    begin = start_ref[0]
     for q in range(2 * slots):
         foreign, local = slot_of(q, hist)
         source = other_ref if foreign else block_ref
@@ -131,7 +129,7 @@
         time = deal_ref[mem_of * slots + local]
         for apart in range(columns):
             column = own_column ^ apart
-            keep = jnp.logical_and(time >= columns_ref[hist * columns + column], time >= begin)
+            keep = time >= columns_ref[hist * columns + column]
             upper = source[local, column].astype(F32) * jnp.where(keep, 1.0, 0.0).astype(F32)
             lower = pltpu.roll(upper, orbitals, 1) * flip
             weights_ref[q * lanes:q * lanes + orbitals, apart * lanes:(apart + 1) * lanes] = upper.astype(BF16)
@@ -174,16 +172,18 @@
         out[...] = total[at * size:(at + 1) * size].astype(out.dtype)
 
 
-def last_body(chunks, n_got, consts_ref, base_ref, *refs):
-    keeps, gots = refs[:chunks], refs[chunks:chunks + chunks * n_got]
-    rows_ref, sigma_ref = refs[chunks + chunks * n_got:]
+def last_body(counts, consts_ref, base_ref, *refs):
+    chunks = len(counts)
+    keeps, gots = refs[:chunks], refs[chunks:-2]
+    rows_ref, sigma_ref = refs[-2:]
     consts = tuple(consts_ref[at] for at in range(4))
     size = base_ref.shape[0] // chunks
     for c in range(chunks):
         here = slice(c * size, (c + 1) * size)
         collision = keeps[c][...]
-        for got in gots[c * n_got:(c + 1) * n_got]:
+        for got in gots[:counts[c]]:
             collision = collision + got[...].astype(F32)
+        gots = gots[counts[c]:]
         collision = collision.reshape((size,) + base_ref.shape[1:])
         rows = (base_ref[here] + time_step * collision).astype(BF16)
         rows_ref[here] = rows
@@ -240,24 +240,25 @@
     tiles = memory_rows.reshape(held, groups, 2, own_tiles, rows, lanes)
     panel_tiles = panel_rows.reshape(own_tiles, rows, lanes)
     piece = shape((held, groups, part, rows, lanes), BF16)
-    hbm = pl.BlockSpec(memory_space=pltpu.HBM)
     smem = pl.BlockSpec(memory_space=pltpu.SMEM)
     vmem = pl.BlockSpec(memory_space=pltpu.VMEM)
-    split = call(
-        split_body,
-        [piece] * (2 * chunks),
-        tiles,
-        in_specs=[hbm],
-        flops=PREFETCH_FLOPS,
-        scratch_shapes=[pltpu.SemaphoreType.DMA((2 * chunks,))],
+    split = call(split_body, [piece] * (2 * chunks), tiles, in_specs=[vmem], flops=PREFETCH_FLOPS)
+    mine, other = list(split[0::2]), list(split[1::2])
+
+    kept_times = jnp.where(time_deal >= window_start, time_deal, jnp.iinfo(jnp.int32).min)
+    ready_in = [array for c in range(1, chunks) for array in (mine[c], other[c])]
+    consts, *ready = call(
+        functools.partial(ready_body, len(ready_in)),
+        [shape((4, rows, lanes), BF16)] + [piece] * len(ready_in),
+        coupling, *ready_in,
+        in_specs=[vmem] * (1 + len(ready_in)),
     )
-    mine, other = split[0::2], split[1::2]
-
+    mine[1:], other[1:] = ready[0::2], ready[1::2]
+    partner_block = exchange(memory_block, 1, 0)
+    partner = [exchange(other[c], 1, 0) for c in range(chunks)]
     if two_hist:
         same_core = [exchange(mine[c], 0, 1) for c in range(chunks)]
         cross = [exchange(other[c], 1, 1) for c in range(chunks)]
-    partner_block = exchange(memory_block, 1, 0)
-    partner = [exchange(other[c], 1, 0) for c in range(chunks)]
 
     if two_hist:
         def slot_of(q, hist):
@@ -266,28 +267,28 @@
         def slot_of(q, hist):
             return q // held, q % held
 
-    early = [mine, partner]
-    n_early = len(early)
-    flat_early = [array for source in early for array in source]
-    outs = [
-        shape((2 * slots * lanes, columns * lanes), BF16),
-        shape((4, rows, lanes), BF16),
-        shape((own_tiles, rows, lanes), F32),
-    ] + [piece] * (n_early * chunks)
-    weights, consts, base, *sigmas = call(
-        functools.partial(early_body, n_early, slot_of, groups, chunks),
+    outs = [shape((2 * slots * lanes, columns * lanes), BF16), shape((own_tiles, rows, lanes), F32), piece, piece]
+    weights, base, *sigmas = call(
+        functools.partial(early_body, 2, slot_of, groups),
         outs,
-        time_deal, column_times, window_start, coupling, hamiltonian, panel_tiles, memory_block, partner_block, *flat_early,
-        in_specs=[smem] * 3 + [vmem] * (5 + n_early * chunks),
+        kept_times, column_times, consts, hamiltonian, panel_tiles, memory_block, partner_block, mine[0], partner[0],
+        in_specs=[smem] * 2 + [vmem] * 7,
     )
 
-    steps = step_masks(pairs)
-    parts = 2 if len(steps) > 1 else 1
     keeps, received = [], []
     for c in range(chunks):
+        steps = step_masks(pairs)
+        if c < chunks - 1:
+            steps = steps[1:] + steps[:1]
+        parts = 2 if c == chunks - 1 and len(steps) > 1 else 1
         height = part * rows
-        done = [sigmas[e * chunks + c] for e in range(n_early)]
-        late = [same_core[c], cross[c]] if two_hist else []
+        done = list(sigmas) if c == 0 else [mine[c], partner[c]]
+        late = []
+        if two_hist:
+            if c == 0:
+                late = [same_core[c], cross[c]]
+            else:
+                done += [same_core[c], cross[c]]
         count = pairs // len(steps[0]) // parts
 
         def pieces(masks, count):
@@ -314,13 +315,13 @@
                 outs += call(functools.partial(add_body, len(gots[p])), pieces(after[p * share:(p + 1) * share], count), keep, *gots[p])
             state = [(outs[:-1], outs[-1])]
         keeps.append(state[0][1])
-        received += gots[0]
+        received.append(gots[0])
 
     result = shape((own_tiles, rows, lanes), BF16)
     new_rows, new_sigma = call(
-        functools.partial(last_body, chunks, len(received) // chunks),
+        functools.partial(last_body, [len(gots) for gots in received]),
         [result, result],
-        consts, base, *keeps, *received,
+        consts, base, *keeps, *[got for gots in received for got in gots],
     )
     return new_rows.reshape(panel_rows.shape), new_sigma.reshape(panel_rows.shape)
 

time: 40.5 us -> 43.7 us (1.079)
  waiting for transfers between devices: 8.31 us -> 15.4 us
  starting transfers between devices: 22 us -> 18.8 us
  Pallas kernels: 7.57 us -> 6.94 us
    ppermute x17 -> x16, waiting for transfers between devices: 8.31 us -> 15.4 us  [exchange(): return lax.ppermute(value, ('mem', 'hist'), pairs)]
    ppermute x17 -> x16, starting transfers between devices: 22 us -> 18.8 us  [exchange(): return lax.ppermute(value, ('mem', 'hist'), pairs)]
    pallas_call x9, Pallas kernels: 7.57 us -> 6.94 us  [call(): pl.pallas_call(body, out_shape=outs, cost_estimate=pl.CostEstimate(flops=...]
  transfers between devices with their start and end apart: 17 -> 16, of which waited for: 6 -> 5; matrix products, arithmetic and copies ran while one was open for 0% -> 0% of each run, Pallas kernels for 16% -> 13%
where the time goes in v4:
time: 43.7 us; the launch traced here: 43.6 us
  starting transfers between devices  18.8 us (43%)
  waiting for transfers between devices  15.4 us (35%)
  Pallas kernels  6.94 us (16%)
  between operations  1.41 us (3%)
  local copies, waits for them, and re-layouts  1.06 us (2%)
    ppermute x16, starting transfers between devices, exchange(): return lax.ppermute(value, ('mem', 'hist'), pairs)  18.8 us
    ppermute x16, waiting for transfers between devices, exchange(): return lax.ppermute(value, ('mem', 'hist'), pairs)  15.4 us
    pallas_call x9, Pallas kernels, call(): pl.pallas_call(body, out_shape=outs, cost_estimate=pl.CostEstimate(flops=...  6.94 us
    unnamed x14, local copies, waits for them, and re-layouts  1.06 us
  transfers between devices with their start and end apart: 16, of which 5 were waited for; matrix products, arithmetic and copies ran while one was open for 0% of the time, Pallas kernels for 13%

profile of v4, /device:TPU:0, one launch (start us, length us, event | category | flops | bytes accessed | tf_op | source)
XLA Modules:
  0.0 43.6 jit_solution(18254529618672740883)
XLA Ops:
  0.6 0.6 %collective-permute-start = (bf16[4,8,64,128]{3,2,1,0:T(8,128)(2,1)}, bf16[4,8,64,128]{3,2,1,0:T(8,128)(2,1)S(1)}, u32[]{:S(2)}, u32[]{:S(2)}) collective-permute-start(bf16[4,8,64,128]{3,2,1,0:T(8,128)(2,1)} %block_ref.1), channel_id=1, source_target_pairs={{0,2},{1,3},{2,0},{3,1},{4,6},{5,7},{6,4},{7,5},{8,10},{9,11},{10,... | collective-permute-start | bytes 1572872 | tf_op jit(solution)/shard_map/ppermute | solution.py:221
  1.2 0.0 copy-start.5
  1.2 1.0 %copy-done.5 = bf16[1024,2,128]{2,1,0:T(2,128)(2,1)S(1)} copy-done((bf16[1024,2,128]{2,1,0:T(2,128)(2,1)S(1)}, bf16[1024,2,128]{2,1,0:T(2,128)(2,1)}, u32[]{:S(2)}) %copy-start.5) | copy-done | bytes 524312
  2.2 0.0 copy-start.3
  2.3 0.0 copy-start.4
  2.3 0.1 collective-permute-start.1
  2.4 2.7 %collective-permute-start.3 = (bf16[2,1,2,128,128]{4,3,2,1,0:T(8,128)(2,1)S(1)}, bf16[2,1,2,128,128]{4,3,2,1,0:T(8,128)(2,1)S(1)}, u32[]{:S(2)}, u32[]{:S(2)}) collective-permute-start(bf16[2,1,2,128,128]{4,3,2,1,0:T(8,128)(2,1)S(1)} %get-tuple-element.33), channel_id=1, source_target_pairs={{0,3},{1,2},{2,1},{3,0},{4,7},{5,6},{6,5},{7,4},{8,11},{9,10},{10,... | collective-permute-start | bytes 393224 | tf_op jit(solution)/shard_map/ppermute | solution.py:221
  5.1 0.0 copy-done.2
  5.1 1.6 %shard_map.96 = (bf16[4,128,128]{2,1,0:T(8,128)(2,1)S(1)}, bf16[2,1,2,128,128]{4,3,2,1,0:T(8,128)(2,1)S(1)}, bf16[2,1,2,128,128]{4,3,2,1,0:T(8,128)(2,1)S(1)}) custom-call(f32[64,64]{1,0:T(8,128)S(1)} %copy-done.2, bf16[2,1,2,128,128]{4,3,2,1,0:T(8,128)(2,1)S(1)} %get-tuple-element.29.refs_0_, bf16[2,1,2,128,128]{4,3,2,1,0:T(8,128)(2,1)S(1)} %get-tuple-element.30.refs_1_), custom_call_target="tpu_custom_call" | custom-call | bytes 671744 | tf_op jit(solution)/shard_map/pallas_call | solution.py:52
  6.7 0.5 %collective-permute-start.7 = (bf16[2,1,2,128,128]{4,3,2,1,0:T(8,128)(2,1)S(1)}, bf16[2,1,2,128,128]{4,3,2,1,0:T(8,128)(2,1)S(1)}, u32[]{:S(2)}, u32[]{:S(2)}) collective-permute-start(bf16[2,1,2,128,128]{4,3,2,1,0:T(8,128)(2,1)S(1)} %get-tuple-element.44), channel_id=1, source_target_pairs={{0,2},{1,3},{2,0},{3,1},{4,6},{5,7},{6,4},{7,5},{8,10},{9,11},{10,... | collective-permute-start | bytes 393224 | tf_op jit(solution)/shard_map/ppermute | solution.py:221
  7.2 0.2 collective-permute-start.9
  8.0 0.0 collective-permute-done.1.refs_1_
  8.0 1.6 %collective-permute-start.2 = (bf16[2,1,2,128,128]{4,3,2,1,0:T(8,128)(2,1)S(1)}, bf16[2,1,2,128,128]{4,3,2,1,0:T(8,128)(2,1)S(1)}, u32[]{:S(2)}, u32[]{:S(2)}) collective-permute-start(bf16[2,1,2,128,128]{4,3,2,1,0:T(8,128)(2,1)S(1)} %get-tuple-element.32.refs_0_), channel_id=1, source_target_pairs={{0,1},{1,0},{2,3},{3,2},{4,5},{5,4},{6,7},{7,6},{8,9},{9,8},{10,11... | collective-permute-start | bytes 393224 | tf_op jit(solution)/shard_map/ppermute | solution.py:221
  9.6 0.0 collective-permute-done.other_ref
  9.6 0.5 %collective-permute-start.8 = (bf16[2,1,2,128,128]{4,3,2,1,0:T(8,128)(2,1)S(1)}, bf16[2,1,2,128,128]{4,3,2,1,0:T(8,128)(2,1)S(1)}, u32[]{:S(2)}, u32[]{:S(2)}) collective-permute-start(bf16[2,1,2,128,128]{4,3,2,1,0:T(8,128)(2,1)S(1)} %get-tuple-element.43.refs_0_), channel_id=1, source_target_pairs={{0,1},{1,0},{2,3},{3,2},{4,5},{5,4},{6,7},{7,6},{8,9},{9,8},{10,11... | collective-permute-start | bytes 393224 | tf_op jit(solution)/shard_map/ppermute | solution.py:221
  10.1 0.0 copy-done.6
  10.1 0.0 copy-done
  10.1 0.0 copy-done.1
  10.1 0.0 copy-done.3
  10.1 0.0 copy-done.4
  10.1 1.8 %shard_map.97 = (bf16[1024,1024]{1,0:T(8,128)(2,1)S(1)}, f32[4,128,128]{2,1,0:T(8,128)S(1)}, bf16[2,1,2,128,128]{4,3,2,1,0:T(8,128)(2,1)S(1)}, bf16[2,1,2,128,128]{4,3,2,1,0:T(8,128)(2,1)S(1)}) custom-call(s32[64]{0:T(128)S(1)} %compare_select_fusion.deal_ref, s32[16]{0:T(128)S(1)} %copy-done.4, bf16[4,128,128]{2,1,0:T(8,128)(2,1)S(1)} %get-tuple-element.31.consts_ref, ...), custom_call_target="tpu_custom_call" | custom-call | bytes 4202816 | tf_op jit(solution)/shard_map/pallas_call | solution.py:52
  12.0 4.0 %collective-permute-done.2.refs_2_ = bf16[2,1,2,128,128]{4,3,2,1,0:T(8,128)(2,1)S(1)} collective-permute-done((bf16[2,1,2,128,128]{4,3,2,1,0:T(8,128)(2,1)S(1)}, bf16[2,1,2,128,128]{4,3,2,1,0:T(8,128)(2,1)S(1)}, u32[]{:S(2)}, u32[]{:S(2)}) %collective-permute-start.2) | collective-permute-done | bytes 131104 | tf_op jit(solution)/shard_map/ppermute | solution.py:221
  16.0 0.0 collective-permute-done.3.refs_3_
  16.0 1.4 %shard_map.98 = (bf16[2,256,128]{2,1,0:T(8,128)(2,1)S(1)}, bf16[2,256,128]{2,1,0:T(8,128)(2,1)S(1)}, bf16[2,256,128]{2,1,0:T(8,128)(2,1)S(1)}, f32[2,256,128]{2,1,0:T(8,128)S(1)}) custom-call(bf16[4,128,128]{2,1,0:T(8,128)(2,1)S(1)} %get-tuple-element.31.consts_ref, bf16[1024,1024]{1,0:T(8,128)(2,1)S(1)} %get-tuple-element.35.weights_ref, ...), custom_call_target="tpu_custom_call" | custom-call | flops 536870912 | bytes 3407872 | tf_op jit(solution)/shard_map/pallas_call | solution.py:52
  17.5 2.7 %collective-permute-start.4 = (bf16[2,256,128]{2,1,0:T(8,128)(2,1)S(1)}, bf16[2,256,128]{2,1,0:T(8,128)(2,1)S(1)}, u32[]{:S(2)}, u32[]{:S(2)}) collective-permute-start(bf16[2,256,128]{2,1,0:T(8,128)(2,1)S(1)} %get-tuple-element.39), channel_id=1, source_target_pairs={{0,16},{1,17},{2,18},{3,19},{4,20},{5,21},{6,22},{7,23},{8,24},{9,... | collective-permute-start | bytes 393224 | tf_op jit(solution)/shard_map/ppermute | solution.py:221
  20.1 1.3 %collective-permute-start.5 = (bf16[2,256,128]{2,1,0:T(8,128)(2,1)S(1)}, bf16[2,256,128]{2,1,0:T(8,128)(2,1)S(1)}, u32[]{:S(2)}, u32[]{:S(2)}) collective-permute-start(bf16[2,256,128]{2,1,0:T(8,128)(2,1)S(1)} %get-tuple-element.40), channel_id=1, source_target_pairs={{0,24},{1,25},{2,26},{3,27},{4,28},{5,29},{6,30},{7,31},{8,16},{9,... | collective-permute-start | bytes 393224 | tf_op jit(solution)/shard_map/ppermute | solution.py:221
  21.5 0.0 collective-permute-done.7.refs_1_
  21.5 0.2 collective-permute-start.6
  21.7 0.0 collective-permute-done.8.refs_2_
  21.7 0.0 collective-permute-done.9.refs_3_
  21.7 0.7 %shard_map.100 = (bf16[2,256,128]{2,1,0:T(8,128)(2,1)S(1)}, f32[2,256,128]{2,1,0:T(8,128)S(1)}, bf16[2,256,128]{2,1,0:T(8,128)(2,1)S(1)}, f32[2,256,128]{2,1,0:T(8,128)S(1)}) custom-call(bf16[4,128,128]{2,1,0:T(8,128)(2,1)S(1)} %get-tuple-element.31.consts_ref, bf16[1024,1024]{1,0:T(8,128)(2,1)S(1)} %get-tuple-element.35.weights_ref, ...), custom_call_target="tpu_custom_call" | custom-call | flops 536870912 | bytes 3538944 | tf_op jit(solution)/shard_map/pallas_call | solution.py:52
  22.4 1.6 %collective-permute-start.12 = (bf16[2,256,128]{2,1,0:T(8,128)(2,1)S(1)}, bf16[2,256,128]{2,1,0:T(8,128)(2,1)S(1)}, u32[]{:S(2)}, u32[]{:S(2)}) collective-permute-start(bf16[2,256,128]{2,1,0:T(8,128)(2,1)S(1)} %get-tuple-element.50), channel_id=1, source_target_pairs={{0,4},{1,5},{2,6},{3,7},{4,0},{5,1},{6,2},{7,3},{8,12},{9,13},{10,... | collective-permute-start | bytes 393224 | tf_op jit(solution)/shard_map/ppermute | solution.py:221
  24.0 0.5 %collective-permute-start.10 = (bf16[2,256,128]{2,1,0:T(8,128)(2,1)S(1)}, bf16[2,256,128]{2,1,0:T(8,128)(2,1)S(1)}, u32[]{:S(2)}, u32[]{:S(2)}) collective-permute-start(bf16[2,256,128]{2,1,0:T(8,128)(2,1)S(1)} %get-tuple-element.46), channel_id=1, source_target_pairs={{0,4},{1,5},{2,6},{3,7},{4,0},{5,1},{6,2},{7,3},{8,12},{9,13},{10,... | collective-permute-start | bytes 393224 | tf_op jit(solution)/shard_map/ppermute | solution.py:221
  24.5 5.7 %collective-permute-done.4.refs_0_ = bf16[2,256,128]{2,1,0:T(8,128)(2,1)S(1)} collective-permute-done((bf16[2,256,128]{2,1,0:T(8,128)(2,1)S(1)}, bf16[2,256,128]{2,1,0:T(8,128)(2,1)S(1)}, u32[]{:S(2)}, u32[]{:S(2)}) %collective-permute-start.4) | collective-permute-done | bytes 131104 | tf_op jit(solution)/shard_map/ppermute | solution.py:221
  30.2 0.0 collective-permute-done.5.refs_1_
  30.2 0.2 collective-permute-done.6.refs_2_
  30.4 0.1 shard_map.99
  30.5 1.6 %collective-permute-start.11 = (bf16[1,256,128]{2,1,0:T(8,128)(2,1)S(1)}, bf16[1,256,128]{2,1,0:T(8,128)(2,1)S(1)}, u32[]{:S(2)}, u32[]{:S(2)}) collective-permute-start(bf16[1,256,128]{2,1,0:T(8,128)(2,1)S(1)} %get-tuple-element.48), channel_id=1, source_target_pairs={{0,4},{1,5},{2,6},{3,7},{4,0},{5,1},{6,2},{7,3},{8,12},{9,13},{10,... | collective-permute-start | bytes 196616 | tf_op jit(solution)/shard_map/ppermute | solution.py:221
  32.0 0.0 collective-permute-done.12.refs_0_
  32.1 4.1 %collective-permute-start.13 = (bf16[1,256,128]{2,1,0:T(8,128)(2,1)S(1)}, bf16[1,256,128]{2,1,0:T(8,128)(2,1)S(1)}, u32[]{:S(2)}, u32[]{:S(2)}) collective-permute-start(bf16[1,256,128]{2,1,0:T(8,128)(2,1)S(1)} %get-tuple-element.51), channel_id=1, source_target_pairs={{0,16},{1,17},{2,18},{3,19},{4,20},{5,21},{6,22},{7,23},{8,24},{9,... | collective-permute-start | bytes 196616 | tf_op jit(solution)/shard_map/ppermute | solution.py:221
  36.2 0.4 %collective-permute-start.14 = (bf16[1,256,128]{2,1,0:T(8,128)(2,1)S(1)}, bf16[1,256,128]{2,1,0:T(8,128)(2,1)S(1)}, u32[]{:S(2)}, u32[]{:S(2)}) collective-permute-start(bf16[1,256,128]{2,1,0:T(8,128)(2,1)S(1)} %get-tuple-element.52), channel_id=1, source_target_pairs={{0,24},{1,25},{2,26},{3,27},{4,28},{5,29},{6,30},{7,31},{8,16},{9,... | collective-permute-start | bytes 196616 | tf_op jit(solution)/shard_map/ppermute | solution.py:221
  36.6 0.0 collective-permute-done.10.refs_0_
  36.7 0.3 collective-permute-start.15
  36.9 0.0 collective-permute-done.11.refs_2_
  36.9 2.9 %collective-permute-done.13.refs_3_ = bf16[1,256,128]{2,1,0:T(8,128)(2,1)S(1)} collective-permute-done((bf16[1,256,128]{2,1,0:T(8,128)(2,1)S(1)}, bf16[1,256,128]{2,1,0:T(8,128)(2,1)S(1)}, u32[]{:S(2)}, u32[]{:S(2)}) %collective-permute-start.13) | collective-permute-done | bytes 65568 | tf_op jit(solution)/shard_map/ppermute | solution.py:221
  39.8 2.5 %collective-permute-done.14.refs_4_ = bf16[1,256,128]{2,1,0:T(8,128)(2,1)S(1)} collective-permute-done((bf16[1,256,128]{2,1,0:T(8,128)(2,1)S(1)}, bf16[1,256,128]{2,1,0:T(8,128)(2,1)S(1)}, u32[]{:S(2)}, u32[]{:S(2)}) %collective-permute-start.14) | collective-permute-done | bytes 65568 | tf_op jit(solution)/shard_map/ppermute | solution.py:221
  42.4 0.0 collective-permute-done.15.refs_5_
  42.4 1.2 %shard_map.103 = (bf16[4,128,128]{2,1,0:T(8,128)(2,1)}, bf16[4,128,128]{2,1,0:T(8,128)(2,1)}) custom-call(bf16[4,128,128]{2,1,0:T(8,128)(2,1)S(1)} %get-tuple-element.31.consts_ref, f32[4,128,128]{2,1,0:T(8,128)S(1)} %get-tuple-element.34.base_ref, f32[1,256,128]{2,1,0:T(8,128)S(1)} %get-tuple-element.42.refs_0_, ...), custom_call_target="tpu_custom_call" | custom-call | bytes 1179648 | tf_op jit(solution)/shard_map/pallas_call | solution.py:52
  (8 shorter events, 0.1 us)
Async XLA Ops:
  0.6 9.0 %collective-permute-start = (bf16[4,8,64,128]{3,2,1,0:T(8,128)(2,1)}, bf16[4,8,64,128]{3,2,1,0:T(8,128)(2,1)S(1)}, u32[]{:S(2)}, u32[]{:S(2)}) collective-permute-start(bf16[4,8,64,128]{3,2,1,0:T(8,128)(2,1)} %block_ref.1), channel_id=1, source_target_pairs={{0,2},{1,3},{2,0},{3,1},{4,6},{5,7},{6,4},{7,5},{8,10},{9,11},{10,... | collective-permute-start | bytes 1572872 | tf_op jit(solution)/shard_map/ppermute | solution.py:221
  1.2 1.0 %copy-start.5 = (bf16[1024,2,128]{2,1,0:T(2,128)(2,1)S(1)}, bf16[1024,2,128]{2,1,0:T(2,128)(2,1)}, u32[]{:S(2)}) copy-start(bf16[1024,2,128]{2,1,0:T(2,128)(2,1)} %param.9) | copy-start | bytes 1572868
  2.2 2.9 %copy-start.2 = (f32[64,64]{1,0:T(8,128)S(1)}, f32[64,64]{1,0:T(8,128)}, u32[]{:S(2)}) copy-start(f32[64,64]{1,0:T(8,128)} %coupling_ref.1) | copy-start | bytes 49156
  2.2 7.9 %copy-start.6 = (s32[64]{0:T(128)S(1)}, s32[64]{0:T(128)}, u32[]{:S(2)}) copy-start(s32[64]{0:T(128)} %param.11) | copy-start | bytes 772
  2.2 7.9 %copy-start = (bf16[4,8,64,128]{3,2,1,0:T(8,128)(2,1)S(1)}, bf16[4,8,64,128]{3,2,1,0:T(8,128)(2,1)}, u32[]{:S(2)}) copy-start(bf16[4,8,64,128]{3,2,1,0:T(8,128)(2,1)} %block_ref.1) | copy-start | bytes 1572868
  2.2 7.9 %copy-start.1 = (bf16[256,2,128]{2,1,0:T(2,128)(2,1)S(1)}, bf16[256,2,128]{2,1,0:T(2,128)(2,1)}, u32[]{:S(2)}) copy-start(bf16[256,2,128]{2,1,0:T(2,128)(2,1)} %param.10) | copy-start | bytes 393220
  2.2 7.9 %copy-start.3 = (bf16[64,64]{1,0:T(8,128)(2,1)S(1)}, bf16[64,64]{1,0:T(8,128)(2,1)}, u32[]{:S(2)}) copy-start(bf16[64,64]{1,0:T(8,128)(2,1)} %ham_ref.1) | copy-start | bytes 24580
  2.3 7.9 %copy-start.4 = (s32[16]{0:T(128)S(1)}, s32[16]{0:T(128)}, u32[]{:S(2)}) copy-start(s32[16]{0:T(128)} %columns_ref.1) | copy-start | bytes 196
  2.3 5.7 %collective-permute-start.1 = (bf16[2,1,2,128,128]{4,3,2,1,0:T(8,128)(2,1)S(1)}, bf16[2,1,2,128,128]{4,3,2,1,0:T(8,128)(2,1)S(1)}, u32[]{:S(2)}, u32[]{:S(2)}) collective-permute-start(bf16[2,1,2,128,128]{4,3,2,1,0:T(8,128)(2,1)S(1)} %get-tuple-element.33), channel_id=1, source_target_pairs={{0,2},{1,3},{2,0},{3,1},{4,6},{5,7},{6,4},{7,5},{8,10},{9,11},{10,... | collective-permute-start | bytes 393224 | tf_op jit(solution)/shard_map/ppermute | solution.py:221
  2.4 13.6 %collective-permute-start.3 = (bf16[2,1,2,128,128]{4,3,2,1,0:T(8,128)(2,1)S(1)}, bf16[2,1,2,128,128]{4,3,2,1,0:T(8,128)(2,1)S(1)}, u32[]{:S(2)}, u32[]{:S(2)}) collective-permute-start(bf16[2,1,2,128,128]{4,3,2,1,0:T(8,128)(2,1)S(1)} %get-tuple-element.33), channel_id=1, source_target_pairs={{0,3},{1,2},{2,1},{3,0},{4,7},{5,6},{6,5},{7,4},{8,11},{9,10},{10,... | collective-permute-start | bytes 393224 | tf_op jit(solution)/shard_map/ppermute | solution.py:221
  6.7 14.8 %collective-permute-start.7 = (bf16[2,1,2,128,128]{4,3,2,1,0:T(8,128)(2,1)S(1)}, bf16[2,1,2,128,128]{4,3,2,1,0:T(8,128)(2,1)S(1)}, u32[]{:S(2)}, u32[]{:S(2)}) collective-permute-start(bf16[2,1,2,128,128]{4,3,2,1,0:T(8,128)(2,1)S(1)} %get-tuple-element.44), channel_id=1, source_target_pairs={{0,2},{1,3},{2,0},{3,1},{4,6},{5,7},{6,4},{7,5},{8,10},{9,11},{10,... | collective-permute-start | bytes 393224 | tf_op jit(solution)/shard_map/ppermute | solution.py:221
  7.2 14.5 %collective-permute-start.9 = (bf16[2,1,2,128,128]{4,3,2,1,0:T(8,128)(2,1)S(1)}, bf16[2,1,2,128,128]{4,3,2,1,0:T(8,128)(2,1)S(1)}, u32[]{:S(2)}, u32[]{:S(2)}) collective-permute-start(bf16[2,1,2,128,128]{4,3,2,1,0:T(8,128)(2,1)S(1)} %get-tuple-element.44), channel_id=1, source_target_pairs={{0,3},{1,2},{2,1},{3,0},{4,7},{5,6},{6,5},{7,4},{8,11},{9,10},{10,... | collective-permute-start | bytes 393224 | tf_op jit(solution)/shard_map/ppermute | solution.py:221
  8.0 8.0 %collective-permute-start.2 = (bf16[2,1,2,128,128]{4,3,2,1,0:T(8,128)(2,1)S(1)}, bf16[2,1,2,128,128]{4,3,2,1,0:T(8,128)(2,1)S(1)}, u32[]{:S(2)}, u32[]{:S(2)}) collective-permute-start(bf16[2,1,2,128,128]{4,3,2,1,0:T(8,128)(2,1)S(1)} %get-tuple-element.32.refs_0_), channel_id=1, source_target_pairs={{0,1},{1,0},{2,3},{3,2},{4,5},{5,4},{6,7},{7,6},{8,9},{9,8},{10,11... | collective-permute-start | bytes 393224 | tf_op jit(solution)/shard_map/ppermute | solution.py:221
  9.6 12.1 %collective-permute-start.8 = (bf16[2,1,2,128,128]{4,3,2,1,0:T(8,128)(2,1)S(1)}, bf16[2,1,2,128,128]{4,3,2,1,0:T(8,128)(2,1)S(1)}, u32[]{:S(2)}, u32[]{:S(2)}) collective-permute-start(bf16[2,1,2,128,128]{4,3,2,1,0:T(8,128)(2,1)S(1)} %get-tuple-element.43.refs_0_), channel_id=1, source_target_pairs={{0,1},{1,0},{2,3},{3,2},{4,5},{5,4},{6,7},{7,6},{8,9},{9,8},{10,11... | collective-permute-start | bytes 393224 | tf_op jit(solution)/shard_map/ppermute | solution.py:221
  17.5 12.7 %collective-permute-start.4 = (bf16[2,256,128]{2,1,0:T(8,128)(2,1)S(1)}, bf16[2,256,128]{2,1,0:T(8,128)(2,1)S(1)}, u32[]{:S(2)}, u32[]{:S(2)}) collective-permute-start(bf16[2,256,128]{2,1,0:T(8,128)(2,1)S(1)} %get-tuple-element.39), channel_id=1, source_target_pairs={{0,16},{1,17},{2,18},{3,19},{4,20},{5,21},{6,22},{7,23},{8,24},{9,... | collective-permute-start | bytes 393224 | tf_op jit(solution)/shard_map/ppermute | solution.py:221
  20.1 10.1 %collective-permute-start.5 = (bf16[2,256,128]{2,1,0:T(8,128)(2,1)S(1)}, bf16[2,256,128]{2,1,0:T(8,128)(2,1)S(1)}, u32[]{:S(2)}, u32[]{:S(2)}) collective-permute-start(bf16[2,256,128]{2,1,0:T(8,128)(2,1)S(1)} %get-tuple-element.40), channel_id=1, source_target_pairs={{0,24},{1,25},{2,26},{3,27},{4,28},{5,29},{6,30},{7,31},{8,16},{9,... | collective-permute-start | bytes 393224 | tf_op jit(solution)/shard_map/ppermute | solution.py:221
  21.5 9.0 %collective-permute-start.6 = (bf16[2,256,128]{2,1,0:T(8,128)(2,1)S(1)}, bf16[2,256,128]{2,1,0:T(8,128)(2,1)S(1)}, u32[]{:S(2)}, u32[]{:S(2)}) collective-permute-start(bf16[2,256,128]{2,1,0:T(8,128)(2,1)S(1)} %get-tuple-element.41), channel_id=1, source_target_pairs={{0,8},{1,9},{2,10},{3,11},{4,12},{5,13},{6,14},{7,15},{8,0},{9,1},... | collective-permute-start | bytes 393224 | tf_op jit(solution)/shard_map/ppermute | solution.py:221
  22.4 9.6 %collective-permute-start.12 = (bf16[2,256,128]{2,1,0:T(8,128)(2,1)S(1)}, bf16[2,256,128]{2,1,0:T(8,128)(2,1)S(1)}, u32[]{:S(2)}, u32[]{:S(2)}) collective-permute-start(bf16[2,256,128]{2,1,0:T(8,128)(2,1)S(1)} %get-tuple-element.50), channel_id=1, source_target_pairs={{0,4},{1,5},{2,6},{3,7},{4,0},{5,1},{6,2},{7,3},{8,12},{9,13},{10,... | collective-permute-start | bytes 393224 | tf_op jit(solution)/shard_map/ppermute | solution.py:221
  24.0 12.6 %collective-permute-start.10 = (bf16[2,256,128]{2,1,0:T(8,128)(2,1)S(1)}, bf16[2,256,128]{2,1,0:T(8,128)(2,1)S(1)}, u32[]{:S(2)}, u32[]{:S(2)}) collective-permute-start(bf16[2,256,128]{2,1,0:T(8,128)(2,1)S(1)} %get-tuple-element.46), channel_id=1, source_target_pairs={{0,4},{1,5},{2,6},{3,7},{4,0},{5,1},{6,2},{7,3},{8,12},{9,13},{10,... | collective-permute-start | bytes 393224 | tf_op jit(solution)/shard_map/ppermute | solution.py:221
  30.5 6.4 %collective-permute-start.11 = (bf16[1,256,128]{2,1,0:T(8,128)(2,1)S(1)}, bf16[1,256,128]{2,1,0:T(8,128)(2,1)S(1)}, u32[]{:S(2)}, u32[]{:S(2)}) collective-permute-start(bf16[1,256,128]{2,1,0:T(8,128)(2,1)S(1)} %get-tuple-element.48), channel_id=1, source_target_pairs={{0,4},{1,5},{2,6},{3,7},{4,0},{5,1},{6,2},{7,3},{8,12},{9,13},{10,... | collective-permute-start | bytes 196616 | tf_op jit(solution)/shard_map/ppermute | solution.py:221
  32.1 7.8 %collective-permute-start.13 = (bf16[1,256,128]{2,1,0:T(8,128)(2,1)S(1)}, bf16[1,256,128]{2,1,0:T(8,128)(2,1)S(1)}, u32[]{:S(2)}, u32[]{:S(2)}) collective-permute-start(bf16[1,256,128]{2,1,0:T(8,128)(2,1)S(1)} %get-tuple-element.51), channel_id=1, source_target_pairs={{0,16},{1,17},{2,18},{3,19},{4,20},{5,21},{6,22},{7,23},{8,24},{9,... | collective-permute-start | bytes 196616 | tf_op jit(solution)/shard_map/ppermute | solution.py:221
  36.2 6.2 %collective-permute-start.14 = (bf16[1,256,128]{2,1,0:T(8,128)(2,1)S(1)}, bf16[1,256,128]{2,1,0:T(8,128)(2,1)S(1)}, u32[]{:S(2)}, u32[]{:S(2)}) collective-permute-start(bf16[1,256,128]{2,1,0:T(8,128)(2,1)S(1)} %get-tuple-element.52), channel_id=1, source_target_pairs={{0,24},{1,25},{2,26},{3,27},{4,28},{5,29},{6,30},{7,31},{8,16},{9,... | collective-permute-start | bytes 196616 | tf_op jit(solution)/shard_map/ppermute | solution.py:221
  36.7 5.7 %collective-permute-start.15 = (bf16[1,256,128]{2,1,0:T(8,128)(2,1)S(1)}, bf16[1,256,128]{2,1,0:T(8,128)(2,1)S(1)}, u32[]{:S(2)}, u32[]{:S(2)}) collective-permute-start(bf16[1,256,128]{2,1,0:T(8,128)(2,1)S(1)} %get-tuple-element.53), channel_id=1, source_target_pairs={{0,8},{1,9},{2,10},{3,11},{4,12},{5,13},{6,14},{7,15},{8,0},{9,1},... | collective-permute-start | bytes 196616 | tf_op jit(solution)/shard_map/ppermute | solution.py:221

commit v5 on v4

--- a/solution.py
+++ b/solution.py
@@ -48,7 +48,7 @@
 
 
 def call(body, outs, *args, flops=0, grant=16, **keywords):
-    moved = sum(a.size * a.dtype.itemsize for a in list(args) + list(outs))
+    moved = sum(a.size * a.dtype.itemsize for a in jax.tree.leaves((args, outs)))
     return pl.pallas_call(
         body,
         out_shape=outs,
@@ -72,12 +72,13 @@
 
 def ready_body(count, coupling_ref, *refs):
     sources, consts_ref, sigmas = refs[:count], refs[count], refs[count + 1:]
-    orbitals = coupling_ref.shape[0]
-    lanes = 2 * orbitals
-    fold = (lax.broadcasted_iota(jnp.int32, (lanes, orbitals), 0) % orbitals == lax.broadcasted_iota(jnp.int32, (lanes, orbitals), 1)).astype(F32)
-    coupling = coupling_ref[...]
-    right = exact(exact(fold, coupling, ((1,), (1,))), fold, ((1,), (1,)))
-    consts = (*halves(right), *halves(row_matrix(coupling, consts_ref.shape[1])))
+    rows, lanes = consts_ref.shape[1:]
+    orbitals = lanes // 2
+    fold = one_hot(lanes, orbitals, lambda at: at % orbitals)
+    consts = []
+    for part in halves(coupling_ref[...]):
+        consts.append(across(across(fold, part).astype(BF16), fold).astype(BF16))
+    consts = [*consts, *(row_matrix(part, rows) for part in halves(coupling_ref[...]))]
     for at, value in enumerate(consts):
         consts_ref[at] = value
     for source, sigma in zip(sources, sigmas):
@@ -85,25 +86,29 @@
         sigma[...] = tiles.astype(BF16).reshape(source.shape)
 
 
-def exact(left, right, dims):
-    return lax.dot_general(left, right, (dims, ((), ())), precision=lax.Precision.HIGHEST, preferred_element_type=F32)
+def one_hot(rows, orbitals, orbital_of):
+    at = lax.broadcasted_iota(jnp.int32, (rows, orbitals), 0)
+    return (orbital_of(at) == lax.broadcasted_iota(jnp.int32, (rows, orbitals), 1)).astype(F32).astype(BF16)
+
+
+def across(left, right):
+    return lax.dot_general(left, right, (((1,), (1,)), ((), ())), preferred_element_type=F32)
 
 
 def row_matrix(matrix, rows):
     orbitals = matrix.shape[0]
     panels = rows // orbitals
-    spread = (lax.broadcasted_iota(jnp.int32, (rows, orbitals), 0) // panels == lax.broadcasted_iota(jnp.int32, (rows, orbitals), 1)).astype(F32)
-    same = (lax.broadcasted_iota(jnp.int32, (rows, rows), 0) % panels == lax.broadcasted_iota(jnp.int32, (rows, rows), 1) % panels).astype(F32)
-    return exact(exact(spread, matrix, ((1,), (0,))), spread, ((1,), (1,))) * same
-
-
-def early_body(n_early, slot_of, groups, deal_ref, columns_ref, consts_ref, ham_ref, panel_ref, block_ref, other_ref, *refs):
+    spread = one_hot(rows, orbitals, lambda at: at // panels)
+    row_at = lax.broadcasted_iota(jnp.int32, (rows, rows), 0)
+    lane_at = lax.broadcasted_iota(jnp.int32, (rows, rows), 1)
+    spreaded = across(dot(spread, matrix).astype(BF16), spread)
+    return jnp.where(row_at % panels == lane_at % panels, spreaded, 0.0).astype(BF16)
+
+
+def early_body(n_early, slot_of, groups, deal_ref, columns_ref, consts_ref, block_ref, other_ref, *refs):
     early = refs[:n_early]
-    weights_ref, base_ref = refs[n_early:n_early + 2]
-    sigmas = refs[n_early + 2:]
-    orbitals = ham_ref.shape[0]
-    lanes = 2 * orbitals
-    rows = panel_ref.shape[1]
+    weights_ref, sigmas = refs[n_early], refs[n_early + 1:]
+    orbitals, lanes = block_ref.shape[2:]
     mem, hist = lax.axis_index("mem"), lax.axis_index("hist")
     pair = mem >> 1
     slots, columns = block_ref.shape[0], block_ref.shape[1]
@@ -112,13 +117,6 @@
     for source, sigma in zip(early, sigmas):
         tiles = sigma_tiles(source[...].reshape((-1,) + source.shape[3:]), consts)
         sigma[...] = tiles.astype(BF16).reshape(source.shape)
-
-    ham = row_matrix(ham_ref[...].astype(F32), rows).astype(BF16)
-    sign = jnp.where(lax.broadcasted_iota(jnp.int32, (rows, lanes), 1) < orbitals, 1.0, -1.0).astype(F32)
-    for tile in range(panel_ref.shape[0]):
-        values = panel_ref[tile]
-        turned = pltpu.roll(dot(ham, values), orbitals, 1) * sign
-        base_ref[tile] = values.astype(F32) + time_step * turned
 
     flip = jnp.where(lax.broadcasted_iota(jnp.int32, (orbitals, lanes), 1) < orbitals, -1.0, 1.0).astype(F32)
     own_column = pair // groups
@@ -172,22 +170,34 @@
         out[...] = total[at * size:(at + 1) * size].astype(out.dtype)
 
 
-def last_body(counts, consts_ref, base_ref, *refs):
-    chunks = len(counts)
-    keeps, gots = refs[:chunks], refs[chunks:-2]
-    rows_ref, sigma_ref = refs[-2:]
-    consts = tuple(consts_ref[at] for at in range(4))
-    size = base_ref.shape[0] // chunks
-    for c in range(chunks):
-        here = slice(c * size, (c + 1) * size)
-        collision = keeps[c][...]
-        for got in gots[:counts[c]]:
-            collision = collision + got[...].astype(F32)
-        gots = gots[counts[c]:]
-        collision = collision.reshape((size,) + base_ref.shape[1:])
-        rows = (base_ref[here] + time_step * collision).astype(BF16)
-        rows_ref[here] = rows
-        sigma_ref[here] = sigma_tiles(rows, consts).astype(BF16)
+def base_body(ham_ref, panel_ref, base_ref):
+    rows, lanes = panel_ref.shape[1:]
+    orbitals = ham_ref.shape[0]
+    ham = row_matrix(ham_ref[...], rows)
+    sign = jnp.where(lax.broadcasted_iota(jnp.int32, (rows, lanes), 1) < orbitals, 1.0, -1.0).astype(F32)
+    for tile in range(panel_ref.shape[0]):
+        values = panel_ref[tile]
+        turned = pltpu.roll(dot(ham, values), orbitals, 1) * sign
+        base_ref[tile] = values.astype(F32) + time_step * turned
+
+
+def last_body(c, n_got, consts_ref, base_ref, keep_ref, *refs):
+    gots = refs[:n_got]
+    rows_out, sigma_out, rows_ref, sigma_ref, sems = refs[-5:]
+    size = rows_ref.shape[0]
+    here = pl.ds(c * size, size)
+    collision = keep_ref[...]
+    for got in gots:
+        collision = collision + got[...].astype(F32)
+    collision = collision.reshape(rows_ref.shape)
+    rows_ref[...] = (base_ref[here] + time_step * collision).astype(BF16)
+    rows_copy = pltpu.make_async_copy(rows_ref, rows_out.at[here], sems.at[0])
+    rows_copy.start()
+    sigma_ref[...] = sigma_tiles(rows_ref[...], tuple(consts_ref[at] for at in range(4))).astype(BF16)
+    sigma_copy = pltpu.make_async_copy(sigma_ref, sigma_out.at[here], sems.at[1])
+    sigma_copy.start()
+    rows_copy.wait()
+    sigma_copy.wait()
 
 
 def step_masks(count):
@@ -267,12 +277,12 @@
         def slot_of(q, hist):
             return q // held, q % held
 
-    outs = [shape((2 * slots * lanes, columns * lanes), BF16), shape((own_tiles, rows, lanes), F32), piece, piece]
-    weights, base, *sigmas = call(
+    outs = [shape((2 * slots * lanes, columns * lanes), BF16), piece, piece]
+    weights, *sigmas = call(
         functools.partial(early_body, 2, slot_of, groups),
         outs,
-        kept_times, column_times, consts, hamiltonian, panel_tiles, memory_block, partner_block, mine[0], partner[0],
-        in_specs=[smem] * 2 + [vmem] * 7,
+        kept_times, column_times, consts, memory_block, partner_block, mine[0], partner[0],
+        in_specs=[smem] * 2 + [vmem] * 5,
     )
 
     keeps, received = [], []
@@ -294,13 +304,30 @@
         def pieces(masks, count):
             return [shape((count, height, lanes), BF16 if mask else F32) for mask in masks]
 
-        outs = call(
-            functools.partial(term_body, len(done), len(late), block_places(steps, parts), groups),
-            pieces(steps[0], count) * parts,
-            consts, weights, *done, *late,
-            flops=2 * height * groups * 2 * slots * lanes * columns * lanes,
-            scratch_shapes=[pltpu.VMEM((height, 2 * slots * lanes), BF16)],
-        )
+        def term(places, outs):
+            return call(
+                functools.partial(term_body, len(done), len(late), places, groups),
+                outs,
+                consts, weights, *done, *late,
+                flops=2 * height * groups * 2 * slots * lanes * columns * lanes,
+                scratch_shapes=[pltpu.VMEM((height, 2 * slots * lanes), BF16)],
+            )
+
+        if c < chunks - 1 and len(steps) == 2 and len(steps[0]) == 4:
+            (near, far, side, _), (last, _) = steps
+            places = {near ^ last: (0, 0), near: (0, 1), far ^ last: (1, 0), far: (2, 0), side ^ last: (3, 0), side: (3, 1), last: (4, 0), 0: (4, 1)}
+            sizes = ((2, BF16), (1, BF16), (1, F32), (2, BF16), (2, F32))
+            to_near, to_last, to_far, to_side, keep = term(places, [shape((count, height, lanes), kind) for count, kind in sizes])
+            got_near = exchange(to_near, 2 * near, 0)
+            (to_far,) = call(functools.partial(add_body, 1), [shape((1, height, lanes), BF16)], to_far, exchange(to_last, 2 * last, 0))
+            got_far = exchange(to_far, 2 * far, 0)
+            got_side = exchange(to_side, 2 * side, 0)
+            send, keep = call(functools.partial(add_body, 2), [shape((1, height, lanes), kind) for kind in (BF16, F32)], keep, got_near, got_side)
+            keeps.append(keep)
+            received.append([exchange(send, 2 * last, 0), got_far])
+            continue
+
+        outs = term(block_places(steps, parts), pieces(steps[0], count) * parts)
         size = len(steps[0])
         state = [(outs[p * size:(p + 1) * size - 1], outs[(p + 1) * size - 1]) for p in range(parts)]
         for at, masks in enumerate(steps):
@@ -317,12 +344,21 @@
         keeps.append(state[0][1])
         received.append(gots[0])
 
-    result = shape((own_tiles, rows, lanes), BF16)
-    new_rows, new_sigma = call(
-        functools.partial(last_body, [len(gots) for gots in received]),
-        [result, result],
-        consts, base, *keeps, *[got for gots in received for got in gots],
-    )
+    base = call(base_body, shape((own_tiles, rows, lanes), F32), hamiltonian, panel_tiles)
+    anywhere = pl.BlockSpec(memory_space=pl.ANY)
+    result = []
+    for c in range(chunks):
+        given = [consts, base, keeps[c], *received[c]]
+        result = call(
+            functools.partial(last_body, c, len(received[c])),
+            [shape((own_tiles, rows, lanes), BF16)] * 2,
+            *given, *result,
+            in_specs=[vmem] * len(given) + [anywhere] * len(result),
+            out_specs=[anywhere] * 2,
+            input_output_aliases={len(given) + at: at for at in range(len(result))},
+            scratch_shapes=[pltpu.VMEM((part, rows, lanes), BF16)] * 2 + [pltpu.SemaphoreType.DMA((2,))],
+        )
+    new_rows, new_sigma = result
     return new_rows.reshape(panel_rows.shape), new_sigma.reshape(panel_rows.shape)
 
 

time: 43.7 us -> 42.6 us (0.975)
  waiting for transfers between devices: 15.4 us -> 12 us
  starting transfers between devices: 18.8 us -> 20.4 us
  Pallas kernels: 6.94 us -> 7.53 us
    ppermute x16 -> x17, waiting for transfers between devices: 15.4 us -> 12 us  [exchange(): return lax.ppermute(value, ('mem', 'hist'), pairs)]
    ppermute x16 -> x17, starting transfers between devices: 18.8 us -> 20.4 us  [exchange(): return lax.ppermute(value, ('mem', 'hist'), pairs)]
    pallas_call x9 -> x12, Pallas kernels: 6.94 us -> 7.53 us  [call(): pl.pallas_call(body, out_shape=outs, cost_estimate=pl.CostEstimate(flops=...]
  transfers between devices with their start and end apart: 16 -> 17, of which waited for: 5 -> 4; matrix products, arithmetic and copies ran while one was open for 0% -> 0% of each run, Pallas kernels for 13% -> 15%
where the time goes in v5:
time: 42.6 us; the launch traced here: 42.4 us
  starting transfers between devices  20.4 us (48%)
  waiting for transfers between devices  12 us (28%)
  Pallas kernels  7.53 us (18%)
  between operations  1.41 us (3%)
  local copies, waits for them, and re-layouts  1.06 us (2%)
    ppermute x17, starting transfers between devices, exchange(): return lax.ppermute(value, ('mem', 'hist'), pairs)  20.4 us
    ppermute x17, waiting for transfers between devices, exchange(): return lax.ppermute(value, ('mem', 'hist'), pairs)  12 us
    pallas_call x12, Pallas kernels, call(): pl.pallas_call(body, out_shape=outs, cost_estimate=pl.CostEstimate(flops=...  7.53 us
    unnamed x14, local copies, waits for them, and re-layouts  1.06 us
  transfers between devices with their start and end apart: 17, of which 4 were waited for; matrix products, arithmetic and copies ran while one was open for 0% of the time, Pallas kernels for 15%

profile of v5, /device:TPU:0, one launch (start us, length us, event | category | flops | bytes accessed | tf_op | source)
XLA Modules:
  0.0 42.4 jit_solution(16460888997931779092)
XLA Ops:
  0.6 0.6 %collective-permute-start = (bf16[4,8,64,128]{3,2,1,0:T(8,128)(2,1)}, bf16[4,8,64,128]{3,2,1,0:T(8,128)(2,1)S(1)}, u32[]{:S(2)}, u32[]{:S(2)}) collective-permute-start(bf16[4,8,64,128]{3,2,1,0:T(8,128)(2,1)} %block_ref.1), channel_id=1, source_target_pairs={{0,2},{1,3},{2,0},{3,1},{4,6},{5,7},{6,4},{7,5},{8,10},{9,11},{10,... | collective-permute-start | bytes 1572872 | tf_op jit(solution)/shard_map/ppermute | solution.py:231
  1.2 1.0 %copy-done.5 = bf16[1024,2,128]{2,1,0:T(2,128)(2,1)S(1)} copy-done((bf16[1024,2,128]{2,1,0:T(2,128)(2,1)S(1)}, bf16[1024,2,128]{2,1,0:T(2,128)(2,1)}, u32[]{:S(2)}) %copy-start.5) | copy-done | bytes 524312
  2.3 0.1 collective-permute-start.1
  2.4 2.7 %collective-permute-start.11 = (bf16[2,1,2,128,128]{4,3,2,1,0:T(8,128)(2,1)S(1)}, bf16[2,1,2,128,128]{4,3,2,1,0:T(8,128)(2,1)S(1)}, u32[]{:S(2)}, u32[]{:S(2)}) collective-permute-start(bf16[2,1,2,128,128]{4,3,2,1,0:T(8,128)(2,1)S(1)} %get-tuple-element.35), channel_id=1, source_target_pairs={{0,3},{1,2},{2,1},{3,0},{4,7},{5,6},{6,5},{7,4},{8,11},{9,10},{10,... | collective-permute-start | bytes 393224 | tf_op jit(solution)/shard_map/ppermute | solution.py:231
  5.1 0.0 copy-done.2
  5.1 1.1 %shard_map.96 = (bf16[4,128,128]{2,1,0:T(8,128)(2,1)S(1)}, bf16[2,1,2,128,128]{4,3,2,1,0:T(8,128)(2,1)S(1)}, bf16[2,1,2,128,128]{4,3,2,1,0:T(8,128)(2,1)S(1)}) custom-call(f32[64,64]{1,0:T(8,128)S(1)} %copy-done.2, bf16[2,1,2,128,128]{4,3,2,1,0:T(8,128)(2,1)S(1)} %get-tuple-element.31.refs_0_, bf16[2,1,2,128,128]{4,3,2,1,0:T(8,128)(2,1)S(1)} %get-tuple-element.32.refs_1_), custom_call_target="tpu_custom_call" | custom-call | bytes 671744 | tf_op jit(solution)/shard_map/pallas_call | solution.py:52
  6.2 0.5 %collective-permute-start.2 = (bf16[2,1,2,128,128]{4,3,2,1,0:T(8,128)(2,1)S(1)}, bf16[2,1,2,128,128]{4,3,2,1,0:T(8,128)(2,1)S(1)}, u32[]{:S(2)}, u32[]{:S(2)}) collective-permute-start(bf16[2,1,2,128,128]{4,3,2,1,0:T(8,128)(2,1)S(1)} %get-tuple-element.38), channel_id=1, source_target_pairs={{0,2},{1,3},{2,0},{3,1},{4,6},{5,7},{6,4},{7,5},{8,10},{9,11},{10,... | collective-permute-start | bytes 393224 | tf_op jit(solution)/shard_map/ppermute | solution.py:231
  6.7 0.2 collective-permute-start.4
  7.5 0.0 collective-permute-done.1.refs_1_
  7.5 1.6 %collective-permute-start.10 = (bf16[2,1,2,128,128]{4,3,2,1,0:T(8,128)(2,1)S(1)}, bf16[2,1,2,128,128]{4,3,2,1,0:T(8,128)(2,1)S(1)}, u32[]{:S(2)}, u32[]{:S(2)}) collective-permute-start(bf16[2,1,2,128,128]{4,3,2,1,0:T(8,128)(2,1)S(1)} %get-tuple-element.34.refs_0_), channel_id=1, source_target_pairs={{0,1},{1,0},{2,3},{3,2},{4,5},{5,4},{6,7},{7,6},{8,9},{9,8},{10,11... | collective-permute-start | bytes 393224 | tf_op jit(solution)/shard_map/ppermute | solution.py:231
  9.1 0.0 collective-permute-done.other_ref
  9.1 0.5 %collective-permute-start.3 = (bf16[2,1,2,128,128]{4,3,2,1,0:T(8,128)(2,1)S(1)}, bf16[2,1,2,128,128]{4,3,2,1,0:T(8,128)(2,1)S(1)}, u32[]{:S(2)}, u32[]{:S(2)}) collective-permute-start(bf16[2,1,2,128,128]{4,3,2,1,0:T(8,128)(2,1)S(1)} %get-tuple-element.37.refs_0_), channel_id=1, source_target_pairs={{0,1},{1,0},{2,3},{3,2},{4,5},{5,4},{6,7},{7,6},{8,9},{9,8},{10,11... | collective-permute-start | bytes 393224 | tf_op jit(solution)/shard_map/ppermute | solution.py:231
  9.6 0.0 copy-done.6
  9.6 0.0 copy-done
  9.6 0.0 copy-done.4
  9.6 1.4 %shard_map.98 = (bf16[1024,1024]{1,0:T(8,128)(2,1)S(1)}, bf16[2,1,2,128,128]{4,3,2,1,0:T(8,128)(2,1)S(1)}, bf16[2,1,2,128,128]{4,3,2,1,0:T(8,128)(2,1)S(1)}) custom-call(s32[64]{0:T(128)S(1)} %compare_select_fusion.deal_ref, s32[16]{0:T(128)S(1)} %copy-done.4, bf16[4,128,128]{2,1,0:T(8,128)(2,1)S(1)} %get-tuple-element.33.consts_ref, ...), custom_call_target="tpu_custom_call" | custom-call | bytes 3801408 | tf_op jit(solution)/shard_map/pallas_call | solution.py:52
  11.1 4.5 %collective-permute-done.10.refs_2_ = bf16[2,1,2,128,128]{4,3,2,1,0:T(8,128)(2,1)S(1)} collective-permute-done((bf16[2,1,2,128,128]{4,3,2,1,0:T(8,128)(2,1)S(1)}, bf16[2,1,2,128,128]{4,3,2,1,0:T(8,128)(2,1)S(1)}, u32[]{:S(2)}, u32[]{:S(2)}) %collective-permute-start.10) | collective-permute-done | bytes 131104 | tf_op jit(solution)/shard_map/ppermute | solution.py:231
  15.5 0.0 collective-permute-done.11.refs_3_
  15.5 1.4 %shard_map.102 = (bf16[2,256,128]{2,1,0:T(8,128)(2,1)S(1)}, bf16[1,256,128]{2,1,0:T(8,128)(2,1)S(1)}, f32[1,256,128]{2,1,0:T(8,128)S(1)}, bf16[2,256,128]{2,1,0:T(8,128)(2,1)S(1)}, f32[2,256,128]{2,1,0:T(8,128)S(1)}) custom-call(bf16[4,128,128]{2,1,0:T(8,128)(2,1)S(1)} %get-tuple-element.33.consts_ref, bf16[1024,1024]{1,0:T(8,128)(2,1)S(1)} %get-tuple-element.36.weights_ref, ...), custom_call_target="tpu_custom_call" | custom-call | flops 536870912 | bytes 3473408 | tf_op jit(solution)/shard_map/pallas_call | solution.py:52
  17.0 2.7 %collective-permute-start.12 = (bf16[2,256,128]{2,1,0:T(8,128)(2,1)S(1)}, bf16[2,256,128]{2,1,0:T(8,128)(2,1)S(1)}, u32[]{:S(2)}, u32[]{:S(2)}) collective-permute-start(bf16[2,256,128]{2,1,0:T(8,128)(2,1)S(1)} %get-tuple-element.50), channel_id=1, source_target_pairs={{0,16},{1,17},{2,18},{3,19},{4,20},{5,21},{6,22},{7,23},{8,24},{9,... | collective-permute-start | bytes 393224 | tf_op jit(solution)/shard_map/ppermute | solution.py:231
  19.6 1.6 %collective-permute-start.13 = (bf16[2,256,128]{2,1,0:T(8,128)(2,1)S(1)}, bf16[2,256,128]{2,1,0:T(8,128)(2,1)S(1)}, u32[]{:S(2)}, u32[]{:S(2)}) collective-permute-start(bf16[2,256,128]{2,1,0:T(8,128)(2,1)S(1)} %get-tuple-element.51), channel_id=1, source_target_pairs={{0,8},{1,9},{2,10},{3,11},{4,12},{5,13},{6,14},{7,15},{8,0},{9,1},... | collective-permute-start | bytes 393224 | tf_op jit(solution)/shard_map/ppermute | solution.py:231
  21.2 0.0 collective-permute-done.2.refs_1_
  21.2 0.0 collective-permute-done.3.refs_2_
  21.2 0.0 collective-permute-done.4.refs_3_
  21.2 0.7 %shard_map.99 = (bf16[2,256,128]{2,1,0:T(8,128)(2,1)S(1)}, f32[2,256,128]{2,1,0:T(8,128)S(1)}, bf16[2,256,128]{2,1,0:T(8,128)(2,1)S(1)}, f32[2,256,128]{2,1,0:T(8,128)S(1)}) custom-call(bf16[4,128,128]{2,1,0:T(8,128)(2,1)S(1)} %get-tuple-element.33.consts_ref, bf16[1024,1024]{1,0:T(8,128)(2,1)S(1)} %get-tuple-element.36.weights_ref, ...), custom_call_target="tpu_custom_call" | custom-call | flops 536870912 | bytes 3538944 | tf_op jit(solution)/shard_map/pallas_call | solution.py:52
  22.0 1.6 %collective-permute-start.6 = (bf16[2,256,128]{2,1,0:T(8,128)(2,1)S(1)}, bf16[2,256,128]{2,1,0:T(8,128)(2,1)S(1)}, u32[]{:S(2)}, u32[]{:S(2)}) collective-permute-start(bf16[2,256,128]{2,1,0:T(8,128)(2,1)S(1)} %get-tuple-element.43), channel_id=1, source_target_pairs={{0,4},{1,5},{2,6},{3,7},{4,0},{5,1},{6,2},{7,3},{8,12},{9,13},{10,... | collective-permute-start | bytes 393224 | tf_op jit(solution)/shard_map/ppermute | solution.py:231
  23.5 0.5 %collective-permute-start.5 = (bf16[2,256,128]{2,1,0:T(8,128)(2,1)S(1)}, bf16[2,256,128]{2,1,0:T(8,128)(2,1)S(1)}, u32[]{:S(2)}, u32[]{:S(2)}) collective-permute-start(bf16[2,256,128]{2,1,0:T(8,128)(2,1)S(1)} %get-tuple-element.40), channel_id=1, source_target_pairs={{0,4},{1,5},{2,6},{3,7},{4,0},{5,1},{6,2},{7,3},{8,12},{9,13},{10,... | collective-permute-start | bytes 393224 | tf_op jit(solution)/shard_map/ppermute | solution.py:231
  24.0 1.5 %collective-permute-start.15 = (bf16[1,256,128]{2,1,0:T(8,128)(2,1)S(1)}, bf16[1,256,128]{2,1,0:T(8,128)(2,1)S(1)}, u32[]{:S(2)}, u32[]{:S(2)}) collective-permute-start(bf16[1,256,128]{2,1,0:T(8,128)(2,1)S(1)} %get-tuple-element.55), channel_id=1, source_target_pairs={{0,4},{1,5},{2,6},{3,7},{4,0},{5,1},{6,2},{7,3},{8,12},{9,13},{10,... | collective-permute-start | bytes 196616 | tf_op jit(solution)/shard_map/ppermute | solution.py:231
  25.5 5.1 %collective-permute-done.15.refs_0_ = bf16[1,256,128]{2,1,0:T(8,128)(2,1)S(1)} collective-permute-done((bf16[1,256,128]{2,1,0:T(8,128)(2,1)S(1)}, bf16[1,256,128]{2,1,0:T(8,128)(2,1)S(1)}, u32[]{:S(2)}, u32[]{:S(2)}) %collective-permute-start.15) | collective-permute-done | bytes 65568 | tf_op jit(solution)/shard_map/ppermute | solution.py:231
  30.7 1.4 %collective-permute-start.16 = (bf16[1,256,128]{2,1,0:T(8,128)(2,1)S(1)}, bf16[1,256,128]{2,1,0:T(8,128)(2,1)S(1)}, u32[]{:S(2)}, u32[]{:S(2)}) collective-permute-start(bf16[1,256,128]{2,1,0:T(8,128)(2,1)S(1)} %shard_map.104), channel_id=1, source_target_pairs={{0,24},{1,25},{2,26},{3,27},{4,28},{5,29},{6,30},{7,31},{8,16},{9,... | collective-permute-start | bytes 196616 | tf_op jit(solution)/shard_map/ppermute | solution.py:231
  32.1 0.0 collective-permute-done.12.refs_0_
  32.1 0.0 collective-permute-done.13.refs_1_
  32.1 1.6 %collective-permute-start.14 = (bf16[1,256,128]{2,1,0:T(8,128)(2,1)S(1)}, bf16[1,256,128]{2,1,0:T(8,128)(2,1)S(1)}, u32[]{:S(2)}, u32[]{:S(2)}) collective-permute-start(bf16[1,256,128]{2,1,0:T(8,128)(2,1)S(1)} %get-tuple-element.53), channel_id=1, source_target_pairs={{0,4},{1,5},{2,6},{3,7},{4,0},{5,1},{6,2},{7,3},{8,12},{9,13},{10,... | collective-permute-start | bytes 196616 | tf_op jit(solution)/shard_map/ppermute | solution.py:231
  33.7 0.0 collective-permute-done.6.refs_0_
  33.7 0.7 %collective-permute-start.7 = (bf16[1,256,128]{2,1,0:T(8,128)(2,1)S(1)}, bf16[1,256,128]{2,1,0:T(8,128)(2,1)S(1)}, u32[]{:S(2)}, u32[]{:S(2)}) collective-permute-start(bf16[1,256,128]{2,1,0:T(8,128)(2,1)S(1)} %get-tuple-element.44), channel_id=1, source_target_pairs={{0,16},{1,17},{2,18},{3,19},{4,20},{5,21},{6,22},{7,23},{8,24},{9,... | collective-permute-start | bytes 196616 | tf_op jit(solution)/shard_map/ppermute | solution.py:231
  34.4 2.0 %collective-permute-start.8 = (bf16[1,256,128]{2,1,0:T(8,128)(2,1)S(1)}, bf16[1,256,128]{2,1,0:T(8,128)(2,1)S(1)}, u32[]{:S(2)}, u32[]{:S(2)}) collective-permute-start(bf16[1,256,128]{2,1,0:T(8,128)(2,1)S(1)} %get-tuple-element.45), channel_id=1, source_target_pairs={{0,24},{1,25},{2,26},{3,27},{4,28},{5,29},{6,30},{7,31},{8,16},{9,... | collective-permute-start | bytes 196616 | tf_op jit(solution)/shard_map/ppermute | solution.py:231
  36.4 0.0 collective-permute-done.5.refs_0_
  36.4 0.9 %collective-permute-start.9 = (bf16[1,256,128]{2,1,0:T(8,128)(2,1)S(1)}, bf16[1,256,128]{2,1,0:T(8,128)(2,1)S(1)}, u32[]{:S(2)}, u32[]{:S(2)}) collective-permute-start(bf16[1,256,128]{2,1,0:T(8,128)(2,1)S(1)} %get-tuple-element.46), channel_id=1, source_target_pairs={{0,8},{1,9},{2,10},{3,11},{4,12},{5,13},{6,14},{7,15},{8,0},{9,1},... | collective-permute-start | bytes 196616 | tf_op jit(solution)/shard_map/ppermute | solution.py:231
  37.3 0.0 copy-done.1
  37.3 0.0 copy-done.3
  37.3 0.5 %shard_map.97.base_ref = f32[4,128,128]{2,1,0:T(8,128)S(1)} custom-call(bf16[64,64]{1,0:T(8,128)(2,1)S(1)} %copy-done.3, bf16[4,128,128]{2,1,0:T(8,128)(2,1)S(1)} %bitcast.6), custom_call_target="tpu_custom_call" | custom-call | bytes 401408 | tf_op jit(solution)/shard_map/pallas_call | solution.py:52
  37.9 0.0 collective-permute-done.16.refs_1_
  37.9 0.0 collective-permute-done.14.refs_0_
  37.9 1.1 %shard_map.105 = (bf16[4,128,128]{2,1,0:T(8,128)(2,1)}, bf16[4,128,128]{2,1,0:T(8,128)(2,1)}) custom-call(bf16[4,128,128]{2,1,0:T(8,128)(2,1)S(1)} %get-tuple-element.33.consts_ref, f32[4,128,128]{2,1,0:T(8,128)S(1)} %shard_map.97.base_ref, f32[1,256,128]{2,1,0:T(8,128)S(1)} %get-tuple-element.52.keep_ref, ...), custom_call_target="tpu_custom_call" | custom-call | bytes 917504 | tf_op jit(solution)/shard_map/pallas_call | solution.py:52
  39.0 1.6 %collective-permute-done.7.refs_0_ = bf16[1,256,128]{2,1,0:T(8,128)(2,1)S(1)} collective-permute-done((bf16[1,256,128]{2,1,0:T(8,128)(2,1)S(1)}, bf16[1,256,128]{2,1,0:T(8,128)(2,1)S(1)}, u32[]{:S(2)}, u32[]{:S(2)}) %collective-permute-start.7) | collective-permute-done | bytes 65568 | tf_op jit(solution)/shard_map/ppermute | solution.py:231
  40.6 0.0 collective-permute-done.8.refs_1_
  40.6 0.7 %collective-permute-done.9.refs_2_ = bf16[1,256,128]{2,1,0:T(8,128)(2,1)S(1)} collective-permute-done((bf16[1,256,128]{2,1,0:T(8,128)(2,1)S(1)}, bf16[1,256,128]{2,1,0:T(8,128)(2,1)S(1)}, u32[]{:S(2)}, u32[]{:S(2)}) %collective-permute-start.9) | collective-permute-done | bytes 65568 | tf_op jit(solution)/shard_map/ppermute | solution.py:231
  41.3 1.1 %shard_map.106 = (bf16[4,128,128]{2,1,0:T(8,128)(2,1)}, bf16[4,128,128]{2,1,0:T(8,128)(2,1)}) custom-call(bf16[4,128,128]{2,1,0:T(8,128)(2,1)S(1)} %get-tuple-element.33.consts_ref, f32[4,128,128]{2,1,0:T(8,128)S(1)} %shard_map.97.base_ref, f32[1,256,128]{2,1,0:T(8,128)S(1)} %get-tuple-element.41.keep_ref, ...), custom_call_target="tpu_custom_call", output_to_operand_aliasing={{0}: (6, {}), {1}: (7, {})} | custom-call | bytes 1245184 | tf_op jit(solution)/shard_map/pallas_call | solution.py:52
  (13 shorter events, 0.2 us)
Async XLA Ops:
  0.6 8.5 %collective-permute-start = (bf16[4,8,64,128]{3,2,1,0:T(8,128)(2,1)}, bf16[4,8,64,128]{3,2,1,0:T(8,128)(2,1)S(1)}, u32[]{:S(2)}, u32[]{:S(2)}) collective-permute-start(bf16[4,8,64,128]{3,2,1,0:T(8,128)(2,1)} %block_ref.1), channel_id=1, source_target_pairs={{0,2},{1,3},{2,0},{3,1},{4,6},{5,7},{6,4},{7,5},{8,10},{9,11},{10,... | collective-permute-start | bytes 1572872 | tf_op jit(solution)/shard_map/ppermute | solution.py:231
  1.2 1.0 %copy-start.5 = (bf16[1024,2,128]{2,1,0:T(2,128)(2,1)S(1)}, bf16[1024,2,128]{2,1,0:T(2,128)(2,1)}, u32[]{:S(2)}) copy-start(bf16[1024,2,128]{2,1,0:T(2,128)(2,1)} %param.9) | copy-start | bytes 1572868
  2.2 2.8 %copy-start.2 = (f32[64,64]{1,0:T(8,128)S(1)}, f32[64,64]{1,0:T(8,128)}, u32[]{:S(2)}) copy-start(f32[64,64]{1,0:T(8,128)} %coupling_ref.1) | copy-start | bytes 49156
  2.2 7.4 %copy-start.6 = (s32[64]{0:T(128)S(1)}, s32[64]{0:T(128)}, u32[]{:S(2)}) copy-start(s32[64]{0:T(128)} %param.11) | copy-start | bytes 772
  2.2 7.4 %copy-start = (bf16[4,8,64,128]{3,2,1,0:T(8,128)(2,1)S(1)}, bf16[4,8,64,128]{3,2,1,0:T(8,128)(2,1)}, u32[]{:S(2)}) copy-start(bf16[4,8,64,128]{3,2,1,0:T(8,128)(2,1)} %block_ref.1) | copy-start | bytes 1572868
  2.2 7.4 %copy-start.4 = (s32[16]{0:T(128)S(1)}, s32[16]{0:T(128)}, u32[]{:S(2)}) copy-start(s32[16]{0:T(128)} %columns_ref.1) | copy-start | bytes 196
  2.3 5.2 %collective-permute-start.1 = (bf16[2,1,2,128,128]{4,3,2,1,0:T(8,128)(2,1)S(1)}, bf16[2,1,2,128,128]{4,3,2,1,0:T(8,128)(2,1)S(1)}, u32[]{:S(2)}, u32[]{:S(2)}) collective-permute-start(bf16[2,1,2,128,128]{4,3,2,1,0:T(8,128)(2,1)S(1)} %get-tuple-element.35), channel_id=1, source_target_pairs={{0,2},{1,3},{2,0},{3,1},{4,6},{5,7},{6,4},{7,5},{8,10},{9,11},{10,... | collective-permute-start | bytes 393224 | tf_op jit(solution)/shard_map/ppermute | solution.py:231
  2.4 13.2 %collective-permute-start.11 = (bf16[2,1,2,128,128]{4,3,2,1,0:T(8,128)(2,1)S(1)}, bf16[2,1,2,128,128]{4,3,2,1,0:T(8,128)(2,1)S(1)}, u32[]{:S(2)}, u32[]{:S(2)}) collective-permute-start(bf16[2,1,2,128,128]{4,3,2,1,0:T(8,128)(2,1)S(1)} %get-tuple-element.35), channel_id=1, source_target_pairs={{0,3},{1,2},{2,1},{3,0},{4,7},{5,6},{6,5},{7,4},{8,11},{9,10},{10,... | collective-permute-start | bytes 393224 | tf_op jit(solution)/shard_map/ppermute | solution.py:231
  6.2 15.0 %collective-permute-start.2 = (bf16[2,1,2,128,128]{4,3,2,1,0:T(8,128)(2,1)S(1)}, bf16[2,1,2,128,128]{4,3,2,1,0:T(8,128)(2,1)S(1)}, u32[]{:S(2)}, u32[]{:S(2)}) collective-permute-start(bf16[2,1,2,128,128]{4,3,2,1,0:T(8,128)(2,1)S(1)} %get-tuple-element.38), channel_id=1, source_target_pairs={{0,2},{1,3},{2,0},{3,1},{4,6},{5,7},{6,4},{7,5},{8,10},{9,11},{10,... | collective-permute-start | bytes 393224 | tf_op jit(solution)/shard_map/ppermute | solution.py:231
  6.7 14.5 %collective-permute-start.4 = (bf16[2,1,2,128,128]{4,3,2,1,0:T(8,128)(2,1)S(1)}, bf16[2,1,2,128,128]{4,3,2,1,0:T(8,128)(2,1)S(1)}, u32[]{:S(2)}, u32[]{:S(2)}) collective-permute-start(bf16[2,1,2,128,128]{4,3,2,1,0:T(8,128)(2,1)S(1)} %get-tuple-element.38), channel_id=1, source_target_pairs={{0,3},{1,2},{2,1},{3,0},{4,7},{5,6},{6,5},{7,4},{8,11},{9,10},{10,... | collective-permute-start | bytes 393224 | tf_op jit(solution)/shard_map/ppermute | solution.py:231
  7.5 8.0 %collective-permute-start.10 = (bf16[2,1,2,128,128]{4,3,2,1,0:T(8,128)(2,1)S(1)}, bf16[2,1,2,128,128]{4,3,2,1,0:T(8,128)(2,1)S(1)}, u32[]{:S(2)}, u32[]{:S(2)}) collective-permute-start(bf16[2,1,2,128,128]{4,3,2,1,0:T(8,128)(2,1)S(1)} %get-tuple-element.34.refs_0_), channel_id=1, source_target_pairs={{0,1},{1,0},{2,3},{3,2},{4,5},{5,4},{6,7},{7,6},{8,9},{9,8},{10,11... | collective-permute-start | bytes 393224 | tf_op jit(solution)/shard_map/ppermute | solution.py:231
  9.1 12.1 %collective-permute-start.3 = (bf16[2,1,2,128,128]{4,3,2,1,0:T(8,128)(2,1)S(1)}, bf16[2,1,2,128,128]{4,3,2,1,0:T(8,128)(2,1)S(1)}, u32[]{:S(2)}, u32[]{:S(2)}) collective-permute-start(bf16[2,1,2,128,128]{4,3,2,1,0:T(8,128)(2,1)S(1)} %get-tuple-element.37.refs_0_), channel_id=1, source_target_pairs={{0,1},{1,0},{2,3},{3,2},{4,5},{5,4},{6,7},{7,6},{8,9},{9,8},{10,11... | collective-permute-start | bytes 393224 | tf_op jit(solution)/shard_map/ppermute | solution.py:231
  17.0 15.1 %collective-permute-start.12 = (bf16[2,256,128]{2,1,0:T(8,128)(2,1)S(1)}, bf16[2,256,128]{2,1,0:T(8,128)(2,1)S(1)}, u32[]{:S(2)}, u32[]{:S(2)}) collective-permute-start(bf16[2,256,128]{2,1,0:T(8,128)(2,1)S(1)} %get-tuple-element.50), channel_id=1, source_target_pairs={{0,16},{1,17},{2,18},{3,19},{4,20},{5,21},{6,22},{7,23},{8,24},{9,... | collective-permute-start | bytes 393224 | tf_op jit(solution)/shard_map/ppermute | solution.py:231
  19.6 17.7 %copy-start.1 = (bf16[256,2,128]{2,1,0:T(2,128)(2,1)S(1)}, bf16[256,2,128]{2,1,0:T(2,128)(2,1)}, u32[]{:S(2)}) copy-start(bf16[256,2,128]{2,1,0:T(2,128)(2,1)} %param.10) | copy-start | bytes 393220
  19.6 17.7 %copy-start.3 = (bf16[64,64]{1,0:T(8,128)(2,1)S(1)}, bf16[64,64]{1,0:T(8,128)(2,1)}, u32[]{:S(2)}) copy-start(bf16[64,64]{1,0:T(8,128)(2,1)} %ham_ref.1) | copy-start | bytes 24580
  19.6 12.4 %collective-permute-start.13 = (bf16[2,256,128]{2,1,0:T(8,128)(2,1)S(1)}, bf16[2,256,128]{2,1,0:T(8,128)(2,1)S(1)}, u32[]{:S(2)}, u32[]{:S(2)}) collective-permute-start(bf16[2,256,128]{2,1,0:T(8,128)(2,1)S(1)} %get-tuple-element.51), channel_id=1, source_target_pairs={{0,8},{1,9},{2,10},{3,11},{4,12},{5,13},{6,14},{7,15},{8,0},{9,1},... | collective-permute-start | bytes 393224 | tf_op jit(solution)/shard_map/ppermute | solution.py:231
  22.0 11.7 %collective-permute-start.6 = (bf16[2,256,128]{2,1,0:T(8,128)(2,1)S(1)}, bf16[2,256,128]{2,1,0:T(8,128)(2,1)S(1)}, u32[]{:S(2)}, u32[]{:S(2)}) collective-permute-start(bf16[2,256,128]{2,1,0:T(8,128)(2,1)S(1)} %get-tuple-element.43), channel_id=1, source_target_pairs={{0,4},{1,5},{2,6},{3,7},{4,0},{5,1},{6,2},{7,3},{8,12},{9,13},{10,... | collective-permute-start | bytes 393224 | tf_op jit(solution)/shard_map/ppermute | solution.py:231
  23.5 12.9 %collective-permute-start.5 = (bf16[2,256,128]{2,1,0:T(8,128)(2,1)S(1)}, bf16[2,256,128]{2,1,0:T(8,128)(2,1)S(1)}, u32[]{:S(2)}, u32[]{:S(2)}) collective-permute-start(bf16[2,256,128]{2,1,0:T(8,128)(2,1)S(1)} %get-tuple-element.40), channel_id=1, source_target_pairs={{0,4},{1,5},{2,6},{3,7},{4,0},{5,1},{6,2},{7,3},{8,12},{9,13},{10,... | collective-permute-start | bytes 393224 | tf_op jit(solution)/shard_map/ppermute | solution.py:231
  24.0 6.6 %collective-permute-start.15 = (bf16[1,256,128]{2,1,0:T(8,128)(2,1)S(1)}, bf16[1,256,128]{2,1,0:T(8,128)(2,1)S(1)}, u32[]{:S(2)}, u32[]{:S(2)}) collective-permute-start(bf16[1,256,128]{2,1,0:T(8,128)(2,1)S(1)} %get-tuple-element.55), channel_id=1, source_target_pairs={{0,4},{1,5},{2,6},{3,7},{4,0},{5,1},{6,2},{7,3},{8,12},{9,13},{10,... | collective-permute-start | bytes 196616 | tf_op jit(solution)/shard_map/ppermute | solution.py:231
  30.7 7.2 %collective-permute-start.16 = (bf16[1,256,128]{2,1,0:T(8,128)(2,1)S(1)}, bf16[1,256,128]{2,1,0:T(8,128)(2,1)S(1)}, u32[]{:S(2)}, u32[]{:S(2)}) collective-permute-start(bf16[1,256,128]{2,1,0:T(8,128)(2,1)S(1)} %shard_map.104), channel_id=1, source_target_pairs={{0,24},{1,25},{2,26},{3,27},{4,28},{5,29},{6,30},{7,31},{8,16},{9,... | collective-permute-start | bytes 196616 | tf_op jit(solution)/shard_map/ppermute | solution.py:231
  32.1 5.8 %collective-permute-start.14 = (bf16[1,256,128]{2,1,0:T(8,128)(2,1)S(1)}, bf16[1,256,128]{2,1,0:T(8,128)(2,1)S(1)}, u32[]{:S(2)}, u32[]{:S(2)}) collective-permute-start(bf16[1,256,128]{2,1,0:T(8,128)(2,1)S(1)} %get-tuple-element.53), channel_id=1, source_target_pairs={{0,4},{1,5},{2,6},{3,7},{4,0},{5,1},{6,2},{7,3},{8,12},{9,13},{10,... | collective-permute-start | bytes 196616 | tf_op jit(solution)/shard_map/ppermute | solution.py:231
  33.7 6.9 %collective-permute-start.7 = (bf16[1,256,128]{2,1,0:T(8,128)(2,1)S(1)}, bf16[1,256,128]{2,1,0:T(8,128)(2,1)S(1)}, u32[]{:S(2)}, u32[]{:S(2)}) collective-permute-start(bf16[1,256,128]{2,1,0:T(8,128)(2,1)S(1)} %get-tuple-element.44), channel_id=1, source_target_pairs={{0,16},{1,17},{2,18},{3,19},{4,20},{5,21},{6,22},{7,23},{8,24},{9,... | collective-permute-start | bytes 196616 | tf_op jit(solution)/shard_map/ppermute | solution.py:231
  34.4 6.2 %collective-permute-start.8 = (bf16[1,256,128]{2,1,0:T(8,128)(2,1)S(1)}, bf16[1,256,128]{2,1,0:T(8,128)(2,1)S(1)}, u32[]{:S(2)}, u32[]{:S(2)}) collective-permute-start(bf16[1,256,128]{2,1,0:T(8,128)(2,1)S(1)} %get-tuple-element.45), channel_id=1, source_target_pairs={{0,24},{1,25},{2,26},{3,27},{4,28},{5,29},{6,30},{7,31},{8,16},{9,... | collective-permute-start | bytes 196616 | tf_op jit(solution)/shard_map/ppermute | solution.py:231
  36.4 4.9 %collective-permute-start.9 = (bf16[1,256,128]{2,1,0:T(8,128)(2,1)S(1)}, bf16[1,256,128]{2,1,0:T(8,128)(2,1)S(1)}, u32[]{:S(2)}, u32[]{:S(2)}) collective-permute-start(bf16[1,256,128]{2,1,0:T(8,128)(2,1)S(1)} %get-tuple-element.46), channel_id=1, source_target_pairs={{0,8},{1,9},{2,10},{3,11},{4,12},{5,13},{6,14},{7,15},{8,0},{9,1},... | collective-permute-start | bytes 196616 | tf_op jit(solution)/shard_map/ppermute | solution.py:231

commit v6 on v5

--- a/solution.py
+++ b/solution.py
@@ -14,6 +14,7 @@
 
 
 time_step = 0.02
+CUTS = {2: (1,), 4: (2,)}
 F32 = jnp.float32
 BF16 = jnp.bfloat16
 
@@ -181,23 +182,42 @@
         base_ref[tile] = values.astype(F32) + time_step * turned
 
 
-def last_body(c, n_got, consts_ref, base_ref, keep_ref, *refs):
-    gots = refs[:n_got]
-    rows_out, sigma_out, rows_ref, sigma_ref, sems = refs[-5:]
-    size = rows_ref.shape[0]
-    here = pl.ds(c * size, size)
+def advanced(base, keep_ref, gots):
     collision = keep_ref[...]
     for got in gots:
         collision = collision + got[...].astype(F32)
-    collision = collision.reshape(rows_ref.shape)
-    rows_ref[...] = (base_ref[here] + time_step * collision).astype(BF16)
-    rows_copy = pltpu.make_async_copy(rows_ref, rows_out.at[here], sems.at[0])
-    rows_copy.start()
-    sigma_ref[...] = sigma_tiles(rows_ref[...], tuple(consts_ref[at] for at in range(4))).astype(BF16)
-    sigma_copy = pltpu.make_async_copy(sigma_ref, sigma_out.at[here], sems.at[1])
-    sigma_copy.start()
-    rows_copy.wait()
-    sigma_copy.wait()
+    return (base + time_step * collision.reshape(base.shape)).astype(BF16)
+
+
+def new_sigma_of(rows, consts_ref):
+    return sigma_tiles(rows, tuple(consts_ref[at] for at in range(4))).astype(BF16)
+
+
+def finish_body(c, consts_ref, base_ref, keep_ref, *refs):
+    gots, (rows_ref, sigma_ref) = refs[:-2], refs[-2:]
+    size = rows_ref.shape[0]
+    rows = advanced(base_ref[c * size:(c + 1) * size], keep_ref, gots)
+    rows_ref[...] = rows
+    sigma_ref[...] = new_sigma_of(rows, consts_ref)
+
+
+def last_body(n_done, consts_ref, base_ref, keep_ref, *refs):
+    finished, gots = refs[:2 * n_done], refs[2 * n_done:-5]
+    rows_out, sigma_out, rows_ref, sigma_ref, sems = refs[-5:]
+    size = rows_ref.shape[0]
+
+    def copy(source, at):
+        return pltpu.make_async_copy(source, (rows_out, sigma_out)[at % 2].at[pl.ds(at // 2 * size, size)], sems.at[at])
+
+    copies = [copy(source, at) for at, source in enumerate((*finished, rows_ref, sigma_ref))]
+    for at in range(2 * n_done):
+        copies[at].start()
+    rows_ref[...] = advanced(base_ref[n_done * size:], keep_ref, gots)
+    copies[-2].start()
+    sigma_ref[...] = new_sigma_of(rows_ref[...], consts_ref)
+    copies[-1].start()
+    for started in copies:
+        started.wait()
 
 
 def step_masks(count):
@@ -213,7 +233,7 @@
     return steps
 
 
-def block_places(steps, parts):
+def block_places(steps, cuts):
     def spread(rest):
         if not rest:
             return [0]
@@ -221,8 +241,12 @@
         return [mask ^ block for mask in rest[0] for block in inner]
 
     inner = spread(steps[1:])
-    size = len(inner) // parts
-    return {mask ^ block: (place // size * len(steps[0]) + to, place % size) for to, mask in enumerate(steps[0]) for place, block in enumerate(inner)}
+    places = {}
+    for part, (start, stop) in enumerate(cuts):
+        for to, mask in enumerate(steps[0]):
+            for place in range(start, stop):
+                places[mask ^ inner[place]] = (part * len(steps[0]) + to, place - start)
+    return places
 
 
 def exchange(value, mem_mask, hist_mask):
@@ -290,7 +314,12 @@
         steps = step_masks(pairs)
         if c < chunks - 1:
             steps = steps[1:] + steps[:1]
-        parts = 2 if c == chunks - 1 and len(steps) > 1 else 1
+        count = pairs // len(steps[0])
+        cuts = [(0, count)]
+        if c == chunks - 1 and len(steps) > 1:
+            ends = [0, *CUTS[len(steps[1])], len(steps[1])]
+            each = count // len(steps[1])
+            cuts = [(start * each, stop * each) for start, stop in zip(ends, ends[1:])]
         height = part * rows
         done = list(sigmas) if c == 0 else [mine[c], partner[c]]
         late = []
@@ -299,7 +328,6 @@
                 late = [same_core[c], cross[c]]
             else:
                 done += [same_core[c], cross[c]]
-        count = pairs // len(steps[0]) // parts
 
         def pieces(masks, count):
             return [shape((count, height, lanes), BF16 if mask else F32) for mask in masks]
@@ -327,38 +355,38 @@
             received.append([exchange(send, 2 * last, 0), got_far])
             continue
 
-        outs = term(block_places(steps, parts), pieces(steps[0], count) * parts)
+        outs = term(block_places(steps, cuts), [piece for start, stop in cuts for piece in pieces(steps[0], stop - start)])
         size = len(steps[0])
-        state = [(outs[p * size:(p + 1) * size - 1], outs[(p + 1) * size - 1]) for p in range(parts)]
+        state = [(outs[p * size:(p + 1) * size - 1], outs[(p + 1) * size - 1]) for p in range(len(cuts))]
         for at, masks in enumerate(steps):
             gots = [[exchange(sends[i], 2 * masks[i], 0) for i in range(len(sends))] for sends, _ in state]
             if at + 1 == len(steps):
                 break
             after = steps[at + 1]
-            share = len(after) // len(state)
-            count = count * len(state) // len(after)
+            count //= len(after)
             outs = []
             for p, (_, keep) in enumerate(state):
-                outs += call(functools.partial(add_body, len(gots[p])), pieces(after[p * share:(p + 1) * share], count), keep, *gots[p])
+                start, stop = (cut // count for cut in cuts[p])
+                outs += call(functools.partial(add_body, len(gots[p])), pieces(after[start:stop], count), keep, *gots[p])
+            cuts = [(0, count)]
             state = [(outs[:-1], outs[-1])]
         keeps.append(state[0][1])
         received.append(gots[0])
 
     base = call(base_body, shape((own_tiles, rows, lanes), F32), hamiltonian, panel_tiles)
-    anywhere = pl.BlockSpec(memory_space=pl.ANY)
-    result = []
-    for c in range(chunks):
-        given = [consts, base, keeps[c], *received[c]]
-        result = call(
-            functools.partial(last_body, c, len(received[c])),
-            [shape((own_tiles, rows, lanes), BF16)] * 2,
-            *given, *result,
-            in_specs=[vmem] * len(given) + [anywhere] * len(result),
-            out_specs=[anywhere] * 2,
-            input_output_aliases={len(given) + at: at for at in range(len(result))},
-            scratch_shapes=[pltpu.VMEM((part, rows, lanes), BF16)] * 2 + [pltpu.SemaphoreType.DMA((2,))],
-        )
-    new_rows, new_sigma = result
+    finished = []
+    done_piece = [shape((part, rows, lanes), BF16)] * 2
+    for c in range(chunks - 1):
+        finished += call(functools.partial(finish_body, c), done_piece, consts, base, keeps[c], *received[c])
+    given = [consts, base, keeps[-1], *finished, *received[-1]]
+    new_rows, new_sigma = call(
+        functools.partial(last_body, chunks - 1),
+        [shape((own_tiles, rows, lanes), BF16)] * 2,
+        *given,
+        in_specs=[vmem] * len(given),
+        out_specs=[pl.BlockSpec(memory_space=pl.ANY)] * 2,
+        scratch_shapes=[pltpu.VMEM((part, rows, lanes), BF16)] * 2 + [pltpu.SemaphoreType.DMA((2 * chunks,))],
+    )
     return new_rows.reshape(panel_rows.shape), new_sigma.reshape(panel_rows.shape)
 
 

time: 42.6 us -> 43 us (level)
  waiting for transfers between devices: 12 us -> 12.8 us
  Pallas kernels: 7.53 us -> 6.91 us
  local copies, waits for them, and re-layouts: 1.06 us -> 1.67 us
    ppermute x17, waiting for transfers between devices: 12 us -> 12.8 us  [exchange(): return lax.ppermute(value, ('mem', 'hist'), pairs)]
    pallas_call x12, Pallas kernels: 7.53 us -> 6.91 us  [call(): pl.pallas_call(body, out_shape=outs, cost_estimate=pl.CostEstimate(flops=...]
    unnamed x14, local copies, waits for them, and re-layouts: 1.06 us -> 1.67 us
    ppermute x17, starting transfers between devices: 20.4 us -> 20 us  [exchange(): return lax.ppermute(value, ('mem', 'hist'), pairs)]
  transfers between devices with their start and end apart: 17 -> 17, of which waited for: 4 -> 5; matrix products, arithmetic and copies ran while one was open for 0% -> 0% of each run, Pallas kernels for 15% -> 14%
where the time goes in v6:
time: 43 us; the launch traced here: 42.8 us
  starting transfers between devices  20 us (47%)
  waiting for transfers between devices  12.8 us (30%)
  Pallas kernels  6.91 us (16%)
  local copies, waits for them, and re-layouts  1.67 us (4%)
  between operations  1.42 us (3%)
    ppermute x17, starting transfers between devices, exchange(): return lax.ppermute(value, ('mem', 'hist'), pairs)  20 us
    ppermute x17, waiting for transfers between devices, exchange(): return lax.ppermute(value, ('mem', 'hist'), pairs)  12.8 us
    pallas_call x12, Pallas kernels, call(): pl.pallas_call(body, out_shape=outs, cost_estimate=pl.CostEstimate(flops=...  6.91 us
    unnamed x14, local copies, waits for them, and re-layouts  1.67 us
  transfers between devices with their start and end apart: 17, of which 5 were waited for; matrix products, arithmetic and copies ran while one was open for 0% of the time, Pallas kernels for 14%

profile of v6, /device:TPU:0, one launch (start us, length us, event | category | flops | bytes accessed | tf_op | source)
XLA Modules:
  0.0 42.8 jit_solution(5339611145179427740)
XLA Ops:
  0.6 0.6 %collective-permute-start = (bf16[4,8,64,128]{3,2,1,0:T(8,128)(2,1)}, bf16[4,8,64,128]{3,2,1,0:T(8,128)(2,1)S(1)}, u32[]{:S(2)}, u32[]{:S(2)}) collective-permute-start(bf16[4,8,64,128]{3,2,1,0:T(8,128)(2,1)} %block_ref.1), channel_id=1, source_target_pairs={{0,2},{1,3},{2,0},{3,1},{4,6},{5,7},{6,4},{7,5},{8,10},{9,11},{10,... | collective-permute-start | bytes 1572872 | tf_op jit(solution)/shard_map/ppermute | solution.py:255
  1.2 1.0 %copy-done.5 = bf16[1024,2,128]{2,1,0:T(2,128)(2,1)S(1)} copy-done((bf16[1024,2,128]{2,1,0:T(2,128)(2,1)S(1)}, bf16[1024,2,128]{2,1,0:T(2,128)(2,1)}, u32[]{:S(2)}) %copy-start.5) | copy-done | bytes 524312
  2.3 0.1 collective-permute-start.1
  2.4 0.6 %copy-done.2 = f32[64,64]{1,0:T(8,128)S(1)} copy-done((f32[64,64]{1,0:T(8,128)S(1)}, f32[64,64]{1,0:T(8,128)}, u32[]{:S(2)}) %copy-start.2) | copy-done | bytes 16408
  3.0 1.1 %shard_map.96 = (bf16[4,128,128]{2,1,0:T(8,128)(2,1)S(1)}, bf16[2,1,2,128,128]{4,3,2,1,0:T(8,128)(2,1)S(1)}, bf16[2,1,2,128,128]{4,3,2,1,0:T(8,128)(2,1)S(1)}) custom-call(f32[64,64]{1,0:T(8,128)S(1)} %copy-done.2, bf16[2,1,2,128,128]{4,3,2,1,0:T(8,128)(2,1)S(1)} %get-tuple-element.31.refs_0_, bf16[2,1,2,128,128]{4,3,2,1,0:T(8,128)(2,1)S(1)} %get-tuple-element.32.refs_1_), custom_call_target="tpu_custom_call" | custom-call | bytes 671744 | tf_op jit(solution)/shard_map/pallas_call | solution.py:53
  4.1 0.1 collective-permute-start.2
  4.2 2.7 %collective-permute-start.4 = (bf16[2,1,2,128,128]{4,3,2,1,0:T(8,128)(2,1)S(1)}, bf16[2,1,2,128,128]{4,3,2,1,0:T(8,128)(2,1)S(1)}, u32[]{:S(2)}, u32[]{:S(2)}) collective-permute-start(bf16[2,1,2,128,128]{4,3,2,1,0:T(8,128)(2,1)S(1)} %get-tuple-element.38), channel_id=1, source_target_pairs={{0,3},{1,2},{2,1},{3,0},{4,7},{5,6},{6,5},{7,4},{8,11},{9,10},{10,... | collective-permute-start | bytes 393224 | tf_op jit(solution)/shard_map/ppermute | solution.py:255
  6.9 0.1 collective-permute-start.7
  7.6 0.0 collective-permute-done.1.refs_1_
  7.6 2.0 %collective-permute-start.3 = (bf16[2,1,2,128,128]{4,3,2,1,0:T(8,128)(2,1)S(1)}, bf16[2,1,2,128,128]{4,3,2,1,0:T(8,128)(2,1)S(1)}, u32[]{:S(2)}, u32[]{:S(2)}) collective-permute-start(bf16[2,1,2,128,128]{4,3,2,1,0:T(8,128)(2,1)S(1)} %get-tuple-element.37.refs_0_), channel_id=1, source_target_pairs={{0,1},{1,0},{2,3},{3,2},{4,5},{5,4},{6,7},{7,6},{8,9},{9,8},{10,11... | collective-permute-start | bytes 393224 | tf_op jit(solution)/shard_map/ppermute | solution.py:255
  9.7 0.0 collective-permute-done.other_ref
  9.7 0.1 collective-permute-start.6
  9.7 0.0 copy-done.6
  9.8 0.0 copy-done
  9.8 0.0 copy-done.4
  9.8 1.4 %shard_map.98 = (bf16[1024,1024]{1,0:T(8,128)(2,1)S(1)}, bf16[2,1,2,128,128]{4,3,2,1,0:T(8,128)(2,1)S(1)}, bf16[2,1,2,128,128]{4,3,2,1,0:T(8,128)(2,1)S(1)}) custom-call(s32[64]{0:T(128)S(1)} %compare_select_fusion.deal_ref, s32[16]{0:T(128)S(1)} %copy-done.4, bf16[4,128,128]{2,1,0:T(8,128)(2,1)S(1)} %get-tuple-element.33.consts_ref, ...), custom_call_target="tpu_custom_call" | custom-call | bytes 3801408 | tf_op jit(solution)/shard_map/pallas_call | solution.py:53
  11.2 0.0 collective-permute-done.2.refs_1_
  11.2 6.0 %collective-permute-done.3.refs_2_ = bf16[2,1,2,128,128]{4,3,2,1,0:T(8,128)(2,1)S(1)} collective-permute-done((bf16[2,1,2,128,128]{4,3,2,1,0:T(8,128)(2,1)S(1)}, bf16[2,1,2,128,128]{4,3,2,1,0:T(8,128)(2,1)S(1)}, u32[]{:S(2)}, u32[]{:S(2)}) %collective-permute-start.3) | collective-permute-done | bytes 131104 | tf_op jit(solution)/shard_map/ppermute | solution.py:255
  17.1 0.0 collective-permute-done.4.refs_3_
  17.1 0.7 %shard_map.99 = (bf16[2,256,128]{2,1,0:T(8,128)(2,1)S(1)}, f32[2,256,128]{2,1,0:T(8,128)S(1)}, bf16[2,256,128]{2,1,0:T(8,128)(2,1)S(1)}, f32[2,256,128]{2,1,0:T(8,128)S(1)}) custom-call(bf16[4,128,128]{2,1,0:T(8,128)(2,1)S(1)} %get-tuple-element.33.consts_ref, bf16[1024,1024]{1,0:T(8,128)(2,1)S(1)} %get-tuple-element.36.weights_ref, ...), custom_call_target="tpu_custom_call" | custom-call | flops 536870912 | bytes 3538944 | tf_op jit(solution)/shard_map/pallas_call | solution.py:53
  17.9 1.7 %collective-permute-start.13 = (bf16[2,256,128]{2,1,0:T(8,128)(2,1)S(1)}, bf16[2,256,128]{2,1,0:T(8,128)(2,1)S(1)}, u32[]{:S(2)}, u32[]{:S(2)}) collective-permute-start(bf16[2,256,128]{2,1,0:T(8,128)(2,1)S(1)} %get-tuple-element.54), channel_id=1, source_target_pairs={{0,4},{1,5},{2,6},{3,7},{4,0},{5,1},{6,2},{7,3},{8,12},{9,13},{10,... | collective-permute-start | bytes 393224 | tf_op jit(solution)/shard_map/ppermute | solution.py:255
  19.6 0.0 collective-permute-done.6.refs_2_
  19.6 0.0 collective-permute-done.7.refs_3_
  19.6 0.0 copy-start.3
  19.7 1.4 %shard_map.101 = (bf16[2,256,128]{2,1,0:T(8,128)(2,1)S(1)}, bf16[1,256,128]{2,1,0:T(8,128)(2,1)S(1)}, f32[1,256,128]{2,1,0:T(8,128)S(1)}, bf16[2,256,128]{2,1,0:T(8,128)(2,1)S(1)}, f32[2,256,128]{2,1,0:T(8,128)S(1)}) custom-call(bf16[4,128,128]{2,1,0:T(8,128)(2,1)S(1)} %get-tuple-element.33.consts_ref, bf16[1024,1024]{1,0:T(8,128)(2,1)S(1)} %get-tuple-element.36.weights_ref, ...), custom_call_target="tpu_custom_call" | custom-call | flops 536870912 | bytes 3473408 | tf_op jit(solution)/shard_map/pallas_call | solution.py:53
  21.1 2.9 %collective-permute-start.8 = (bf16[2,256,128]{2,1,0:T(8,128)(2,1)S(1)}, bf16[2,256,128]{2,1,0:T(8,128)(2,1)S(1)}, u32[]{:S(2)}, u32[]{:S(2)}) collective-permute-start(bf16[2,256,128]{2,1,0:T(8,128)(2,1)S(1)} %get-tuple-element.45), channel_id=1, source_target_pairs={{0,16},{1,17},{2,18},{3,19},{4,20},{5,21},{6,22},{7,23},{8,24},{9,... | collective-permute-start | bytes 393224 | tf_op jit(solution)/shard_map/ppermute | solution.py:255
  24.0 1.6 %collective-permute-start.9 = (bf16[2,256,128]{2,1,0:T(8,128)(2,1)S(1)}, bf16[2,256,128]{2,1,0:T(8,128)(2,1)S(1)}, u32[]{:S(2)}, u32[]{:S(2)}) collective-permute-start(bf16[2,256,128]{2,1,0:T(8,128)(2,1)S(1)} %get-tuple-element.46), channel_id=1, source_target_pairs={{0,8},{1,9},{2,10},{3,11},{4,12},{5,13},{6,14},{7,15},{8,0},{9,1},... | collective-permute-start | bytes 393224 | tf_op jit(solution)/shard_map/ppermute | solution.py:255
  25.6 1.5 %collective-permute-start.5 = (bf16[2,256,128]{2,1,0:T(8,128)(2,1)S(1)}, bf16[2,256,128]{2,1,0:T(8,128)(2,1)S(1)}, u32[]{:S(2)}, u32[]{:S(2)}) collective-permute-start(bf16[2,256,128]{2,1,0:T(8,128)(2,1)S(1)} %get-tuple-element.40), channel_id=1, source_target_pairs={{0,4},{1,5},{2,6},{3,7},{4,0},{5,1},{6,2},{7,3},{8,12},{9,13},{10,... | collective-permute-start | bytes 393224 | tf_op jit(solution)/shard_map/ppermute | solution.py:255
  27.0 0.5 %collective-permute-start.11 = (bf16[1,256,128]{2,1,0:T(8,128)(2,1)S(1)}, bf16[1,256,128]{2,1,0:T(8,128)(2,1)S(1)}, u32[]{:S(2)}, u32[]{:S(2)}) collective-permute-start(bf16[1,256,128]{2,1,0:T(8,128)(2,1)S(1)} %get-tuple-element.50), channel_id=1, source_target_pairs={{0,4},{1,5},{2,6},{3,7},{4,0},{5,1},{6,2},{7,3},{8,12},{9,13},{10,... | collective-permute-start | bytes 196616 | tf_op jit(solution)/shard_map/ppermute | solution.py:255
  27.6 4.1 %collective-permute-done.11.refs_0_ = bf16[1,256,128]{2,1,0:T(8,128)(2,1)S(1)} collective-permute-done((bf16[1,256,128]{2,1,0:T(8,128)(2,1)S(1)}, bf16[1,256,128]{2,1,0:T(8,128)(2,1)S(1)}, u32[]{:S(2)}, u32[]{:S(2)}) %collective-permute-start.11) | collective-permute-done | bytes 65568 | tf_op jit(solution)/shard_map/ppermute | solution.py:255
  31.7 0.3 collective-permute-start.12
  32.0 0.0 collective-permute-done.13.refs_0_
  32.0 1.7 %collective-permute-start.14 = (bf16[1,256,128]{2,1,0:T(8,128)(2,1)S(1)}, bf16[1,256,128]{2,1,0:T(8,128)(2,1)S(1)}, u32[]{:S(2)}, u32[]{:S(2)}) collective-permute-start(bf16[1,256,128]{2,1,0:T(8,128)(2,1)S(1)} %get-tuple-element.55), channel_id=1, source_target_pairs={{0,16},{1,17},{2,18},{3,19},{4,20},{5,21},{6,22},{7,23},{8,24},{9,... | collective-permute-start | bytes 196616 | tf_op jit(solution)/shard_map/ppermute | solution.py:255
  33.8 0.0 collective-permute-done.8.refs_0_
  33.8 2.0 %collective-permute-start.15 = (bf16[1,256,128]{2,1,0:T(8,128)(2,1)S(1)}, bf16[1,256,128]{2,1,0:T(8,128)(2,1)S(1)}, u32[]{:S(2)}, u32[]{:S(2)}) collective-permute-start(bf16[1,256,128]{2,1,0:T(8,128)(2,1)S(1)} %get-tuple-element.56), channel_id=1, source_target_pairs={{0,24},{1,25},{2,26},{3,27},{4,28},{5,29},{6,30},{7,31},{8,16},{9,... | collective-permute-start | bytes 196616 | tf_op jit(solution)/shard_map/ppermute | solution.py:255
  35.8 0.0 collective-permute-done.9.refs_1_
  35.8 1.6 %collective-permute-start.10 = (bf16[1,256,128]{2,1,0:T(8,128)(2,1)S(1)}, bf16[1,256,128]{2,1,0:T(8,128)(2,1)S(1)}, u32[]{:S(2)}, u32[]{:S(2)}) collective-permute-start(bf16[1,256,128]{2,1,0:T(8,128)(2,1)S(1)} %get-tuple-element.48), channel_id=1, source_target_pairs={{0,4},{1,5},{2,6},{3,7},{4,0},{5,1},{6,2},{7,3},{8,12},{9,13},{10,... | collective-permute-start | bytes 196616 | tf_op jit(solution)/shard_map/ppermute | solution.py:255
  37.4 0.0 collective-permute-done.5.refs_0_
  37.4 0.6 %collective-permute-start.16 = (bf16[1,256,128]{2,1,0:T(8,128)(2,1)S(1)}, bf16[1,256,128]{2,1,0:T(8,128)(2,1)S(1)}, u32[]{:S(2)}, u32[]{:S(2)}) collective-permute-start(bf16[1,256,128]{2,1,0:T(8,128)(2,1)S(1)} %get-tuple-element.57), channel_id=1, source_target_pairs={{0,8},{1,9},{2,10},{3,11},{4,12},{5,13},{6,14},{7,15},{8,0},{9,1},... | collective-permute-start | bytes 196616 | tf_op jit(solution)/shard_map/ppermute | solution.py:255
  37.9 0.0 copy-done.1
  37.9 0.5 %shard_map.97.base_ref = f32[4,128,128]{2,1,0:T(8,128)S(1)} custom-call(bf16[64,64]{1,0:T(8,128)(2,1)S(1)} %copy-done.3, bf16[4,128,128]{2,1,0:T(8,128)(2,1)S(1)} %bitcast.6), custom_call_target="tpu_custom_call" | custom-call | bytes 401408 | tf_op jit(solution)/shard_map/pallas_call | solution.py:53
  38.5 0.0 collective-permute-done.12.refs_1_
  38.5 1.7 %collective-permute-done.10.refs_0_ = bf16[1,256,128]{2,1,0:T(8,128)(2,1)S(1)} collective-permute-done((bf16[1,256,128]{2,1,0:T(8,128)(2,1)S(1)}, bf16[1,256,128]{2,1,0:T(8,128)(2,1)S(1)}, u32[]{:S(2)}, u32[]{:S(2)}) %collective-permute-start.10) | collective-permute-done | bytes 65568 | tf_op jit(solution)/shard_map/ppermute | solution.py:255
  40.1 0.5 %shard_map.104 = (bf16[2,128,128]{2,1,0:T(8,128)(2,1)S(1)}, bf16[2,128,128]{2,1,0:T(8,128)(2,1)S(1)}) custom-call(bf16[4,128,128]{2,1,0:T(8,128)(2,1)S(1)} %get-tuple-element.33.consts_ref, f32[4,128,128]{2,1,0:T(8,128)S(1)} %shard_map.97.base_ref, f32[1,256,128]{2,1,0:T(8,128)S(1)} %get-tuple-element.47.keep_ref, ...), custom_call_target="tpu_custom_call" | custom-call | bytes 786432 | tf_op jit(solution)/shard_map/pallas_call | solution.py:53
  40.6 0.4 collective-permute-done.14.refs_2_
  41.0 0.0 collective-permute-done.15.refs_3_
  41.0 0.7 %collective-permute-done.16.refs_4_ = bf16[1,256,128]{2,1,0:T(8,128)(2,1)S(1)} collective-permute-done((bf16[1,256,128]{2,1,0:T(8,128)(2,1)S(1)}, bf16[1,256,128]{2,1,0:T(8,128)(2,1)S(1)}, u32[]{:S(2)}, u32[]{:S(2)}) %collective-permute-start.16) | collective-permute-done | bytes 65568 | tf_op jit(solution)/shard_map/ppermute | solution.py:255
  41.7 1.1 %shard_map.106 = (bf16[4,128,128]{2,1,0:T(8,128)(2,1)}, bf16[4,128,128]{2,1,0:T(8,128)(2,1)}) custom-call(bf16[4,128,128]{2,1,0:T(8,128)(2,1)S(1)} %get-tuple-element.33.consts_ref, f32[4,128,128]{2,1,0:T(8,128)S(1)} %shard_map.97.base_ref, f32[1,256,128]{2,1,0:T(8,128)S(1)} %get-tuple-element.41.keep_ref, ...), custom_call_target="tpu_custom_call" | custom-call | bytes 1114112 | tf_op jit(solution)/shard_map/pallas_call | solution.py:53
  (13 shorter events, 0.2 us)
Async XLA Ops:
  0.6 9.0 %collective-permute-start = (bf16[4,8,64,128]{3,2,1,0:T(8,128)(2,1)}, bf16[4,8,64,128]{3,2,1,0:T(8,128)(2,1)S(1)}, u32[]{:S(2)}, u32[]{:S(2)}) collective-permute-start(bf16[4,8,64,128]{3,2,1,0:T(8,128)(2,1)} %block_ref.1), channel_id=1, source_target_pairs={{0,2},{1,3},{2,0},{3,1},{4,6},{5,7},{6,4},{7,5},{8,10},{9,11},{10,... | collective-permute-start | bytes 1572872 | tf_op jit(solution)/shard_map/ppermute | solution.py:255
  1.2 1.0 %copy-start.5 = (bf16[1024,2,128]{2,1,0:T(2,128)(2,1)S(1)}, bf16[1024,2,128]{2,1,0:T(2,128)(2,1)}, u32[]{:S(2)}) copy-start(bf16[1024,2,128]{2,1,0:T(2,128)(2,1)} %param.9) | copy-start | bytes 1572868
  2.2 0.8 %copy-start.2 = (f32[64,64]{1,0:T(8,128)S(1)}, f32[64,64]{1,0:T(8,128)}, u32[]{:S(2)}) copy-start(f32[64,64]{1,0:T(8,128)} %coupling_ref.1) | copy-start | bytes 49156
  2.2 7.5 %copy-start.6 = (s32[64]{0:T(128)S(1)}, s32[64]{0:T(128)}, u32[]{:S(2)}) copy-start(s32[64]{0:T(128)} %param.11) | copy-start | bytes 772
  2.2 7.5 %copy-start = (bf16[4,8,64,128]{3,2,1,0:T(8,128)(2,1)S(1)}, bf16[4,8,64,128]{3,2,1,0:T(8,128)(2,1)}, u32[]{:S(2)}) copy-start(bf16[4,8,64,128]{3,2,1,0:T(8,128)(2,1)} %block_ref.1) | copy-start | bytes 1572868
  2.2 7.5 %copy-start.4 = (s32[16]{0:T(128)S(1)}, s32[16]{0:T(128)}, u32[]{:S(2)}) copy-start(s32[16]{0:T(128)} %columns_ref.1) | copy-start | bytes 196
  2.3 5.3 %collective-permute-start.1 = (bf16[2,1,2,128,128]{4,3,2,1,0:T(8,128)(2,1)S(1)}, bf16[2,1,2,128,128]{4,3,2,1,0:T(8,128)(2,1)S(1)}, u32[]{:S(2)}, u32[]{:S(2)}) collective-permute-start(bf16[2,1,2,128,128]{4,3,2,1,0:T(8,128)(2,1)S(1)} %get-tuple-element.35), channel_id=1, source_target_pairs={{0,2},{1,3},{2,0},{3,1},{4,6},{5,7},{6,4},{7,5},{8,10},{9,11},{10,... | collective-permute-start | bytes 393224 | tf_op jit(solution)/shard_map/ppermute | solution.py:255
  4.1 7.1 %collective-permute-start.2 = (bf16[2,1,2,128,128]{4,3,2,1,0:T(8,128)(2,1)S(1)}, bf16[2,1,2,128,128]{4,3,2,1,0:T(8,128)(2,1)S(1)}, u32[]{:S(2)}, u32[]{:S(2)}) collective-permute-start(bf16[2,1,2,128,128]{4,3,2,1,0:T(8,128)(2,1)S(1)} %get-tuple-element.38), channel_id=1, source_target_pairs={{0,2},{1,3},{2,0},{3,1},{4,6},{5,7},{6,4},{7,5},{8,10},{9,11},{10,... | collective-permute-start | bytes 393224 | tf_op jit(solution)/shard_map/ppermute | solution.py:255
  4.2 13.0 %collective-permute-start.4 = (bf16[2,1,2,128,128]{4,3,2,1,0:T(8,128)(2,1)S(1)}, bf16[2,1,2,128,128]{4,3,2,1,0:T(8,128)(2,1)S(1)}, u32[]{:S(2)}, u32[]{:S(2)}) collective-permute-start(bf16[2,1,2,128,128]{4,3,2,1,0:T(8,128)(2,1)S(1)} %get-tuple-element.38), channel_id=1, source_target_pairs={{0,3},{1,2},{2,1},{3,0},{4,7},{5,6},{6,5},{7,4},{8,11},{9,10},{10,... | collective-permute-start | bytes 393224 | tf_op jit(solution)/shard_map/ppermute | solution.py:255
  6.9 12.8 %collective-permute-start.7 = (bf16[2,1,2,128,128]{4,3,2,1,0:T(8,128)(2,1)S(1)}, bf16[2,1,2,128,128]{4,3,2,1,0:T(8,128)(2,1)S(1)}, u32[]{:S(2)}, u32[]{:S(2)}) collective-permute-start(bf16[2,1,2,128,128]{4,3,2,1,0:T(8,128)(2,1)S(1)} %get-tuple-element.35), channel_id=1, source_target_pairs={{0,3},{1,2},{2,1},{3,0},{4,7},{5,6},{6,5},{7,4},{8,11},{9,10},{10,... | collective-permute-start | bytes 393224 | tf_op jit(solution)/shard_map/ppermute | solution.py:255
  7.6 9.5 %collective-permute-start.3 = (bf16[2,1,2,128,128]{4,3,2,1,0:T(8,128)(2,1)S(1)}, bf16[2,1,2,128,128]{4,3,2,1,0:T(8,128)(2,1)S(1)}, u32[]{:S(2)}, u32[]{:S(2)}) collective-permute-start(bf16[2,1,2,128,128]{4,3,2,1,0:T(8,128)(2,1)S(1)} %get-tuple-element.37.refs_0_), channel_id=1, source_target_pairs={{0,1},{1,0},{2,3},{3,2},{4,5},{5,4},{6,7},{7,6},{8,9},{9,8},{10,11... | collective-permute-start | bytes 393224 | tf_op jit(solution)/shard_map/ppermute | solution.py:255
  9.7 10.0 %collective-permute-start.6 = (bf16[2,1,2,128,128]{4,3,2,1,0:T(8,128)(2,1)S(1)}, bf16[2,1,2,128,128]{4,3,2,1,0:T(8,128)(2,1)S(1)}, u32[]{:S(2)}, u32[]{:S(2)}) collective-permute-start(bf16[2,1,2,128,128]{4,3,2,1,0:T(8,128)(2,1)S(1)} %get-tuple-element.34.refs_0_), channel_id=1, source_target_pairs={{0,1},{1,0},{2,3},{3,2},{4,5},{5,4},{6,7},{7,6},{8,9},{9,8},{10,11... | collective-permute-start | bytes 393224 | tf_op jit(solution)/shard_map/ppermute | solution.py:255
  17.9 14.1 %collective-permute-start.13 = (bf16[2,256,128]{2,1,0:T(8,128)(2,1)S(1)}, bf16[2,256,128]{2,1,0:T(8,128)(2,1)S(1)}, u32[]{:S(2)}, u32[]{:S(2)}) collective-permute-start(bf16[2,256,128]{2,1,0:T(8,128)(2,1)S(1)} %get-tuple-element.54), channel_id=1, source_target_pairs={{0,4},{1,5},{2,6},{3,7},{4,0},{5,1},{6,2},{7,3},{8,12},{9,13},{10,... | collective-permute-start | bytes 393224 | tf_op jit(solution)/shard_map/ppermute | solution.py:255
  19.6 18.3 %copy-start.1 = (bf16[256,2,128]{2,1,0:T(2,128)(2,1)S(1)}, bf16[256,2,128]{2,1,0:T(2,128)(2,1)}, u32[]{:S(2)}) copy-start(bf16[256,2,128]{2,1,0:T(2,128)(2,1)} %param.10) | copy-start | bytes 393220
  19.6 18.3 %copy-start.3 = (bf16[64,64]{1,0:T(8,128)(2,1)S(1)}, bf16[64,64]{1,0:T(8,128)(2,1)}, u32[]{:S(2)}) copy-start(bf16[64,64]{1,0:T(8,128)(2,1)} %ham_ref.1) | copy-start | bytes 24580
  21.1 12.7 %collective-permute-start.8 = (bf16[2,256,128]{2,1,0:T(8,128)(2,1)S(1)}, bf16[2,256,128]{2,1,0:T(8,128)(2,1)S(1)}, u32[]{:S(2)}, u32[]{:S(2)}) collective-permute-start(bf16[2,256,128]{2,1,0:T(8,128)(2,1)S(1)} %get-tuple-element.45), channel_id=1, source_target_pairs={{0,16},{1,17},{2,18},{3,19},{4,20},{5,21},{6,22},{7,23},{8,24},{9,... | collective-permute-start | bytes 393224 | tf_op jit(solution)/shard_map/ppermute | solution.py:255
  24.0 11.8 %collective-permute-start.9 = (bf16[2,256,128]{2,1,0:T(8,128)(2,1)S(1)}, bf16[2,256,128]{2,1,0:T(8,128)(2,1)S(1)}, u32[]{:S(2)}, u32[]{:S(2)}) collective-permute-start(bf16[2,256,128]{2,1,0:T(8,128)(2,1)S(1)} %get-tuple-element.46), channel_id=1, source_target_pairs={{0,8},{1,9},{2,10},{3,11},{4,12},{5,13},{6,14},{7,15},{8,0},{9,1},... | collective-permute-start | bytes 393224 | tf_op jit(solution)/shard_map/ppermute | solution.py:255
  25.6 11.8 %collective-permute-start.5 = (bf16[2,256,128]{2,1,0:T(8,128)(2,1)S(1)}, bf16[2,256,128]{2,1,0:T(8,128)(2,1)S(1)}, u32[]{:S(2)}, u32[]{:S(2)}) collective-permute-start(bf16[2,256,128]{2,1,0:T(8,128)(2,1)S(1)} %get-tuple-element.40), channel_id=1, source_target_pairs={{0,4},{1,5},{2,6},{3,7},{4,0},{5,1},{6,2},{7,3},{8,12},{9,13},{10,... | collective-permute-start | bytes 393224 | tf_op jit(solution)/shard_map/ppermute | solution.py:255
  27.0 4.6 %collective-permute-start.11 = (bf16[1,256,128]{2,1,0:T(8,128)(2,1)S(1)}, bf16[1,256,128]{2,1,0:T(8,128)(2,1)S(1)}, u32[]{:S(2)}, u32[]{:S(2)}) collective-permute-start(bf16[1,256,128]{2,1,0:T(8,128)(2,1)S(1)} %get-tuple-element.50), channel_id=1, source_target_pairs={{0,4},{1,5},{2,6},{3,7},{4,0},{5,1},{6,2},{7,3},{8,12},{9,13},{10,... | collective-permute-start | bytes 196616 | tf_op jit(solution)/shard_map/ppermute | solution.py:255
  31.7 6.8 %collective-permute-start.12 = (bf16[1,256,128]{2,1,0:T(8,128)(2,1)S(1)}, bf16[1,256,128]{2,1,0:T(8,128)(2,1)S(1)}, u32[]{:S(2)}, u32[]{:S(2)}) collective-permute-start(bf16[1,256,128]{2,1,0:T(8,128)(2,1)S(1)} %shard_map.103), channel_id=1, source_target_pairs={{0,24},{1,25},{2,26},{3,27},{4,28},{5,29},{6,30},{7,31},{8,16},{9,... | collective-permute-start | bytes 196616 | tf_op jit(solution)/shard_map/ppermute | solution.py:255
  32.0 9.0 %collective-permute-start.14 = (bf16[1,256,128]{2,1,0:T(8,128)(2,1)S(1)}, bf16[1,256,128]{2,1,0:T(8,128)(2,1)S(1)}, u32[]{:S(2)}, u32[]{:S(2)}) collective-permute-start(bf16[1,256,128]{2,1,0:T(8,128)(2,1)S(1)} %get-tuple-element.55), channel_id=1, source_target_pairs={{0,16},{1,17},{2,18},{3,19},{4,20},{5,21},{6,22},{7,23},{8,24},{9,... | collective-permute-start | bytes 196616 | tf_op jit(solution)/shard_map/ppermute | solution.py:255
  33.8 7.3 %collective-permute-start.15 = (bf16[1,256,128]{2,1,0:T(8,128)(2,1)S(1)}, bf16[1,256,128]{2,1,0:T(8,128)(2,1)S(1)}, u32[]{:S(2)}, u32[]{:S(2)}) collective-permute-start(bf16[1,256,128]{2,1,0:T(8,128)(2,1)S(1)} %get-tuple-element.56), channel_id=1, source_target_pairs={{0,24},{1,25},{2,26},{3,27},{4,28},{5,29},{6,30},{7,31},{8,16},{9,... | collective-permute-start | bytes 196616 | tf_op jit(solution)/shard_map/ppermute | solution.py:255
  35.8 4.3 %collective-permute-start.10 = (bf16[1,256,128]{2,1,0:T(8,128)(2,1)S(1)}, bf16[1,256,128]{2,1,0:T(8,128)(2,1)S(1)}, u32[]{:S(2)}, u32[]{:S(2)}) collective-permute-start(bf16[1,256,128]{2,1,0:T(8,128)(2,1)S(1)} %get-tuple-element.48), channel_id=1, source_target_pairs={{0,4},{1,5},{2,6},{3,7},{4,0},{5,1},{6,2},{7,3},{8,12},{9,13},{10,... | collective-permute-start | bytes 196616 | tf_op jit(solution)/shard_map/ppermute | solution.py:255
  37.4 4.3 %collective-permute-start.16 = (bf16[1,256,128]{2,1,0:T(8,128)(2,1)S(1)}, bf16[1,256,128]{2,1,0:T(8,128)(2,1)S(1)}, u32[]{:S(2)}, u32[]{:S(2)}) collective-permute-start(bf16[1,256,128]{2,1,0:T(8,128)(2,1)S(1)} %get-tuple-element.57), channel_id=1, source_target_pairs={{0,8},{1,9},{2,10},{3,11},{4,12},{5,13},{6,14},{7,15},{8,0},{9,1},... | collective-permute-start | bytes 196616 | tf_op jit(solution)/shard_map/ppermute | solution.py:255

commit v7 on v6

--- a/solution.py
+++ b/solution.py
@@ -14,7 +14,7 @@
 
 
 time_step = 0.02
-CUTS = {2: (1,), 4: (2,)}
+CUTS = {2: (1,), 4: (1, 2)}
 F32 = jnp.float32
 BF16 = jnp.bfloat16
 
@@ -135,7 +135,8 @@
             weights_ref[q * lanes + orbitals:(q + 1) * lanes, apart * lanes:(apart + 1) * lanes] = lower.astype(BF16)
 
 
-def term_body(n_done, n_late, places, groups, consts_ref, weights_ref, *refs):
+def term_body(n_done, n_late, places, groups, skipped, consts_ref, weights_ref, *refs):
+    begun, refs = refs[:bool(skipped)], refs[bool(skipped):]
     done, late = refs[:n_done], refs[n_done:n_done + n_late]
     outs, left_ref = refs[n_done + n_late:-1], refs[-1]
     pair = lax.axis_index("mem") >> 1
@@ -153,12 +154,25 @@
             for s in range(count):
                 left_ref[:, q * lanes:(q + 1) * lanes] = tiles[s].reshape(rows, lanes)
                 q += 1
-        total = dot(left_ref[...], weights_ref[...])
+        total = dot(left_ref[...], weights_ref[skipped * lanes:])
+        if begun:
+            total = begun[0][...] + total
         for block, (to, place) in places.items():
             if block % groups == step:
                 apart = block // groups
                 value = total[:, apart * lanes:(apart + 1) * lanes]
                 outs[to][place] = value.astype(outs[to].dtype)
+
+
+def begin_body(weights_ref, *refs):
+    sources, begun_ref, left_ref = refs[:-2], refs[-2], refs[-1]
+    rows, lanes = begun_ref.shape[0], sources[0].shape[-1]
+    q = 0
+    for source in sources:
+        for s in range(source.shape[0]):
+            left_ref[:, q * lanes:(q + 1) * lanes] = source[s, 0].reshape(rows, lanes)
+            q += 1
+    begun_ref[...] = dot(left_ref[...], weights_ref[:q * lanes])
 
 
 def add_body(n_got, keep_ref, *refs):
@@ -322,10 +336,19 @@
             cuts = [(start * each, stop * each) for start, stop in zip(ends, ends[1:])]
         height = part * rows
         done = list(sigmas) if c == 0 else [mine[c], partner[c]]
-        late = []
+        late, begun, skipped = [], [], 0
         if two_hist:
             if c == 0:
                 late = [same_core[c], cross[c]]
+            elif groups == 1:
+                skipped = sum(source.shape[0] for source in done)
+                begun = [call(
+                    begin_body,
+                    shape((height, columns * lanes), F32),
+                    weights, *done,
+                    scratch_shapes=[pltpu.VMEM((height, skipped * lanes), BF16)],
+                )]
+                done = [same_core[c], cross[c]]
             else:
                 done += [same_core[c], cross[c]]
 
@@ -334,11 +357,11 @@
 
         def term(places, outs):
             return call(
-                functools.partial(term_body, len(done), len(late), places, groups),
+                functools.partial(term_body, len(done), len(late), places, groups, skipped),
                 outs,
-                consts, weights, *done, *late,
+                consts, weights, *begun, *done, *late,
                 flops=2 * height * groups * 2 * slots * lanes * columns * lanes,
-                scratch_shapes=[pltpu.VMEM((height, 2 * slots * lanes), BF16)],
+                scratch_shapes=[pltpu.VMEM((height, (2 * slots - skipped) * lanes), BF16)],
             )
 
         if c < chunks - 1 and len(steps) == 2 and len(steps[0]) == 4:

time: 43 us -> 44.3 us (1.030)
  waiting for transfers between devices: 12.8 us -> 15 us
  starting transfers between devices: 20 us -> 18.9 us
    ppermute x17 -> x18, waiting for transfers between devices: 12.8 us -> 15 us  [exchange(): return lax.ppermute(value, ('mem', 'hist'), pairs)]
    ppermute x17 -> x18, starting transfers between devices: 20 us -> 18.9 us  [exchange(): return lax.ppermute(value, ('mem', 'hist'), pairs)]
    pallas_call x12 -> x14, Pallas kernels: 6.91 us -> 7.03 us  [call(): pl.pallas_call(body, out_shape=outs, cost_estimate=pl.CostEstimate(flops=...]
  transfers between devices with their start and end apart: 17 -> 18, of which waited for: 5 -> 6; matrix products, arithmetic and copies ran while one was open for 0% -> 0% of each run, Pallas kernels for 14% -> 13%
where the time goes in v7:
time: 44.3 us; the launch traced here: 44.1 us
  starting transfers between devices  18.9 us (43%)
  waiting for transfers between devices  15 us (34%)
  Pallas kernels  7.03 us (16%)
  local copies, waits for them, and re-layouts  1.67 us (4%)
  between operations  1.45 us (3%)
    ppermute x18, starting transfers between devices, exchange(): return lax.ppermute(value, ('mem', 'hist'), pairs)  18.9 us
    ppermute x18, waiting for transfers between devices, exchange(): return lax.ppermute(value, ('mem', 'hist'), pairs)  15 us
    pallas_call x14, Pallas kernels, call(): pl.pallas_call(body, out_shape=outs, cost_estimate=pl.CostEstimate(flops=...  7.03 us
    unnamed x14, local copies, waits for them, and re-layouts  1.67 us
  transfers between devices with their start and end apart: 18, of which 6 were waited for; matrix products, arithmetic and copies ran while one was open for 0% of the time, Pallas kernels for 13%

profile of v7, /device:TPU:0, one launch (start us, length us, event | category | flops | bytes accessed | tf_op | source)
XLA Modules:
  0.0 44.1 jit_solution(7940445672345214575)
XLA Ops:
  0.6 0.6 %collective-permute-start = (bf16[4,8,64,128]{3,2,1,0:T(8,128)(2,1)}, bf16[4,8,64,128]{3,2,1,0:T(8,128)(2,1)S(1)}, u32[]{:S(2)}, u32[]{:S(2)}) collective-permute-start(bf16[4,8,64,128]{3,2,1,0:T(8,128)(2,1)} %block_ref.1), channel_id=1, source_target_pairs={{0,2},{1,3},{2,0},{3,1},{4,6},{5,7},{6,4},{7,5},{8,10},{9,11},{10,... | collective-permute-start | bytes 1572872 | tf_op jit(solution)/shard_map/ppermute | solution.py:269
  1.2 1.0 %copy-done.5 = bf16[1024,2,128]{2,1,0:T(2,128)(2,1)S(1)} copy-done((bf16[1024,2,128]{2,1,0:T(2,128)(2,1)S(1)}, bf16[1024,2,128]{2,1,0:T(2,128)(2,1)}, u32[]{:S(2)}) %copy-start.5) | copy-done | bytes 524312
  2.3 0.1 collective-permute-start.1
  2.4 0.6 %copy-done.2 = f32[64,64]{1,0:T(8,128)S(1)} copy-done((f32[64,64]{1,0:T(8,128)S(1)}, f32[64,64]{1,0:T(8,128)}, u32[]{:S(2)}) %copy-start.2) | copy-done | bytes 16408
  3.0 1.1 %shard_map.96 = (bf16[4,128,128]{2,1,0:T(8,128)(2,1)S(1)}, bf16[2,1,2,128,128]{4,3,2,1,0:T(8,128)(2,1)S(1)}, bf16[2,1,2,128,128]{4,3,2,1,0:T(8,128)(2,1)S(1)}) custom-call(f32[64,64]{1,0:T(8,128)S(1)} %copy-done.2, bf16[2,1,2,128,128]{4,3,2,1,0:T(8,128)(2,1)S(1)} %get-tuple-element.31.refs_0_, bf16[2,1,2,128,128]{4,3,2,1,0:T(8,128)(2,1)S(1)} %get-tuple-element.32.refs_1_), custom_call_target="tpu_custom_call" | custom-call | bytes 671744 | tf_op jit(solution)/shard_map/pallas_call | solution.py:53
  4.1 2.7 %collective-permute-start.4 = (bf16[2,1,2,128,128]{4,3,2,1,0:T(8,128)(2,1)S(1)}, bf16[2,1,2,128,128]{4,3,2,1,0:T(8,128)(2,1)S(1)}, u32[]{:S(2)}, u32[]{:S(2)}) collective-permute-start(bf16[2,1,2,128,128]{4,3,2,1,0:T(8,128)(2,1)S(1)} %get-tuple-element.38), channel_id=1, source_target_pairs={{0,3},{1,2},{2,1},{3,0},{4,7},{5,6},{6,5},{7,4},{8,11},{9,10},{10,... | collective-permute-start | bytes 393224 | tf_op jit(solution)/shard_map/ppermute | solution.py:269
  6.8 0.0 collective-permute-start.2
  6.8 0.1 collective-permute-start.7
  7.6 0.0 collective-permute-done.1.refs_1_
  7.6 2.0 %collective-permute-start.3 = (bf16[2,1,2,128,128]{4,3,2,1,0:T(8,128)(2,1)S(1)}, bf16[2,1,2,128,128]{4,3,2,1,0:T(8,128)(2,1)S(1)}, u32[]{:S(2)}, u32[]{:S(2)}) collective-permute-start(bf16[2,1,2,128,128]{4,3,2,1,0:T(8,128)(2,1)S(1)} %get-tuple-element.37.refs_0_), channel_id=1, source_target_pairs={{0,1},{1,0},{2,3},{3,2},{4,5},{5,4},{6,7},{7,6},{8,9},{9,8},{10,11... | collective-permute-start | bytes 393224 | tf_op jit(solution)/shard_map/ppermute | solution.py:269
  9.7 0.0 collective-permute-done.other_ref
  9.7 0.1 collective-permute-start.6
  9.8 1.4 %shard_map.98 = (bf16[1024,1024]{1,0:T(8,128)(2,1)S(1)}, bf16[2,1,2,128,128]{4,3,2,1,0:T(8,128)(2,1)S(1)}, bf16[2,1,2,128,128]{4,3,2,1,0:T(8,128)(2,1)S(1)}) custom-call(s32[64]{0:T(128)S(1)} %compare_select_fusion.deal_ref, s32[16]{0:T(128)S(1)} %copy-done.4, bf16[4,128,128]{2,1,0:T(8,128)(2,1)S(1)} %get-tuple-element.33.consts_ref, ...), custom_call_target="tpu_custom_call" | custom-call | bytes 3801408 | tf_op jit(solution)/shard_map/pallas_call | solution.py:53
  11.2 8.1 %collective-permute-done.6.refs_2_ = bf16[2,1,2,128,128]{4,3,2,1,0:T(8,128)(2,1)S(1)} collective-permute-done((bf16[2,1,2,128,128]{4,3,2,1,0:T(8,128)(2,1)S(1)}, bf16[2,1,2,128,128]{4,3,2,1,0:T(8,128)(2,1)S(1)}, u32[]{:S(2)}, u32[]{:S(2)}) %collective-permute-start.6) | collective-permute-done | bytes 131104 | tf_op jit(solution)/shard_map/ppermute | solution.py:269
  19.3 0.0 collective-permute-done.7.refs_3_
  19.3 1.4 %shard_map.102 = (bf16[2,256,128]{2,1,0:T(8,128)(2,1)S(1)}, bf16[1,256,128]{2,1,0:T(8,128)(2,1)S(1)}, f32[1,256,128]{2,1,0:T(8,128)S(1)}, bf16[2,256,128]{2,1,0:T(8,128)(2,1)S(1)}, f32[2,256,128]{2,1,0:T(8,128)S(1)}) custom-call(bf16[4,128,128]{2,1,0:T(8,128)(2,1)S(1)} %get-tuple-element.33.consts_ref, bf16[1024,1024]{1,0:T(8,128)(2,1)S(1)} %get-tuple-element.36.weights_ref, ...), custom_call_target="tpu_custom_call" | custom-call | flops 536870912 | bytes 3473408 | tf_op jit(solution)/shard_map/pallas_call | solution.py:53
  20.7 1.7 %collective-permute-start.11 = (bf16[1,256,128]{2,1,0:T(8,128)(2,1)S(1)}, bf16[1,256,128]{2,1,0:T(8,128)(2,1)S(1)}, u32[]{:S(2)}, u32[]{:S(2)}) collective-permute-start(bf16[1,256,128]{2,1,0:T(8,128)(2,1)S(1)} %get-tuple-element.50), channel_id=1, source_target_pairs={{0,4},{1,5},{2,6},{3,7},{4,0},{5,1},{6,2},{7,3},{8,12},{9,13},{10,... | collective-permute-start | bytes 196616 | tf_op jit(solution)/shard_map/ppermute | solution.py:269
  22.4 2.6 %collective-permute-start.8 = (bf16[2,256,128]{2,1,0:T(8,128)(2,1)S(1)}, bf16[2,256,128]{2,1,0:T(8,128)(2,1)S(1)}, u32[]{:S(2)}, u32[]{:S(2)}) collective-permute-start(bf16[2,256,128]{2,1,0:T(8,128)(2,1)S(1)} %get-tuple-element.45), channel_id=1, source_target_pairs={{0,16},{1,17},{2,18},{3,19},{4,20},{5,21},{6,22},{7,23},{8,24},{9,... | collective-permute-start | bytes 393224 | tf_op jit(solution)/shard_map/ppermute | solution.py:269
  24.9 0.0 collective-permute-done.2.refs_1_
  24.9 1.6 %collective-permute-start.9 = (bf16[2,256,128]{2,1,0:T(8,128)(2,1)S(1)}, bf16[2,256,128]{2,1,0:T(8,128)(2,1)S(1)}, u32[]{:S(2)}, u32[]{:S(2)}) collective-permute-start(bf16[2,256,128]{2,1,0:T(8,128)(2,1)S(1)} %get-tuple-element.46), channel_id=1, source_target_pairs={{0,8},{1,9},{2,10},{3,11},{4,12},{5,13},{6,14},{7,15},{8,0},{9,1},... | collective-permute-start | bytes 393224 | tf_op jit(solution)/shard_map/ppermute | solution.py:269
  26.5 0.4 shard_map.99.refs_0_
  27.0 0.0 copy-start.1
  27.0 0.0 copy-start.3
  27.0 0.0 collective-permute-done.3.refs_1_
  27.0 0.0 collective-permute-done.4.refs_2_
  27.0 0.4 %shard_map.100 = (bf16[1,256,128]{2,1,0:T(8,128)(2,1)S(1)}, f32[1,256,128]{2,1,0:T(8,128)S(1)}, bf16[1,256,128]{2,1,0:T(8,128)(2,1)S(1)}, f32[1,256,128]{2,1,0:T...) custom-call(bf16[4,128,128]{2,1,0:T(8,128)(2,1)S(1)} %get-tuple-element.33.consts_ref, ...), custom_call_target="tpu_custom_call" | custom-call | flops 536870912 | bytes 4325376 | tf_op jit(solution)/shard_map/pallas_call | solution.py:53
  27.5 0.6 %collective-permute-start.5 = (bf16[2,256,128]{2,1,0:T(8,128)(2,1)S(1)}, bf16[2,256,128]{2,1,0:T(8,128)(2,1)S(1)}, u32[]{:S(2)}, u32[]{:S(2)}) collective-permute-start(bf16[2,256,128]{2,1,0:T(8,128)(2,1)S(1)} %get-tuple-element.40), channel_id=1, source_target_pairs={{0,4},{1,5},{2,6},{3,7},{4,0},{5,1},{6,2},{7,3},{8,12},{9,13},{10,... | collective-permute-start | bytes 393224 | tf_op jit(solution)/shard_map/ppermute | solution.py:269
  28.1 1.5 %collective-permute-start.13 = (bf16[1,256,128]{2,1,0:T(8,128)(2,1)S(1)}, bf16[1,256,128]{2,1,0:T(8,128)(2,1)S(1)}, u32[]{:S(2)}, u32[]{:S(2)}) collective-permute-start(bf16[1,256,128]{2,1,0:T(8,128)(2,1)S(1)} %get-tuple-element.54), channel_id=1, source_target_pairs={{0,4},{1,5},{2,6},{3,7},{4,0},{5,1},{6,2},{7,3},{8,12},{9,13},{10,... | collective-permute-start | bytes 196616 | tf_op jit(solution)/shard_map/ppermute | solution.py:269
  29.6 0.0 collective-permute-done.11.refs_0_
  29.6 0.5 %collective-permute-start.15 = (bf16[1,256,128]{2,1,0:T(8,128)(2,1)S(1)}, bf16[1,256,128]{2,1,0:T(8,128)(2,1)S(1)}, u32[]{:S(2)}, u32[]{:S(2)}) collective-permute-start(bf16[1,256,128]{2,1,0:T(8,128)(2,1)S(1)} %get-tuple-element.56), channel_id=1, source_target_pairs={{0,4},{1,5},{2,6},{3,7},{4,0},{5,1},{6,2},{7,3},{8,12},{9,13},{10,... | collective-permute-start | bytes 196616 | tf_op jit(solution)/shard_map/ppermute | solution.py:269
  30.1 3.5 %collective-permute-done.13.refs_0_ = bf16[1,256,128]{2,1,0:T(8,128)(2,1)S(1)} collective-permute-done((bf16[1,256,128]{2,1,0:T(8,128)(2,1)S(1)}, bf16[1,256,128]{2,1,0:T(8,128)(2,1)S(1)}, u32[]{:S(2)}, u32[]{:S(2)}) %collective-permute-start.13) | collective-permute-done | bytes 65568 | tf_op jit(solution)/shard_map/ppermute | solution.py:269
  33.6 0.2 collective-permute-start.12
  33.9 0.5 %collective-permute-done.15.refs_0_ = bf16[1,256,128]{2,1,0:T(8,128)(2,1)S(1)} collective-permute-done((bf16[1,256,128]{2,1,0:T(8,128)(2,1)S(1)}, bf16[1,256,128]{2,1,0:T(8,128)(2,1)S(1)}, u32[]{:S(2)}, u32[]{:S(2)}) %collective-permute-start.15) | collective-permute-done | bytes 65568 | tf_op jit(solution)/shard_map/ppermute | solution.py:269
  34.3 1.3 %collective-permute-start.14 = (bf16[1,256,128]{2,1,0:T(8,128)(2,1)S(1)}, bf16[1,256,128]{2,1,0:T(8,128)(2,1)S(1)}, u32[]{:S(2)}, u32[]{:S(2)}) collective-permute-start(bf16[1,256,128]{2,1,0:T(8,128)(2,1)S(1)} %shard_map.106), channel_id=1, source_target_pairs={{0,16},{1,17},{2,18},{3,19},{4,20},{5,21},{6,22},{7,23},{8,24},{9,... | collective-permute-start | bytes 196616 | tf_op jit(solution)/shard_map/ppermute | solution.py:269
  35.7 0.0 collective-permute-done.8.refs_0_
  35.7 2.0 %collective-permute-start.16 = (bf16[1,256,128]{2,1,0:T(8,128)(2,1)S(1)}, bf16[1,256,128]{2,1,0:T(8,128)(2,1)S(1)}, u32[]{:S(2)}, u32[]{:S(2)}) collective-permute-start(bf16[1,256,128]{2,1,0:T(8,128)(2,1)S(1)} %shard_map.107), channel_id=1, source_target_pairs={{0,24},{1,25},{2,26},{3,27},{4,28},{5,29},{6,30},{7,31},{8,16},{9,... | collective-permute-start | bytes 196616 | tf_op jit(solution)/shard_map/ppermute | solution.py:269
  37.7 0.0 collective-permute-done.9.refs_1_
  37.7 0.6 %collective-permute-start.10 = (bf16[1,256,128]{2,1,0:T(8,128)(2,1)S(1)}, bf16[1,256,128]{2,1,0:T(8,128)(2,1)S(1)}, u32[]{:S(2)}, u32[]{:S(2)}) collective-permute-start(bf16[1,256,128]{2,1,0:T(8,128)(2,1)S(1)} %get-tuple-element.48), channel_id=1, source_target_pairs={{0,4},{1,5},{2,6},{3,7},{4,0},{5,1},{6,2},{7,3},{8,12},{9,13},{10,... | collective-permute-start | bytes 196616 | tf_op jit(solution)/shard_map/ppermute | solution.py:269
  38.3 0.0 collective-permute-done.5.refs_0_
  38.3 0.7 %collective-permute-start.17 = (bf16[1,256,128]{2,1,0:T(8,128)(2,1)S(1)}, bf16[1,256,128]{2,1,0:T(8,128)(2,1)S(1)}, u32[]{:S(2)}, u32[]{:S(2)}) collective-permute-start(bf16[1,256,128]{2,1,0:T(8,128)(2,1)S(1)} %get-tuple-element.57), channel_id=1, source_target_pairs={{0,8},{1,9},{2,10},{3,11},{4,12},{5,13},{6,14},{7,15},{8,0},{9,1},... | collective-permute-start | bytes 196616 | tf_op jit(solution)/shard_map/ppermute | solution.py:269
  39.0 0.5 %shard_map.97.base_ref = f32[4,128,128]{2,1,0:T(8,128)S(1)} custom-call(bf16[64,64]{1,0:T(8,128)(2,1)S(1)} %copy-done.3, bf16[4,128,128]{2,1,0:T(8,128)(2,1)S(1)} %bitcast.6), custom_call_target="tpu_custom_call" | custom-call | bytes 401408 | tf_op jit(solution)/shard_map/pallas_call | solution.py:53
  39.5 0.6 %collective-permute-done.12.refs_1_ = bf16[1,256,128]{2,1,0:T(8,128)(2,1)S(1)} collective-permute-done((bf16[1,256,128]{2,1,0:T(8,128)(2,1)S(1)}, bf16[1,256,128]{2,1,0:T(8,128)(2,1)S(1)}, u32[]{:S(2)}, u32[]{:S(2)}) %collective-permute-start.12) | collective-permute-done | bytes 65568 | tf_op jit(solution)/shard_map/ppermute | solution.py:269
  40.1 1.9 %collective-permute-done.10.refs_0_ = bf16[1,256,128]{2,1,0:T(8,128)(2,1)S(1)} collective-permute-done((bf16[1,256,128]{2,1,0:T(8,128)(2,1)S(1)}, bf16[1,256,128]{2,1,0:T(8,128)(2,1)S(1)}, u32[]{:S(2)}, u32[]{:S(2)}) %collective-permute-start.10) | collective-permute-done | bytes 65568 | tf_op jit(solution)/shard_map/ppermute | solution.py:269
  42.1 0.5 %shard_map.105 = (bf16[2,128,128]{2,1,0:T(8,128)(2,1)S(1)}, bf16[2,128,128]{2,1,0:T(8,128)(2,1)S(1)}) custom-call(bf16[4,128,128]{2,1,0:T(8,128)(2,1)S(1)} %get-tuple-element.33.consts_ref, f32[4,128,128]{2,1,0:T(8,128)S(1)} %shard_map.97.base_ref, f32[1,256,128]{2,1,0:T(8,128)S(1)} %get-tuple-element.47.keep_ref, ...), custom_call_target="tpu_custom_call" | custom-call | bytes 786432 | tf_op jit(solution)/shard_map/pallas_call | solution.py:53
  42.5 0.0 collective-permute-done.14.refs_2_
  42.5 0.0 collective-permute-done.16.refs_3_
  42.5 0.4 collective-permute-done.17.refs_4_
  42.9 1.1 %shard_map.108 = (bf16[4,128,128]{2,1,0:T(8,128)(2,1)}, bf16[4,128,128]{2,1,0:T(8,128)(2,1)}) custom-call(bf16[4,128,128]{2,1,0:T(8,128)(2,1)S(1)} %get-tuple-element.33.consts_ref, f32[4,128,128]{2,1,0:T(8,128)S(1)} %shard_map.97.base_ref, f32[1,256,128]{2,1,0:T(8,128)S(1)} %get-tuple-element.41.keep_ref, ...), custom_call_target="tpu_custom_call" | custom-call | bytes 1114112 | tf_op jit(solution)/shard_map/pallas_call | solution.py:53
  (17 shorter events, 0.2 us)
Async XLA Ops:
  0.6 9.0 %collective-permute-start = (bf16[4,8,64,128]{3,2,1,0:T(8,128)(2,1)}, bf16[4,8,64,128]{3,2,1,0:T(8,128)(2,1)S(1)}, u32[]{:S(2)}, u32[]{:S(2)}) collective-permute-start(bf16[4,8,64,128]{3,2,1,0:T(8,128)(2,1)} %block_ref.1), channel_id=1, source_target_pairs={{0,2},{1,3},{2,0},{3,1},{4,6},{5,7},{6,4},{7,5},{8,10},{9,11},{10,... | collective-permute-start | bytes 1572872 | tf_op jit(solution)/shard_map/ppermute | solution.py:269
  1.2 1.0 %copy-start.5 = (bf16[1024,2,128]{2,1,0:T(2,128)(2,1)S(1)}, bf16[1024,2,128]{2,1,0:T(2,128)(2,1)}, u32[]{:S(2)}) copy-start(bf16[1024,2,128]{2,1,0:T(2,128)(2,1)} %param.9) | copy-start | bytes 1572868
  2.2 0.8 %copy-start.2 = (f32[64,64]{1,0:T(8,128)S(1)}, f32[64,64]{1,0:T(8,128)}, u32[]{:S(2)}) copy-start(f32[64,64]{1,0:T(8,128)} %coupling_ref.1) | copy-start | bytes 49156
  2.2 7.5 %copy-start.6 = (s32[64]{0:T(128)S(1)}, s32[64]{0:T(128)}, u32[]{:S(2)}) copy-start(s32[64]{0:T(128)} %param.11) | copy-start | bytes 772
  2.2 7.5 %copy-start = (bf16[4,8,64,128]{3,2,1,0:T(8,128)(2,1)S(1)}, bf16[4,8,64,128]{3,2,1,0:T(8,128)(2,1)}, u32[]{:S(2)}) copy-start(bf16[4,8,64,128]{3,2,1,0:T(8,128)(2,1)} %block_ref.1) | copy-start | bytes 1572868
  2.2 7.5 %copy-start.4 = (s32[16]{0:T(128)S(1)}, s32[16]{0:T(128)}, u32[]{:S(2)}) copy-start(s32[16]{0:T(128)} %columns_ref.1) | copy-start | bytes 196
  2.3 5.3 %collective-permute-start.1 = (bf16[2,1,2,128,128]{4,3,2,1,0:T(8,128)(2,1)S(1)}, bf16[2,1,2,128,128]{4,3,2,1,0:T(8,128)(2,1)S(1)}, u32[]{:S(2)}, u32[]{:S(2)}) collective-permute-start(bf16[2,1,2,128,128]{4,3,2,1,0:T(8,128)(2,1)S(1)} %get-tuple-element.35), channel_id=1, source_target_pairs={{0,2},{1,3},{2,0},{3,1},{4,6},{5,7},{6,4},{7,5},{8,10},{9,11},{10,... | collective-permute-start | bytes 393224 | tf_op jit(solution)/shard_map/ppermute | solution.py:269
  4.1 22.9 %collective-permute-start.4 = (bf16[2,1,2,128,128]{4,3,2,1,0:T(8,128)(2,1)S(1)}, bf16[2,1,2,128,128]{4,3,2,1,0:T(8,128)(2,1)S(1)}, u32[]{:S(2)}, u32[]{:S(2)}) collective-permute-start(bf16[2,1,2,128,128]{4,3,2,1,0:T(8,128)(2,1)S(1)} %get-tuple-element.38), channel_id=1, source_target_pairs={{0,3},{1,2},{2,1},{3,0},{4,7},{5,6},{6,5},{7,4},{8,11},{9,10},{10,... | collective-permute-start | bytes 393224 | tf_op jit(solution)/shard_map/ppermute | solution.py:269
  6.8 18.2 %collective-permute-start.2 = (bf16[2,1,2,128,128]{4,3,2,1,0:T(8,128)(2,1)S(1)}, bf16[2,1,2,128,128]{4,3,2,1,0:T(8,128)(2,1)S(1)}, u32[]{:S(2)}, u32[]{:S(2)}) collective-permute-start(bf16[2,1,2,128,128]{4,3,2,1,0:T(8,128)(2,1)S(1)} %get-tuple-element.38), channel_id=1, source_target_pairs={{0,2},{1,3},{2,0},{3,1},{4,6},{5,7},{6,4},{7,5},{8,10},{9,11},{10,... | collective-permute-start | bytes 393224 | tf_op jit(solution)/shard_map/ppermute | solution.py:269
  6.8 12.5 %collective-permute-start.7 = (bf16[2,1,2,128,128]{4,3,2,1,0:T(8,128)(2,1)S(1)}, bf16[2,1,2,128,128]{4,3,2,1,0:T(8,128)(2,1)S(1)}, u32[]{:S(2)}, u32[]{:S(2)}) collective-permute-start(bf16[2,1,2,128,128]{4,3,2,1,0:T(8,128)(2,1)S(1)} %get-tuple-element.35), channel_id=1, source_target_pairs={{0,3},{1,2},{2,1},{3,0},{4,7},{5,6},{6,5},{7,4},{8,11},{9,10},{10,... | collective-permute-start | bytes 393224 | tf_op jit(solution)/shard_map/ppermute | solution.py:269
  7.6 19.4 %collective-permute-start.3 = (bf16[2,1,2,128,128]{4,3,2,1,0:T(8,128)(2,1)S(1)}, bf16[2,1,2,128,128]{4,3,2,1,0:T(8,128)(2,1)S(1)}, u32[]{:S(2)}, u32[]{:S(2)}) collective-permute-start(bf16[2,1,2,128,128]{4,3,2,1,0:T(8,128)(2,1)S(1)} %get-tuple-element.37.refs_0_), channel_id=1, source_target_pairs={{0,1},{1,0},{2,3},{3,2},{4,5},{5,4},{6,7},{7,6},{8,9},{9,8},{10,11... | collective-permute-start | bytes 393224 | tf_op jit(solution)/shard_map/ppermute | solution.py:269
  9.7 9.6 %collective-permute-start.6 = (bf16[2,1,2,128,128]{4,3,2,1,0:T(8,128)(2,1)S(1)}, bf16[2,1,2,128,128]{4,3,2,1,0:T(8,128)(2,1)S(1)}, u32[]{:S(2)}, u32[]{:S(2)}) collective-permute-start(bf16[2,1,2,128,128]{4,3,2,1,0:T(8,128)(2,1)S(1)} %get-tuple-element.34.refs_0_), channel_id=1, source_target_pairs={{0,1},{1,0},{2,3},{3,2},{4,5},{5,4},{6,7},{7,6},{8,9},{9,8},{10,11... | collective-permute-start | bytes 393224 | tf_op jit(solution)/shard_map/ppermute | solution.py:269
  20.7 8.9 %collective-permute-start.11 = (bf16[1,256,128]{2,1,0:T(8,128)(2,1)S(1)}, bf16[1,256,128]{2,1,0:T(8,128)(2,1)S(1)}, u32[]{:S(2)}, u32[]{:S(2)}) collective-permute-start(bf16[1,256,128]{2,1,0:T(8,128)(2,1)S(1)} %get-tuple-element.50), channel_id=1, source_target_pairs={{0,4},{1,5},{2,6},{3,7},{4,0},{5,1},{6,2},{7,3},{8,12},{9,13},{10,... | collective-permute-start | bytes 196616 | tf_op jit(solution)/shard_map/ppermute | solution.py:269
  22.4 13.3 %collective-permute-start.8 = (bf16[2,256,128]{2,1,0:T(8,128)(2,1)S(1)}, bf16[2,256,128]{2,1,0:T(8,128)(2,1)S(1)}, u32[]{:S(2)}, u32[]{:S(2)}) collective-permute-start(bf16[2,256,128]{2,1,0:T(8,128)(2,1)S(1)} %get-tuple-element.45), channel_id=1, source_target_pairs={{0,16},{1,17},{2,18},{3,19},{4,20},{5,21},{6,22},{7,23},{8,24},{9,... | collective-permute-start | bytes 393224 | tf_op jit(solution)/shard_map/ppermute | solution.py:269
  24.9 12.7 %collective-permute-start.9 = (bf16[2,256,128]{2,1,0:T(8,128)(2,1)S(1)}, bf16[2,256,128]{2,1,0:T(8,128)(2,1)S(1)}, u32[]{:S(2)}, u32[]{:S(2)}) collective-permute-start(bf16[2,256,128]{2,1,0:T(8,128)(2,1)S(1)} %get-tuple-element.46), channel_id=1, source_target_pairs={{0,8},{1,9},{2,10},{3,11},{4,12},{5,13},{6,14},{7,15},{8,0},{9,1},... | collective-permute-start | bytes 393224 | tf_op jit(solution)/shard_map/ppermute | solution.py:269
  27.0 12.1 %copy-start.1 = (bf16[256,2,128]{2,1,0:T(2,128)(2,1)S(1)}, bf16[256,2,128]{2,1,0:T(2,128)(2,1)}, u32[]{:S(2)}) copy-start(bf16[256,2,128]{2,1,0:T(2,128)(2,1)} %param.10) | copy-start | bytes 393220
  27.0 12.1 %copy-start.3 = (bf16[64,64]{1,0:T(8,128)(2,1)S(1)}, bf16[64,64]{1,0:T(8,128)(2,1)}, u32[]{:S(2)}) copy-start(bf16[64,64]{1,0:T(8,128)(2,1)} %ham_ref.1) | copy-start | bytes 24580
  27.5 10.8 %collective-permute-start.5 = (bf16[2,256,128]{2,1,0:T(8,128)(2,1)S(1)}, bf16[2,256,128]{2,1,0:T(8,128)(2,1)S(1)}, u32[]{:S(2)}, u32[]{:S(2)}) collective-permute-start(bf16[2,256,128]{2,1,0:T(8,128)(2,1)S(1)} %get-tuple-element.40), channel_id=1, source_target_pairs={{0,4},{1,5},{2,6},{3,7},{4,0},{5,1},{6,2},{7,3},{8,12},{9,13},{10,... | collective-permute-start | bytes 393224 | tf_op jit(solution)/shard_map/ppermute | solution.py:269
  28.1 5.6 %collective-permute-start.13 = (bf16[1,256,128]{2,1,0:T(8,128)(2,1)S(1)}, bf16[1,256,128]{2,1,0:T(8,128)(2,1)S(1)}, u32[]{:S(2)}, u32[]{:S(2)}) collective-permute-start(bf16[1,256,128]{2,1,0:T(8,128)(2,1)S(1)} %get-tuple-element.54), channel_id=1, source_target_pairs={{0,4},{1,5},{2,6},{3,7},{4,0},{5,1},{6,2},{7,3},{8,12},{9,13},{10,... | collective-permute-start | bytes 196616 | tf_op jit(solution)/shard_map/ppermute | solution.py:269
  29.6 4.8 %collective-permute-start.15 = (bf16[1,256,128]{2,1,0:T(8,128)(2,1)S(1)}, bf16[1,256,128]{2,1,0:T(8,128)(2,1)S(1)}, u32[]{:S(2)}, u32[]{:S(2)}) collective-permute-start(bf16[1,256,128]{2,1,0:T(8,128)(2,1)S(1)} %get-tuple-element.56), channel_id=1, source_target_pairs={{0,4},{1,5},{2,6},{3,7},{4,0},{5,1},{6,2},{7,3},{8,12},{9,13},{10,... | collective-permute-start | bytes 196616 | tf_op jit(solution)/shard_map/ppermute | solution.py:269
  33.6 6.5 %collective-permute-start.12 = (bf16[1,256,128]{2,1,0:T(8,128)(2,1)S(1)}, bf16[1,256,128]{2,1,0:T(8,128)(2,1)S(1)}, u32[]{:S(2)}, u32[]{:S(2)}) collective-permute-start(bf16[1,256,128]{2,1,0:T(8,128)(2,1)S(1)} %shard_map.104), channel_id=1, source_target_pairs={{0,24},{1,25},{2,26},{3,27},{4,28},{5,29},{6,30},{7,31},{8,16},{9,... | collective-permute-start | bytes 196616 | tf_op jit(solution)/shard_map/ppermute | solution.py:269
  34.3 8.2 %collective-permute-start.14 = (bf16[1,256,128]{2,1,0:T(8,128)(2,1)S(1)}, bf16[1,256,128]{2,1,0:T(8,128)(2,1)S(1)}, u32[]{:S(2)}, u32[]{:S(2)}) collective-permute-start(bf16[1,256,128]{2,1,0:T(8,128)(2,1)S(1)} %shard_map.106), channel_id=1, source_target_pairs={{0,16},{1,17},{2,18},{3,19},{4,20},{5,21},{6,22},{7,23},{8,24},{9,... | collective-permute-start | bytes 196616 | tf_op jit(solution)/shard_map/ppermute | solution.py:269
  35.7 6.9 %collective-permute-start.16 = (bf16[1,256,128]{2,1,0:T(8,128)(2,1)S(1)}, bf16[1,256,128]{2,1,0:T(8,128)(2,1)S(1)}, u32[]{:S(2)}, u32[]{:S(2)}) collective-permute-start(bf16[1,256,128]{2,1,0:T(8,128)(2,1)S(1)} %shard_map.107), channel_id=1, source_target_pairs={{0,24},{1,25},{2,26},{3,27},{4,28},{5,29},{6,30},{7,31},{8,16},{9,... | collective-permute-start | bytes 196616 | tf_op jit(solution)/shard_map/ppermute | solution.py:269
  37.7 4.3 %collective-permute-start.10 = (bf16[1,256,128]{2,1,0:T(8,128)(2,1)S(1)}, bf16[1,256,128]{2,1,0:T(8,128)(2,1)S(1)}, u32[]{:S(2)}, u32[]{:S(2)}) collective-permute-start(bf16[1,256,128]{2,1,0:T(8,128)(2,1)S(1)} %get-tuple-element.48), channel_id=1, source_target_pairs={{0,4},{1,5},{2,6},{3,7},{4,0},{5,1},{6,2},{7,3},{8,12},{9,13},{10,... | collective-permute-start | bytes 196616 | tf_op jit(solution)/shard_map/ppermute | solution.py:269
  38.3 4.6 %collective-permute-start.17 = (bf16[1,256,128]{2,1,0:T(8,128)(2,1)S(1)}, bf16[1,256,128]{2,1,0:T(8,128)(2,1)S(1)}, u32[]{:S(2)}, u32[]{:S(2)}) collective-permute-start(bf16[1,256,128]{2,1,0:T(8,128)(2,1)S(1)} %get-tuple-element.57), channel_id=1, source_target_pairs={{0,8},{1,9},{2,10},{3,11},{4,12},{5,13},{6,14},{7,15},{8,0},{9,1},... | collective-permute-start | bytes 196616 | tf_op jit(solution)/shard_map/ppermute | solution.py:269
